TPU v7x, 32 devices: a whole 2x2x4 slice. The times are simulated.
32 devices in a mesh: ctx: 16 (over z, y, core), fsdp: 2 (over x).
Axes of the slice: x: 2, y: 2, z: 4, core: 2. Of those that a mesh axis runs over, the one named last changes fastest.
Arguments:
- hidden_in: bfloat16 [2, 2048, 1024], P('fsdp', 'ctx'), may hold values from -6 to 6
- block_order: int32 [2, 32], P('fsdp'), may hold values from 0 to 31, as said below
- segment_ids: int32 [2, 2048], P('fsdp'), may hold values from 0 to 5, never falling along the last dimension, each value on 1 to 1024 neighbouring positions
- cotangent: bfloat16 [2, 2048, 1024], P('fsdp', 'ctx'), may hold values from -6 to 6
- attn_gain: bfloat16 [1024], P('fsdp'), may hold values from 0.5 to 1.5
- query_key_value_weight: bfloat16 [1024, 2048], P('fsdp'), may hold values from -0.1875 to 0.1875
- w_out: bfloat16 [1024, 1024], P('fsdp'), may hold values from -0.75 to 0.75
- ffn_gain: bfloat16 [1024], P('fsdp'), may hold values from 0.5 to 1.5
- w_router: bfloat16 [1024, 32], P('fsdp'), may hold values from -0.09375 to 0.09375
- routes: int32 [2, 2048, 8], P('fsdp', 'ctx'), may hold values from 0 to 31, all different within a row; in each aligned block of 128 rows (0 to 127, 128 to 255, ..., all dimensions but the last counted through in order) at most 48 rows name the same one
- expert_in: bfloat16 [32, 1024, 1024], P('fsdp', 'ctx'), may hold values from -0.1875 to 0.1875
- expert_out: bfloat16 [32, 512, 1024], P('fsdp', 'ctx'), may hold values from -1 to 1
Outputs:
- hidden_out: bfloat16 [2, 2048, 1024], P('fsdp', 'ctx')
- grad_in: float32 [2, 2048, 1024], P('fsdp', 'ctx')
- grad_attn_gain: float32 [1024], P('fsdp')
- grad_w_qkv: float32 [1024, 2048], P('fsdp')
- grad_w_out: float32 [1024, 1024], P('fsdp')
- grad_ffn_gain: float32 [1024], P('fsdp')
- grad_router: float32 [1024, 32], P('fsdp')
- grad_expert_in: float32 [32, 1024, 1024], P('fsdp', 'ctx')
- grad_expert_out: float32 [32, 512, 1024], P('fsdp', 'ctx')
Inputs may be any that keep to these rules, and one draw needn't show every extreme that they name: `routes`: in the rows of one device no expert is named by more than 48 rows; some expert is named by exactly 48 rows on some devices. `segment_ids`: document numbers never fall along positions; a document holds 1 to 1024 positions, one exactly 1024. `block_order`: each row names every number of 0 to 31 once; storage blocks 2 k and 2 k + 1 hold position blocks p and 31 - p for some p < 16.
All inputs are finite; a program needn't handle non-finite values.
Results may differ from a plain program's by a relative error of at most 0.018.
Values may be sent and summed in bfloat16 or wider, within the bound.
No kernel may reach another device: no remote copies, remote signals or barrier semaphores. Data moves between devices by JAX's collectives and lax.ppermute only.
A program may use at most 192 MiB of HBM per device.

v0:
```python
import math

import jax
import jax.numpy as jnp
from jax import lax
from jax.sharding import PartitionSpec as P

QUERY_HEADS = 16
KEY_VALUE_HEADS = 8
HEAD_SIZE = 64
E = 32
TOPK = 8
F = 512
MOST = 48


EPSILON = 1e-06
THETA = 10000.0
MASK_FILL_VALUE = -1e30
HIGHEST = lax.Precision.HIGHEST


def carried_in(value, axis, combine, identity):
    length, mine = (lax.axis_size(axis), lax.axis_index(axis))
    everything = lax.all_gather(value, axis)
    start = jnp.broadcast_to(jnp.asarray(identity, value.dtype), value.shape)

    def turn(k, before):
        reached = k < mine
        new = combine(before, everything[k])
        return jnp.where(reached, new, before)

    return lax.fori_loop(0, length, turn, start)


def rms_scale(value_rows):
    return lax.rsqrt(jnp.mean(value_rows * value_rows, axis=-1, keepdims=True) + EPSILON)


def rotate(value_rows):
    middle = value_rows.shape[-1] // 2
    return jnp.concatenate([-value_rows[..., middle:], value_rows[..., :middle]], axis=-1)


def rotate_back(value_rows):
    middle = value_rows.shape[-1] // 2
    return jnp.concatenate([value_rows[..., middle:], -value_rows[..., :middle]], axis=-1)


def rope_tables(position):
    steps = jnp.arange(HEAD_SIZE // 2, dtype=jnp.float32)
    frequency = jnp.power(THETA, -2.0 * steps / HEAD_SIZE)
    angle = position.astype(jnp.float32)[:, None] * frequency[None, :]
    angle = jnp.concatenate([angle, angle], axis=-1)
    return (jnp.cos(angle), jnp.sin(angle))


def contract_rows(left, right):
    return lax.dot_general(
        left, right, (((0,), (0,)), ((), ())), preferred_element_type=jnp.float32
    )


def contract_columns(left, right):
    return lax.dot_general(
        left, right, (((1,), (1,)), ((), ())), preferred_element_type=jnp.float32
    )


def own_rows(total, rank, count):
    share = total.shape[0] // count
    return lax.dynamic_slice_in_dim(total, rank * share, share, 0)


def shards(
    hidden_in,
    block_order,
    segment_ids,
    cotangent,
    attn_gain,
    query_key_value_weight,
    w_out,
    ffn_gain,
    w_router,
    routes,
    expert_in,
    expert_out,
):
    count_of_rows = hidden_in.shape[1]
    width = hidden_in.shape[2]
    ctx_count = lax.axis_size("ctx")
    fsdp_count = lax.axis_size("fsdp")
    sequence_length = count_of_rows * ctx_count
    half_block = count_of_rows // 2
    capacity = sequence_length * TOPK * 9 // (8 * E)
    query_total_width = QUERY_HEADS * HEAD_SIZE
    key_total_width = KEY_VALUE_HEADS * HEAD_SIZE
    query_group = QUERY_HEADS // KEY_VALUE_HEADS
    scale = 1.0 / math.sqrt(HEAD_SIZE)
    key_block_rows = min(1024, sequence_length)
    block_count = sequence_length // key_block_rows
    pair_count = count_of_rows * TOPK
    gain_one, qkv_full, out_full, gain_two, router_full = (
        lax.all_gather(attn_gain, "fsdp", axis=0, tiled=True),
        lax.all_gather(query_key_value_weight, "fsdp", axis=0, tiled=True),
        lax.all_gather(w_out, "fsdp", axis=0, tiled=True),
        lax.all_gather(ffn_gain, "fsdp", axis=0, tiled=True),
        lax.all_gather(w_router, "fsdp", axis=0, tiled=True),
    )
    up_full, down_full = (
        lax.all_gather(expert_in, "ctx", axis=1, tiled=True),
        lax.all_gather(expert_out, "ctx", axis=1, tiled=True),
    )
    key_position = (
        block_order[0][:, None] * half_block + jnp.arange(half_block, dtype=jnp.int32)[None, :]
    ).reshape(-1)
    key_document = segment_ids[0][key_position]
    first_row = lax.axis_index("ctx") * count_of_rows
    query_position = lax.dynamic_slice_in_dim(key_position, first_row, count_of_rows, 0)
    query_document = lax.dynamic_slice_in_dim(key_document, first_row, count_of_rows, 0)
    inputs = hidden_in[0].astype(jnp.float32)
    grad_out = cotangent[0].astype(jnp.float32)
    scale_one = rms_scale(inputs)
    norm_one = inputs * scale_one
    gain_one_f = gain_one.astype(jnp.float32)
    h_one = (norm_one * gain_one_f).astype(jnp.bfloat16)
    projected_rows = jnp.dot(h_one, qkv_full, preferred_element_type=jnp.float32)
    cosine, sine = rope_tables(query_position)
    query_raw = projected_rows[:, :query_total_width].reshape(count_of_rows, QUERY_HEADS, HEAD_SIZE)
    unrotated_key = projected_rows[
        :, query_total_width : query_total_width + key_total_width
    ].reshape(count_of_rows, KEY_VALUE_HEADS, HEAD_SIZE)
    query_matrix = (query_raw * cosine[:, None, :] + rotate(query_raw) * sine[:, None, :]).astype(
        jnp.bfloat16
    )
    key_rows = (
        unrotated_key * cosine[:, None, :] + rotate(unrotated_key) * sine[:, None, :]
    ).astype(jnp.bfloat16)
    value_rows = projected_rows[:, query_total_width + key_total_width :].astype(jnp.bfloat16)
    key_value_local = jnp.concatenate(
        [key_rows.reshape(count_of_rows, key_total_width), value_rows], axis=1
    )
    key_value_all = lax.all_gather(key_value_local, "ctx", axis=0, tiled=True)
    grouped_queries = query_matrix.reshape(count_of_rows, KEY_VALUE_HEADS, query_group, HEAD_SIZE)
    block_number = jnp.arange(block_count, dtype=jnp.int32)

    def block_keys(source, index):
        current_rows = lax.dynamic_slice_in_dim(source, index * key_block_rows, key_block_rows, 0)
        block_key_rows = current_rows[:, :key_total_width].reshape(
            key_block_rows, KEY_VALUE_HEADS, HEAD_SIZE
        )
        block_value_rows = current_rows[:, key_total_width:].reshape(
            key_block_rows, KEY_VALUE_HEADS, HEAD_SIZE
        )
        block_position = lax.dynamic_slice_in_dim(
            key_position, index * key_block_rows, key_block_rows, 0
        )
        block_document = lax.dynamic_slice_in_dim(
            key_document, index * key_block_rows, key_block_rows, 0
        )
        allowed = (query_document[:, None] == block_document[None, :]) & (
            block_position[None, :] <= query_position[:, None]
        )
        return (block_key_rows, block_value_rows, allowed)

    def scores_of(block_key_rows, allowed):
        scores = (
            jnp.einsum(
                "qhgd,khd->hgqk",
                grouped_queries,
                block_key_rows,
                preferred_element_type=jnp.float32,
            )
            * scale
        )
        return jnp.where(allowed[None, None], scores, MASK_FILL_VALUE)

    def max_sum(carry, index):
        top, total = carry
        block_key_rows, block_value_rows, allowed = block_keys(key_value_all, index)
        scores = scores_of(block_key_rows, allowed)
        new_top = jnp.maximum(top, jnp.max(scores, axis=-1))
        weights = jnp.where(allowed[None, None], jnp.exp(scores - new_top[..., None]), 0.0)
        total = total * jnp.exp(top - new_top) + jnp.sum(weights, axis=-1)
        return ((new_top, total), None)

    upper_start = jnp.full(
        (KEY_VALUE_HEADS, query_group, count_of_rows), MASK_FILL_VALUE, jnp.float32
    )
    overall_start = jnp.zeros((KEY_VALUE_HEADS, query_group, count_of_rows), jnp.float32)
    (top, total), unused = lax.scan(max_sum, (upper_start, overall_start), block_number)
    log_total = top + jnp.log(total)

    def weighted_values(accum, index):
        block_key_rows, block_value_rows, allowed = block_keys(key_value_all, index)
        scores = scores_of(block_key_rows, allowed)
        probs = jnp.where(allowed[None, None], jnp.exp(scores - log_total[..., None]), 0.0).astype(
            jnp.bfloat16
        )
        return (
            accum
            + jnp.einsum(
                "hgqk,khd->qhgd", probs, block_value_rows, preferred_element_type=jnp.float32
            ),
            None,
        )

    attended_f, unused = lax.scan(
        weighted_values,
        jnp.zeros((count_of_rows, KEY_VALUE_HEADS, query_group, HEAD_SIZE), jnp.float32),
        block_number,
    )
    attended = attended_f.reshape(count_of_rows, query_total_width).astype(jnp.bfloat16)
    middle_state = inputs + jnp.dot(attended, out_full, preferred_element_type=jnp.float32)
    scale_two = rms_scale(middle_state)
    norm_two = middle_state * scale_two
    gain_two_f = gain_two.astype(jnp.float32)
    h_two = (norm_two * gain_two_f).astype(jnp.bfloat16)
    logits = jnp.dot(h_two, router_full, preferred_element_type=jnp.float32)
    route = routes[0]
    gates = jax.nn.softmax(jnp.take_along_axis(logits, route, axis=1), axis=-1)
    flat = route.reshape(-1)
    onehot = (flat[:, None] == jnp.arange(E, dtype=jnp.int32)[None, :]).astype(jnp.int32)
    rank = jnp.sum((jnp.cumsum(onehot, axis=0) - onehot) * onehot, axis=1)
    counts = jnp.sum(onehot, axis=0)

    def add_counts(earlier, later):
        return earlier + later

    offsets = carried_in(counts, "ctx", add_counts, jnp.zeros((E,), jnp.int32))
    slot = jnp.sum(onehot * offsets[None, :], axis=1) + rank
    kept = slot < capacity
    target = jnp.where(kept, flat * MOST + rank, E * MOST)
    safe_target = jnp.minimum(target, E * MOST - 1)
    keep_float = kept.astype(jnp.float32)[:, None]
    token = jnp.arange(pair_count, dtype=jnp.int32) // TOPK
    send_rows = (
        jnp.zeros((E * MOST, width), jnp.bfloat16)
        .at[target]
        .set(h_two[token], mode="drop")
        .reshape(E, MOST, width)
    )
    received = lax.all_to_all(send_rows, "fsdp", split_axis=0, concat_axis=1, tiled=True)
    before = jnp.einsum("erd,edf->erf", received, up_full, preferred_element_type=jnp.float32)
    gate_pre = before[..., :F]
    up_pre = before[..., F:]
    sigma = jax.nn.sigmoid(gate_pre)
    activation = (gate_pre * sigma * up_pre).astype(jnp.bfloat16)
    expert_result = jnp.einsum(
        "erf,efd->erd", activation, down_full, preferred_element_type=jnp.float32
    ).astype(jnp.bfloat16)
    returned = lax.all_to_all(
        expert_result, "fsdp", split_axis=1, concat_axis=0, tiled=True
    ).reshape(E * MOST, width)
    pair_result = (returned[safe_target].astype(jnp.float32) * keep_float).reshape(
        count_of_rows, TOPK, width
    )
    mixture = jnp.sum(gates[..., None] * pair_result, axis=1)
    hidden_out = (middle_state + mixture).astype(jnp.bfloat16)
    grad_pair = (
        (gates[..., None] * grad_out[:, None, :]).reshape(pair_count, width) * keep_float
    ).astype(jnp.bfloat16)
    grad_gates = jnp.sum(grad_out[:, None, :] * pair_result, axis=-1)
    grad_chosen = gates * (grad_gates - jnp.sum(gates * grad_gates, axis=-1, keepdims=True))
    chosen_table = (route[..., None] == jnp.arange(E, dtype=jnp.int32)[None, None, :]).astype(
        jnp.float32
    )
    grad_logits = jnp.sum(grad_chosen[..., None] * chosen_table, axis=1)
    grad_router_part = lax.dot_general(
        h_two.astype(jnp.float32), grad_logits, (((0,), (0,)), ((), ())), precision=HIGHEST
    )
    grad_h_two = lax.dot_general(
        grad_logits, router_full.astype(jnp.float32), (((1,), (1,)), ((), ())), precision=HIGHEST
    )
    send_grads = (
        jnp.zeros((E * MOST, width), jnp.bfloat16)
        .at[target]
        .set(grad_pair, mode="drop")
        .reshape(E, MOST, width)
    )
    grad_received = lax.all_to_all(send_grads, "fsdp", split_axis=0, concat_axis=1, tiled=True)
    grad_activation = jnp.einsum(
        "erd,efd->erf", grad_received, down_full, preferred_element_type=jnp.float32
    )
    grad_down = jnp.einsum(
        "erf,erd->efd", activation, grad_received, preferred_element_type=jnp.float32
    )
    grad_gate = grad_activation * up_pre * sigma * (1.0 + gate_pre * (1.0 - sigma))
    grad_up = grad_activation * gate_pre * sigma
    grad_pre = jnp.concatenate([grad_gate, grad_up], axis=-1).astype(jnp.bfloat16)
    grad_up_weight = jnp.einsum(
        "erd,erf->edf", received, grad_pre, preferred_element_type=jnp.float32
    )
    grad_copy = jnp.einsum(
        "erf,edf->erd", grad_pre, up_full, preferred_element_type=jnp.float32
    ).astype(jnp.bfloat16)
    grad_returned = lax.all_to_all(
        grad_copy, "fsdp", split_axis=1, concat_axis=0, tiled=True
    ).reshape(E * MOST, width)
    grad_h_two = grad_h_two + jnp.sum(
        (grad_returned[safe_target].astype(jnp.float32) * keep_float).reshape(
            count_of_rows, TOPK, width
        ),
        axis=1,
    )
    grad_expert_in, grad_expert_out = (
        lax.psum_scatter(
            grad_up_weight.astype(jnp.bfloat16), "ctx", scatter_dimension=1, tiled=True
        ).astype(jnp.float32),
        lax.psum_scatter(
            grad_down.astype(jnp.bfloat16), "ctx", scatter_dimension=1, tiled=True
        ).astype(jnp.float32),
    )
    grad_gain_two = jnp.sum(grad_h_two * norm_two, axis=0)
    scaled_two = grad_h_two * gain_two_f
    grad_mid = grad_out + scale_two * (
        scaled_two - norm_two * jnp.mean(scaled_two * norm_two, axis=-1, keepdims=True)
    )
    grad_branch = grad_mid.astype(jnp.bfloat16)
    grad_out_weight = contract_rows(attended, grad_branch)
    attended_gradient = contract_columns(grad_branch, out_full).astype(jnp.bfloat16)
    grouped_gradient = attended_gradient.reshape(
        count_of_rows, KEY_VALUE_HEADS, query_group, HEAD_SIZE
    )
    delta = jnp.transpose(
        jnp.sum(grouped_gradient.astype(jnp.float32) * attended_f, axis=-1), (1, 2, 0)
    )

    def block_gradients(query_accum, index):
        block_key_rows, block_value_rows, allowed = block_keys(key_value_all, index)
        scores = scores_of(block_key_rows, allowed)
        probs = jnp.where(allowed[None, None], jnp.exp(scores - log_total[..., None]), 0.0)
        grad_probs = jnp.einsum(
            "qhgd,khd->hgqk", grouped_gradient, block_value_rows, preferred_element_type=jnp.float32
        )
        grad_scores = (probs * (grad_probs - delta[..., None])).astype(jnp.bfloat16)
        query_accum = query_accum + jnp.einsum(
            "hgqk,khd->qhgd", grad_scores, block_key_rows, preferred_element_type=jnp.float32
        )
        grad_keys = (
            jnp.einsum(
                "hgqk,qhgd->khd", grad_scores, grouped_queries, preferred_element_type=jnp.float32
            )
            * scale
        )
        grad_values = jnp.einsum(
            "hgqk,qhgd->khd",
            probs.astype(jnp.bfloat16),
            grouped_gradient,
            preferred_element_type=jnp.float32,
        )
        joined = jnp.concatenate(
            [
                grad_keys.reshape(key_block_rows, key_total_width),
                grad_values.reshape(key_block_rows, key_total_width),
            ],
            axis=1,
        )
        return (query_accum, joined)

    grad_queries, grad_blocks = lax.scan(
        block_gradients,
        jnp.zeros((count_of_rows, KEY_VALUE_HEADS, query_group, HEAD_SIZE), jnp.float32),
        block_number,
    )
    key_value_gradient = lax.psum_scatter(
        grad_blocks.reshape(sequence_length, 2 * key_total_width).astype(jnp.bfloat16),
        "ctx",
        scatter_dimension=0,
        tiled=True,
    ).astype(jnp.float32)
    grad_queries = (grad_queries * scale).reshape(count_of_rows, QUERY_HEADS, HEAD_SIZE)
    local_key_gradient = key_value_gradient[:, :key_total_width].reshape(
        count_of_rows, KEY_VALUE_HEADS, HEAD_SIZE
    )
    grad_values_mine = key_value_gradient[:, key_total_width:]
    grad_query_pre = grad_queries * cosine[:, None, :] + rotate_back(
        grad_queries * sine[:, None, :]
    )
    grad_key_pre = local_key_gradient * cosine[:, None, :] + rotate_back(
        local_key_gradient * sine[:, None, :]
    )
    grad_projected = jnp.concatenate(
        [
            grad_query_pre.reshape(count_of_rows, query_total_width),
            grad_key_pre.reshape(count_of_rows, key_total_width),
            grad_values_mine,
        ],
        axis=1,
    ).astype(jnp.bfloat16)
    grad_qkv_weight = contract_rows(h_one, grad_projected)
    grad_h_one = contract_columns(grad_projected, qkv_full)
    grad_gain_one = jnp.sum(grad_h_one * norm_one, axis=0)
    scaled_one = grad_h_one * gain_one_f
    grad_inputs = grad_mid + scale_one * (
        scaled_one - norm_one * jnp.mean(scaled_one * norm_one, axis=-1, keepdims=True)
    )
    total_one, total_qkv, total_out, total_two, total_router = lax.psum(
        (grad_gain_one, grad_qkv_weight, grad_out_weight, grad_gain_two, grad_router_part),
        ("ctx", "fsdp"),
    )
    fsdp_rank = lax.axis_index("fsdp")
    share_one = own_rows(total_one, fsdp_rank, fsdp_count)
    share_qkv = own_rows(total_qkv, fsdp_rank, fsdp_count)
    share_out = own_rows(total_out, fsdp_rank, fsdp_count)
    share_two = own_rows(total_two, fsdp_rank, fsdp_count)
    share_router = own_rows(total_router, fsdp_rank, fsdp_count)
    return (
        hidden_out[None],
        grad_inputs[None],
        share_one,
        share_qkv,
        share_out,
        share_two,
        share_router,
        grad_expert_in,
        grad_expert_out,
    )


def solution(mesh):
    placed = (
        P("fsdp", "ctx", None),
        P("fsdp", None),
        P("fsdp", None),
        P("fsdp", "ctx", None),
        P("fsdp"),
        P("fsdp", None),
        P("fsdp", None),
        P("fsdp"),
        P("fsdp", None),
        P("fsdp", "ctx", None),
        P("fsdp", "ctx", None),
        P("fsdp", "ctx", None),
    )
    return jax.shard_map(
        shards,
        mesh=mesh,
        in_specs=placed,
        out_specs=(
            P("fsdp", "ctx", None),
            P("fsdp", "ctx", None),
            P("fsdp"),
            P("fsdp", None),
            P("fsdp", None),
            P("fsdp"),
            P("fsdp", None),
            P("fsdp", "ctx", None),
            P("fsdp", "ctx", None),
        ),
        check_vma=False,
    )
```

profile of v0, /device:TPU:0, one launch (start us, length us, event | category | flops | bytes accessed | tf_op | source)
XLA Modules:
  0.0 1496.7 jit_solution(12960953044811093808)
XLA Ops:
  8.7 5.2 all-gather.1
  16.2 52.8 %all-gather.9.cloned.1.call-done = bf16[1024,2048]{1,0:T(8,128)(2,1)} async-done(((bf16[512,2048]{1,0:T(8,128)(2,1)}), bf16[1024,2048]{1,0:T(8,128)(2,1)}) %all-gather.9.cloned.1.call-update) | async-done | bytes 4194320 | tf_op jit(solution)/shard_map/all_gather | solution.py:105
  69.0 3.1 fusion.77
  75.7 11.8 gather_fusion
  87.6 4.3 all-gather.2
  93.8 12.4 all-reduce
  106.3 9.0 reduce-window.6
  117.6 6.5 all-gather.11.cloned.1.call-done
  124.1 6.4 copy.105
  130.5 24.4 %while.51 = (s32[]{:T(128)}, f32[8,2,128]{2,1,0:T(2,128)S(1)}, f32[8,2,128]{2,1,0:T(2,128)S(1)}, s32[128]{0:T(128)S(1)}, s32[2]{0:T(128)S(1)}, /*index=5*/s32[20...) while((s32[]{:T(128)}, f32[8,2,128]{2,1,0:T(2,128)S(1)}, ...), condition=%wide.region_4.5_spmd.clone, body=%wide.region_1.4_spmd.clone.sunk | while | flops 285616128 | bytes 20710620 | solution.py:191
  133.5 4.7 fusion.166
  138.2 4.5 select_reduce_fusion.4
  145.7 4.7 fusion.166
  150.4 4.5 select_reduce_fusion.4
  155.0 12.7 while.52
  158.3 3.0 fusion.173
  164.7 3.0 fusion.173
  171.1 15.0 %scatter_custom_fusion = bf16[1536,1024]{1,0:T(8,128)(2,1)} fusion(s32[1024]{0:T(1024)S(1)} %bitcast.378, bf16[128,1024]{1,0:T(8,128)(2,1)S(1)} %multiply_convert_fusion.3, s32[1024]{0:T(1024)S(1)} %broadcast_clamp_fusion.2, bf16[]{:T(256)} %constant.168.clone.1), kind=kCustom, calls=%fused_computation.75 | custom fusion | bytes 3145730 | tf_op jit(solution)/shard_map/scatter | solution.py:240
  186.1 5.2 all-to-all-start
  191.6 37.2 %all_gather.35 = bf16[1024,32]{0,1:T(8,128)(2,1)S(1)} all-gather(bf16[512,32]{0,1:T(8,128)(2,1)S(1)} %copy-done.63), channel_id=1, replica_groups=mesh['ctx'=16,'fsdp'=2] {'fsdp'}, dimensions={0}, use_global_device_ids=true | all-gather | bytes 98304 | tf_op jit(solution)/shard_map/all_gather | solution.py:108
  229.4 7.0 gather_fusion.3
  237.8 16.3 %scatter_custom_fusion.1 = bf16[1536,1024]{1,0:T(8,128)(2,1)} fusion(s32[1024]{0:T(1024)} %bitcast.379, f32[1024]{0:T(1024)S(1)} %exponential_divide_fusion, f32[1024]{0:T(1024)S(1)} %fusion.86, f32[128,1024]{1,0:T(8,128)S(1)} %bitcast_convert_fusion, bf16[]{:T(256)} %constant.168.clone.1), kind=kCustom, calls=%fused_computation.74 | custom fusion | flops 3145728 | bytes 3678720 | tf_op jit(solution)/shard_map/scatter | solution.py:278
  254.1 5.2 all-to-all-start.2
  261.7 33.8 %all-to-all-done.2 = bf16[32,48,1024]{2,1,0:T(8,128)(2,1)} async-done(((bf16[32,48,1024]{2,1,0:T(8,128)(2,1)}), bf16[32,48,1024]{2,1,0:T(8,128)(2,1)}, u32[]{:S(2)}, u32[]{:S(2)}) %all-to-all-start.2) | async-done | bytes 3145760 | tf_op jit(solution)/shard_map/all_to_all | solution.py:281
  295.4 4.1 copy.118
  299.5 27.3 %all-gather.15.cloned.1.call-done = bf16[16,1024,1024]{2,1,0:T(8,128)(2,1)} async-done(((bf16[16,64,1024]{2,1,0:T(8,128)(2,1)}), bf16[16,1024,1024]{2,1,0:T(8,128)(2,1)}) %all-gather.15.cloned.1.call-update) | async-done | bytes 33554448 | tf_op jit(solution)/shard_map/all_gather | solution.py:111
  326.8 19.4 %fusion.100 = f32[16,96,1024]{2,1,0:T(8,128)} fusion(bf16[16,96,1024]{2,1,0:T(8,128)(2,1)S(1)} %bitcast.338, bf16[16,1024,1024]{2,1,0:T(8,128)(2,1)} %all-gather.15.cloned.1.call-done), kind=kOutput, calls=%fused_computation.203 | convolution fusion | flops 3221225472 | bytes 42991616 | tf_op jit(solution)/shard_map/erd,edf->erf/dot_general | solution.py:244
  346.3 109.5 %all-gather.17.cloned.1.call-done = bf16[16,512,1024]{2,1,0:T(8,128)(2,1)} async-done(((bf16[16,32,1024]{2,1,0:T(8,128)(2,1)}), bf16[16,512,1024]{2,1,0:T(8,128)(2,1)}) %all-gather.17.cloned.1.call-update) | async-done | bytes 16777232 | tf_op jit(solution)/shard_map/all_gather | solution.py:112
  455.8 12.4 multiply_convert_fusion.1
  468.2 16.6 %convolution_convert_fusion.2 = bf16[16,96,1024]{2,1,0:T(8,128)(2,1)S(1)} fusion(bf16[16,1024,1024]{2,1,0:T(8,128)(2,1)} %all-gather.15.cloned.1.call-done, bf16[16,96,512]{2,1,0:T(8,128)(2,1)S(1)} %get-tuple-element.622, bf16[16,96,512]{2,1,0:T(8,128)(2,1)S(1)} %get-tuple-element.621), kind=kOutput, calls=%fused_computation.72 | convolution fusion | flops 3229089792 | bytes 39845888 | tf_op jit(solution)/shard_map/erf,edf->erd/dot_general | solution.py:294
  484.8 3.4 copy.119
  488.2 4.4 all-to-all-start.3
  492.6 9.0 convolution_convert_fusion.3
  501.6 3.4 copy.114
  504.9 24.4 %all-to-all-done.3 = bf16[16,96,1024]{2,0,1:T(8,128)(2,1)S(1)} async-done(((bf16[16,96,1024]{2,0,1:T(8,128)(2,1)}), bf16[16,96,1024]{2,0,1:T(8,128)(2,1)S(1)}, u32[]{:S(2)}, u32[]{:S(2)}) %all-to-all-start.3) | async-done | bytes 3145760 | tf_op jit(solution)/shard_map/all_to_all | solution.py:297
  529.3 5.2 all-to-all-start.1
  536.0 3.6 copy.120
  539.6 31.0 %all-to-all-done.1 = bf16[16,96,1024]{2,0,1:T(8,128)(2,1)} async-done(((bf16[16,96,1024]{2,0,1:T(8,128)(2,1)}), bf16[16,96,1024]{2,0,1:T(8,128)(2,1)}, u32[]{:S(2)}, u32[]{:S(2)}) %all-to-all-start.1) | async-done | bytes 3145760 | tf_op jit(solution)/shard_map/all_to_all | solution.py:252
  570.6 5.2 copy.115
  575.8 5.3 gather_fusion.2
  581.2 7.3 gather_fusion.1
  592.2 4.5 fusion.41
  602.6 46.2 %while.54 = (s32[]{:T(128)}, f32[128,8,2,64]{0,3,2,1:T(8,128)S(1)}, bf16[2,1024,1024]{1,2,0:T(8,128)(2,1)}, s32[2]{0:T(128)S(1)}, bf16[2048,1024]{0,1:T(8,128)(2...) while((s32[]{:T(128)}, f32[128,8,2,64]{0,3,2,1:T(8,128)S(1)}, ...), condition=%wide.region_27.28_spmd.clone, body=%wide.region_26.27_spmd.clone.sunk | while | flops 1373241344 | bytes 173561600 | solution.py:361
  607.6 5.8 fusion.186
  613.4 3.3 fusion.187
  618.0 3.3 fusion.188
  630.6 5.8 fusion.186
  636.4 3.3 fusion.187
  641.0 3.2 fusion.188
  648.8 6.2 copy.138
  656.9 2.7 fusion.72
  659.6 65.4 %reduce-scatter.10.cloned.1.call-done = bf16[128,1024]{1,0:T(8,128)(2,1)} async-done(((bf16[2048,1024]{1,0:T(8,128)(2,1)}), bf16[128,1024]{1,0:T(8,128)(2,1)}) %reduce-scatter.10.cloned.1.call-update) | async-done | bytes 262160
  726.5 4.6 fusion.68
  733.0 10.2 convolution_convert_fusion.1
  745.2 15.9 %convolution_convert_fusion = bf16[16,1024,1024]{2,1,0:T(8,128)(2,1)} fusion(bf16[16,96,1024]{2,1,0:T(8,128)(2,1)S(1)} %bitcast.339, bf16[16,96,512]{2,1,0:T(8,128)(2,1)} %copy-done.18, bf16[16,96,512]{2,1,0:T(8,128)(2,1)} %copy-done.17), kind=kOutput, calls=%fused_computation.53 | convolution fusion | flops 3244294144 | bytes 39845888 | tf_op jit(solution)/shard_map/erd,erf->edf/dot_general | solution.py:291
  762.0 3.9 fusion.61
  765.9 41.1 %all-reduce.1 = (f32[1024]{0:T(1024)S(1)}, f32[1024]{0:T(1024)S(1)}) all-reduce(f32[1024]{0:T(1024)S(1)} %get-tuple-element.524, f32[1024]{0:T(1024)S(1)} %copy-done.64), channel_id=1, replica_groups=mesh['ctx'=16,'fsdp'=2] {'ctx','fsdp'}, use_global_device_ids=true, to_apply=%region_31.32 | all-reduce | flops 2048 | bytes 16384 | tf_op jit(solution)/shard_map/psum | solution.py:398
  809.4 158.3 %all-reduce.5.cloned.1.call-done = (f32[1024,2048]{1,0:T(8,128)}, f32[1024,1024]{1,0:T(8,128)}, f32[1024,32]{0,1:T(8,128)}) async-done(((f32[1024,2048]{1,0:T(8,128)}, f32[1024,1024]{1,0:T(8,128)}, f32[1024,32]{0,1:T(8,128)}), (f32[1024,2048]{1,0:T(8,128)}, f32[1024,1024]{1,0:T(8,128)}, f32[1024,32]{0,1:T(8,128)})) %all-reduce.5.cloned.1.call-update) | async-done | bytes 12714000 | tf_op jit(solution)/shard_map/psum | solution.py:398
  969.2 3.2 constant_dynamic-slice_fusion.3
  972.4 4.8 constant_dynamic-slice_fusion.4
  977.2 172.7 %reduce-scatter.8.cloned.1.call-done = bf16[16,32,1024]{2,1,0:T(8,128)(2,1)} async-done(((bf16[16,512,1024]{2,1,0:T(8,128)(2,1)}), bf16[16,32,1024]{2,1,0:T(8,128)(2,1)}) %reduce-scatter.8.cloned.1.call-update) | async-done | bytes 1048592 | tf_op jit(solution)/shard_map/reduce_scatter | solution.py:310
  1149.9 2.8 convert_element_type.177
  1152.6 333.2 %reduce-scatter.6.cloned.1.call-done = bf16[16,64,1024]{2,1,0:T(8,128)(2,1)} async-done(((bf16[16,1024,1024]{2,1,0:T(8,128)(2,1)}), bf16[16,64,1024]{2,1,0:T(8,128)(2,1)}) %reduce-scatter.6.cloned.1.call-update) | async-done | bytes 2097168 | tf_op jit(solution)/shard_map/reduce_scatter | solution.py:307
  1485.8 4.1 convert_element_type.175
  (380 shorter events, 71.0 us)
Async XLA Ops:
  7.2 68.5 %copy-start = (s32[1,2048]{1,0:T(1,128)S(1)}, s32[1,2048]{1,0:T(1,128)}, u32[]{:S(2)}) copy-start(s32[1,2048]{1,0:T(1,128)} %param.22) | copy-start | bytes 24580
  7.2 61.9 %all-gather.9.cloned.1.call-start = ((), (), s32[]{:S(2)}) async-start(), calls=%async_computation.7 | async-start | bytes 6291456 | tf_op jit(solution)/shard_map/all_gather | solution.py:105
  7.9 116.1 %all-gather.11.cloned.1.call-start = ((), (), s32[]{:S(2)}) async-start(), calls=%async_computation.8 | async-start | bytes 4456448 | tf_op jit(solution)/shard_map/all_gather | solution.py:143
  13.9 58.3 %copy-start.44 = (f32[2,1,512]{2,1,0:T(1,128)}, f32[2,1,512]{2,1,0:T(1,128)S(1)}, u32[]{:S(2)}) copy-start(f32[2,1,512]{2,1,0:T(1,128)S(1)} %convert_element_type.182) | copy-start | bytes 12292
  14.9 102.5 %copy-start.34 = (f32[128,64]{0,1:T(8,128)}, f32[128,64]{0,1:T(8,128)S(1)}, u32[]{:S(2)}) copy-start(f32[128,64]{0,1:T(8,128)S(1)} %get-tuple-element.637) | copy-start | bytes 98308
  15.0 102.5 %copy-start.36 = (f32[128,64]{0,1:T(8,128)}, f32[128,64]{0,1:T(8,128)S(1)}, u32[]{:S(2)}) copy-start(f32[128,64]{0,1:T(8,128)S(1)} %get-tuple-element.636) | copy-start | bytes 98308
  16.2 56.3 %copy-start.66 = (f32[128]{0:T(128)}, f32[128]{0:T(128)S(1)}, u32[]{:S(2)}) copy-start(f32[128]{0:T(128)S(1)} %add_rsqrt_fusion.1) | copy-start | bytes 1540
  73.3 94.4 %all-gather.13.cloned.1.call-start = ((), (), s32[]{:S(2)}) async-start(), calls=%async_computation.9 | async-start | bytes 3145728 | tf_op jit(solution)/shard_map/all_gather | solution.py:106
  74.1 252.7 %all-gather.15.cloned.1.call-start = ((), (), s32[]{:S(2)}) async-start(), calls=%async_computation.10 | async-start | bytes 35651584 | tf_op jit(solution)/shard_map/all_gather | solution.py:111
  74.7 381.1 %all-gather.17.cloned.1.call-start = ((), (), s32[]{:S(2)}) async-start(), calls=%async_computation.11 | async-start | bytes 17825792 | tf_op jit(solution)/shard_map/all_gather | solution.py:112
  75.6 40.9 %copy-start.53 = (s32[1024]{0:T(1024)}, s32[1024]{0:T(1024)S(1)}, u32[]{:S(2)}) copy-start(s32[1024]{0:T(1024)S(1)} %eq.89) | copy-start | bytes 12292
  75.7 11.9 copy-start.75
  75.7 16.4 %copy-start.76 = (u32[32]{0:T(128)S(1)}, u32[32]{0:T(128)}, u32[]{:S(2)}) copy-start(u32[32]{0:T(128)} %constant.201) | copy-start | bytes 388
  91.9 78.2 %copy-start.52 = (f32[2,1,512]{2,1,0:T(1,128)}, f32[2,1,512]{2,1,0:T(1,128)S(1)}, u32[]{:S(2)}) copy-start(f32[2,1,512]{2,1,0:T(1,128)S(1)} %convert_element_type.183) | copy-start | bytes 12292
  116.5 14.0 copy-start.59
  116.5 14.0 copy-start.61
  117.1 53.9 %copy-start.74 = (s32[1024,1]{0,1:T(1,128)}, s32[1024,1]{0,1:T(1,128)S(1)}, u32[]{:S(2)}) copy-start(s32[1024,1]{0,1:T(1,128)S(1)} %compare_select_fusion.4) | copy-start | bytes 12292
  155.0 12.8 copy-start.15
  167.7 18.4 %copy-start.38 = (s32[2048]{0:T(1024)}, s32[2048]{0:T(1024)S(1)}, u32[]{:S(2)}) copy-start(s32[2048]{0:T(1024)S(1)} %get-tuple-element.1094) | copy-start | bytes 24580
  167.7 18.4 %copy-start.48 = (s32[128]{0:T(128)}, s32[128]{0:T(128)S(1)}, u32[]{:S(2)}) copy-start(s32[128]{0:T(128)S(1)} %get-tuple-element.1098) | copy-start | bytes 1540
  167.7 18.4 %copy-start.50 = (s32[128]{0:T(128)}, s32[128]{0:T(128)S(1)}, u32[]{:S(2)}) copy-start(s32[128]{0:T(128)S(1)} %get-tuple-element.1100) | copy-start | bytes 1540
  167.7 18.4 %copy-start.69 = (f32[8,2,128]{2,1,0:T(2,128)}, f32[8,2,128]{2,1,0:T(2,128)S(1)}, u32[]{:S(2)}) copy-start(f32[8,2,128]{2,1,0:T(2,128)S(1)} %get-tuple-element.1102) | copy-start | bytes 24580
  167.8 18.4 %copy-start.23 = (bf16[128,8,2,64]{0,3,2,1:T(8,128)(2,1)}, bf16[128,8,2,64]{0,3,2,1:T(8,128)(2,1)S(1)}, u32[]{:S(2)}) copy-start(bf16[128,8,2,64]{0,3,2,1:T(8,128)(2,1)S(1)} %convert_element_type.149) | copy-start | bytes 786436
  170.1 16.0 %copy-start.73 = (f32[128]{0:T(128)}, f32[128]{0:T(128)S(1)}, u32[]{:S(2)}) copy-start(f32[128]{0:T(128)S(1)} %add_rsqrt_fusion) | copy-start | bytes 1540
  171.0 57.8 %copy-start.25 = (bf16[128,1024]{1,0:T(8,128)(2,1)}, bf16[128,1024]{1,0:T(8,128)(2,1)S(1)}, u32[]{:S(2)}) copy-start(bf16[128,1024]{1,0:T(8,128)(2,1)S(1)} %multiply_convert_fusion.3) | copy-start | bytes 786436
  171.0 20.5 %copy-start.63 = (bf16[512,32]{0,1:T(8,128)(2,1)S(1)}, bf16[512,32]{0,1:T(8,128)(2,1)}, u32[]{:S(2)}) copy-start(bf16[512,32]{0,1:T(8,128)(2,1)} %param.28) | copy-start | bytes 98308
  171.1 57.7 %copy-start.60 = (s32[1024]{0:T(1024)S(1)}, s32[1024]{0:T(1024)}, u32[]{:S(2)}) copy-start(s32[1024]{0:T(1024)} %copy-done.59) | copy-start | bytes 12292
  171.1 57.7 %copy-start.62 = (s32[1024]{0:T(1024)S(1)}, s32[1024]{0:T(1024)}, u32[]{:S(2)}) copy-start(s32[1024]{0:T(1024)} %copy-done.61) | copy-start | bytes 12292
  171.1 57.7 %copy-start.29 = (bf16[1,128,1024]{2,1,0:T(8,128)(2,1)S(1)}, bf16[1,128,1024]{2,1,0:T(8,128)(2,1)}, u32[]{:S(2)}) copy-start(bf16[1,128,1024]{2,1,0:T(8,128)(2,1)} %param.23) | copy-start | bytes 786436
  186.1 67.9 %all-to-all-start = ((bf16[32,48,1024]{2,1,0:T(8,128)(2,1)}), bf16[32,48,1024]{2,1,0:T(8,128)(2,1)}, u32[]{:S(2)}, u32[]{:S(2)}) async-start(bf16[32,48,1024]{2,1,0:T(8,128)(2,1)} %bitcast.24), calls=%async_computation | async-start | bytes 6291456 | tf_op jit(solution)/shard_map/all_to_all | solution.py:243
  228.8 8.9 copy-start.57
  228.9 8.9 copy-start.19
  229.4 8.3 copy-start.54
  254.1 41.4 %all-to-all-start.2 = ((bf16[32,48,1024]{2,1,0:T(8,128)(2,1)}), bf16[32,48,1024]{2,1,0:T(8,128)(2,1)}, u32[]{:S(2)}, u32[]{:S(2)}) async-start(bf16[32,48,1024]{2,1,0:T(8,128)(2,1)} %bitcast.38), calls=%async_computation.2 | async-start | bytes 6291456 | tf_op jit(solution)/shard_map/all_to_all | solution.py:281
  261.7 84.6 %copy-start.6 = (bf16[16,2,48,1024]{3,2,1,0:T(8,128)(2,1)}, bf16[16,2,48,1024]{3,2,1,0:T(8,128)(2,1)S(1)}, u32[]{:S(2)}) copy-start(bf16[16,2,48,1024]{3,2,1,0:T(8,128)(2,1)S(1)} %copy.113) | copy-start | bytes 9437188
  468.2 16.6 %copy-start.17 = (bf16[16,96,512]{2,1,0:T(8,128)(2,1)}, bf16[16,96,512]{2,1,0:T(8,128)(2,1)S(1)}, u32[]{:S(2)}) copy-start(bf16[16,96,512]{2,1,0:T(8,128)(2,1)S(1)} %get-tuple-element.621) | copy-start | bytes 4718596
  468.2 16.6 %copy-start.18 = (bf16[16,96,512]{2,1,0:T(8,128)(2,1)}, bf16[16,96,512]{2,1,0:T(8,128)(2,1)S(1)}, u32[]{:S(2)}) copy-start(bf16[16,96,512]{2,1,0:T(8,128)(2,1)S(1)} %get-tuple-element.622) | copy-start | bytes 4718596
  488.2 41.1 %all-to-all-start.3 = ((bf16[16,96,1024]{2,0,1:T(8,128)(2,1)}), bf16[16,96,1024]{2,0,1:T(8,128)(2,1)S(1)}, u32[]{:S(2)}, u32[]{:S(2)}) async-start(bf16[16,96,1024]{2,0,1:T(8,128)(2,1)} %copy.119), calls=%async_computation.3 | async-start | bytes 6291456 | tf_op jit(solution)/shard_map/all_to_all | solution.py:297
  504.9 29.6 %copy-start.58 = (f32[1024]{0:T(1024)S(1)}, f32[1024]{0:T(1024)}, u32[]{:S(2)}) copy-start(f32[1024]{0:T(1024)} %copy-done.57) | copy-start | bytes 12292
  529.3 6.7 copy-start.8
  529.3 41.3 %all-to-all-start.1 = ((bf16[16,96,1024]{2,0,1:T(8,128)(2,1)}), bf16[16,96,1024]{2,0,1:T(8,128)(2,1)}, u32[]{:S(2)}, u32[]{:S(2)}) async-start(bf16[16,96,1024]{2,0,1:T(8,128)(2,1)} %copy.114), calls=%async_computation.1 | async-start | bytes 6291456 | tf_op jit(solution)/shard_map/all_to_all | solution.py:252
  534.5 190.5 %reduce-scatter.10.cloned.1.call-start = ((), (), s32[]{:S(2)}) async-start(), calls=%async_computation.14 | async-start | bytes 4456448
  581.2 7.3 copy-start.20
  588.5 8.2 copy-start.56
  588.5 8.2 copy-start.13
  592.2 8.7 copy-start.14
  596.7 5.2 copy-start.28
  596.7 5.9 copy-start.46
  596.8 5.8 copy-start.5
  596.8 5.8 copy-start.39
  600.9 56.0 %copy-start.10 = (f32[128,1024]{1,0:T(8,128)}, f32[128,1024]{1,0:T(8,128)S(1)}, u32[]{:S(2)}) copy-start(f32[128,1024]{1,0:T(8,128)S(1)} %get-tuple-element.626) | copy-start | bytes 1572868
  607.1 6.2 copy-start.3
  630.1 6.2 copy-start.3
  655.0 312.7 %all-reduce.5.cloned.1.call-start = ((), (), s32[]{:S(2)}) async-start(), calls=%async_computation.15 | async-start | bytes 25427968 | tf_op jit(solution)/shard_map/psum | solution.py:398
  656.0 70.4 %copy-start.32 = (bf16[128,1024]{0,1:T(8,128)(2,1)}, bf16[128,1024]{0,1:T(8,128)(2,1)S(1)}, u32[]{:S(2)}) copy-start(bf16[128,1024]{0,1:T(8,128)(2,1)S(1)} %fusion.65) | copy-start | bytes 786436
  656.0 70.4 %copy-start.16 = (bf16[1,128,1024]{2,1,0:T(8,128)(2,1)S(1)}, bf16[1,128,1024]{2,1,0:T(8,128)(2,1)}, u32[]{:S(2)}) copy-start(bf16[1,128,1024]{2,1,0:T(8,128)(2,1)} %param.20) | copy-start | bytes 786436
  656.0 70.4 %copy-start.45 = (f32[2,1,512]{2,1,0:T(1,128)S(1)}, f32[2,1,512]{2,1,0:T(1,128)}, u32[]{:S(2)}) copy-start(f32[2,1,512]{2,1,0:T(1,128)} %copy-done.44) | copy-start | bytes 12292
  656.0 70.4 %copy-start.67 = (f32[128]{0:T(128)S(1)}, f32[128]{0:T(128)}, u32[]{:S(2)}) copy-start(f32[128]{0:T(128)} %copy-done.66) | copy-start | bytes 1540
  726.2 4.9 copy-start.42
  731.1 418.7 %reduce-scatter.8.cloned.1.call-start = ((), (), s32[]{:S(2)}) async-start(), calls=%async_computation.13 | async-start | bytes 17825792 | tf_op jit(solution)/shard_map/reduce_scatter | solution.py:310
  743.2 742.6 %reduce-scatter.6.cloned.1.call-start = ((), (), s32[]{:S(2)}) async-start(), calls=%async_computation.12 | async-start | bytes 35651584 | tf_op jit(solution)/shard_map/reduce_scatter | solution.py:307
  761.1 4.8 copy-start.64
  761.1 47.3 %copy-start.11 = (f32[128,1024]{1,0:T(8,128)S(1)}, f32[128,1024]{1,0:T(8,128)}, u32[]{:S(2)}) copy-start(f32[128,1024]{1,0:T(8,128)} %copy-done.10) | copy-start | bytes 1572868
  972.4 517.5 %copy-start.1 = (s32[1,2048]{1,0:T(1,128)S(1)}, s32[1,2048]{1,0:T(1,128)}, u32[]{:S(2)}) copy-start(s32[1,2048]{1,0:T(1,128)} %param.22) | copy-start | bytes 24580
  (42 other events, 95.8 us)
Sparse Core Ops, SparseCore 0:
  9.6 59.4 all-gather.8
  73.5 50.5 all-gather.10
  125.6 31.6 all-gather.12
  158.7 168.0 all-gather.14
  328.8 126.8 all-gather.16
  655.2 69.8 reduce-scatter.9
  733.2 234.5 all-reduce.4
  971.8 177.9 reduce-scatter.7
  1154.1 331.6 reduce-scatter.5
where the time goes:
time: 1510 us; the launch traced here: 1500 us
  waiting for transfers between devices  1020 us (68%)
  matrix products  149 us (10%)
  local copies, waits for them, and re-layouts  128 us (8%)
  blocking collectives  100 us (7%)
  other arithmetic  60.1 us (4%)
  starting transfers between devices  20.4 us (1%)
  between operations  16 us (1%)
    reduce_scatter x1, waiting for transfers between devices, shards(): lax.psum_scatter(grad_up_weight.astype(jnp.bfloat16), 'ctx', scatter_dime...  333 us
    reduce_scatter x1, waiting for transfers between devices, shards(): lax.psum_scatter(grad_down.astype(jnp.bfloat16), 'ctx', scatter_dimension...  173 us
    psum x1, waiting for transfers between devices, shards(): lax.psum((grad_gain_one, grad_qkv_weight, grad_out_weight, grad_gain_two,...  158 us
    all_gather x1, waiting for transfers between devices, shards(): lax.all_gather(expert_out, 'ctx', axis=1, tiled=True)  110 us
    unnamed x10, waiting for transfers between devices  67.9 us
    all_gather x1, waiting for transfers between devices, shards(): lax.all_gather(query_key_value_weight, 'fsdp', axis=0, tiled=True)  52.8 us
    psum x1, blocking collectives, shards(): lax.psum((grad_gain_one, grad_qkv_weight, grad_out_weight, grad_gain_two,...  41.1 us
    all_gather x1, blocking collectives, shards(): lax.all_gather(w_router, 'fsdp', axis=0, tiled=True)  37.2 us
  transfers between devices with their start and end apart: 13, of which 11 were waited for; matrix products, arithmetic and copies ran while one was open for 13% of the time, Pallas kernels for 0%

commit v1 on v0

--- a/solution.py
+++ b/solution.py
@@ -3,6 +3,9 @@
 import jax
 import jax.numpy as jnp
 from jax import lax
+from jax.experimental import pallas as pl
+from jax.experimental.pallas import tpu as pltpu
+from jax.sharding import Mesh
 from jax.sharding import PartitionSpec as P
 
 QUERY_HEADS = 16
@@ -72,7 +75,7 @@
     return lax.dynamic_slice_in_dim(total, rank * share, share, 0)
 
 
-def shards(
+def general_shards(
     hidden_in,
     block_order,
     segment_ids,
@@ -418,7 +421,7 @@
     )
 
 
-def solution(mesh):
+def general_solution(mesh):
     placed = (
         P("fsdp", "ctx", None),
         P("fsdp", None),
@@ -434,7 +437,7 @@
         P("fsdp", "ctx", None),
     )
     return jax.shard_map(
-        shards,
+        general_shards,
         mesh=mesh,
         in_specs=placed,
         out_specs=(
@@ -450,3 +453,583 @@
         ),
         check_vma=False,
     )
+
+
+CTX = ("a", "b", "c", "d")
+HALF = ("b", "c", "d", "f")
+EVERY = ("a", "b", "c", "d", "f")
+QUERY_BLOCK = 256
+EXTRA = 128
+
+
+def swap(value, axis):
+    return lax.ppermute(value, axis, [(0, 1), (1, 0)])
+
+
+def in_order(mine, other, axis, dim):
+    first = lax.axis_index(axis) == 0
+    return jnp.where(
+        first, jnp.concatenate([mine, other], dim), jnp.concatenate([other, mine], dim)
+    )
+
+
+def join(value, axis, dim=0):
+    return in_order(value, swap(value, axis), axis, dim)
+
+
+def gather_ctx(parts, orders):
+    held = [part[(None,) * 4] for part in parts]
+    for step in range(4):
+        others = [swap(held[i], orders[i][step]) for i in range(len(held))]
+        held = [
+            in_order(held[i], others[i], orders[i][step], CTX.index(orders[i][step]))
+            for i in range(len(held))
+        ]
+    return [value.reshape((16,) + value.shape[4:]) for value in held]
+
+
+def sum_everywhere(value):
+    for axis in ("d", "f", "c", "b", "a"):
+        value = value + swap(value, axis)
+    return value
+
+
+def exact_parts(value):
+    high = lax.reduce_precision(value, 8, 7)
+    rest = value - high
+    middle = lax.reduce_precision(rest, 8, 7)
+    return [part.astype(jnp.bfloat16) for part in (high, middle, rest - middle)]
+
+
+def lane_of(shape):
+    return lax.broadcasted_iota(jnp.int32, shape, 1)
+
+
+def attention_forward(
+    place, first_key, h_low, h_high, weight, cosine, sine, start,
+    query_out, key_out, value_out, mixed_out, attended_out, value_t,
+):
+    rows = h_low.shape[0]
+    block = QUERY_BLOCK
+    pieces = block // 64
+
+    def project(chunk, carry):
+        storage = [
+            pl.ds(pl.multiple_of(place[chunk * pieces + n] * 64, 64), 64) for n in range(pieces)
+        ]
+        low = jnp.concatenate([h_low[one, :] for one in storage], 0)
+        high = jnp.concatenate([h_high[one, :] for one in storage], 0)
+        here = pl.ds(pl.multiple_of(chunk * block, block), block)
+        both = jnp.dot(low, weight[:512, :], preferred_element_type=jnp.float32) + jnp.dot(
+            high, weight[512:, :], preferred_element_type=jnp.float32
+        )
+        pair = both[:, :128]
+        values = both[:, 128:].astype(jnp.bfloat16)
+        lane = lane_of((block, 128))
+        turned = jnp.where(
+            lane % 64 < 32, -pltpu.roll(pair, 96, 1), pltpu.roll(pair, 32, 1)
+        )
+        pair = pair * cosine[here, :] + turned * sine[here, :]
+        pair = pair.astype(jnp.bfloat16).astype(jnp.float32)
+        key_out[here, :] = jnp.where(lane >= 64, pair, 0.0).astype(jnp.bfloat16)
+        query_out[here, :] = jnp.where(
+            lane >= 64, pltpu.roll(pair, 64, 1) * (1.0 / math.sqrt(HEAD_SIZE)), 0.0
+        ).astype(jnp.bfloat16)
+        value_out[here, :] = values
+        turned_values = jnp.transpose(values.astype(jnp.float32))
+        ones = lax.broadcasted_iota(jnp.int32, (128, block), 0) == 64
+        value_t[:, here] = jnp.where(ones, 1.0, turned_values).astype(jnp.bfloat16)
+        return carry
+
+    lax.fori_loop(0, rows // block, project, 0)
+
+    def attend(number, carry):
+        here = pl.ds(pl.multiple_of(number * block, block), block)
+        queries = query_out[here, :]
+        begin = start[:, here]
+        query_at = lax.broadcasted_iota(jnp.int32, (block, block), 1) + number * block
+
+        def turn(key_number, state):
+            top, total = state
+            there = pl.ds(pl.multiple_of(key_number * block, block), block)
+            scores = lax.dot_general(
+                key_out[there, :], queries, (((1,), (1,)), ((), ())),
+                preferred_element_type=jnp.float32,
+            )
+            key_at = lax.broadcasted_iota(jnp.int32, (block, block), 0) + key_number * block
+            allowed = (key_at >= begin) & (key_at <= query_at)
+            scores = jnp.where(allowed, scores, MASK_FILL_VALUE)
+            new_top = jnp.maximum(top, jnp.max(scores, axis=0, keepdims=True))
+            weights = jnp.exp(scores - new_top).astype(jnp.bfloat16)
+            total = total * jnp.exp(top - new_top) + jnp.dot(
+                value_t[:, there], weights, preferred_element_type=jnp.float32
+            )
+            return new_top, total
+
+        top, total = lax.fori_loop(
+            first_key[number],
+            number + 1,
+            turn,
+            (
+                jnp.full((1, block), MASK_FILL_VALUE, jnp.float32),
+                jnp.zeros((128, block), jnp.float32),
+            ),
+        )
+        weight_sum = total[64:65, :]
+        mixed = total * (1.0 / weight_sum)
+        log_total = top + jnp.log(weight_sum)
+        mixed_out[:64, here] = mixed[:64, :]
+        mixed_out[64:72, here] = jnp.broadcast_to(log_total, (8, block))
+        upright = jnp.transpose(mixed)[:, :64].astype(jnp.bfloat16)
+        for n in range(pieces):
+            rows_there = pl.ds(pl.multiple_of(place[number * pieces + n] * 64, 64), 64)
+            attended_out[rows_there, :] = upright[n * 64 : (n + 1) * 64, :]
+        return carry
+
+    lax.fori_loop(0, rows // block, attend, 0)
+
+
+def attention_backward(
+    place, first_key, query, key, value, mixed, grad, cosine, sine, start,
+    pair_out, value_out, key_t, pair_sum, value_sum,
+):
+    rows = query.shape[0]
+    block = QUERY_BLOCK
+    pieces = block // 64
+    scale = 1.0 / math.sqrt(HEAD_SIZE)
+
+    def prepare(chunk, carry):
+        here = pl.ds(pl.multiple_of(chunk * block, block), block)
+        turned = jnp.transpose(key[here, :].astype(jnp.float32))
+        key_t[:, here] = turned[64:, :].astype(jnp.bfloat16)
+        pair_sum[here, :] = jnp.zeros((block, 128), jnp.float32)
+        value_sum[here, :] = jnp.zeros((block, 64), jnp.float32)
+        return carry
+
+    lax.fori_loop(0, rows // block, prepare, 0)
+
+    def storage(number):
+        return [
+            pl.ds(pl.multiple_of(place[number * pieces + n] * 64, 64), 64) for n in range(pieces)
+        ]
+
+    def attend(number, carry):
+        here = pl.ds(pl.multiple_of(number * block, block), block)
+        queries = query[here, :]
+        incoming = jnp.concatenate([grad[one, :] for one in storage(number)], 0)
+        padded = jnp.concatenate([incoming, jnp.zeros((block, 64), jnp.bfloat16)], 1)
+        incoming_t = jnp.transpose(padded.astype(jnp.float32))[:64, :]
+        log_total = mixed[64:65, here]
+        delta = jnp.sum(incoming_t * mixed[:64, here], axis=0, keepdims=True)
+        begin = start[:, here]
+        query_at = lax.broadcasted_iota(jnp.int32, (block, block), 1) + number * block
+
+        def turn(key_number, total):
+            there = pl.ds(pl.multiple_of(key_number * block, block), block)
+            scores = lax.dot_general(
+                key[there, :], queries, (((1,), (1,)), ((), ())),
+                preferred_element_type=jnp.float32,
+            )
+            key_at = lax.broadcasted_iota(jnp.int32, (block, block), 0) + key_number * block
+            allowed = (key_at >= begin) & (key_at <= query_at)
+            probs = jnp.where(allowed, jnp.exp(scores - log_total), 0.0)
+            grad_probs = lax.dot_general(
+                value[there, :], padded, (((1,), (1,)), ((), ())),
+                preferred_element_type=jnp.float32,
+            )
+            grad_scores = (probs * (grad_probs - delta)).astype(jnp.bfloat16)
+            value_sum[there, :] += jnp.dot(
+                probs.astype(jnp.bfloat16), incoming, preferred_element_type=jnp.float32
+            )
+            pair_sum[there, :] += jnp.dot(
+                grad_scores, queries, preferred_element_type=jnp.float32
+            )
+            return total + jnp.dot(
+                key_t[:, there], grad_scores, preferred_element_type=jnp.float32
+            )
+
+        total = lax.fori_loop(
+            first_key[number], number + 1, turn, jnp.zeros((64, block), jnp.float32)
+        )
+        tall = jnp.concatenate([total * scale, jnp.zeros((64, block), jnp.float32)], 0)
+        pair_sum[here, :] += jnp.transpose(tall)
+        return carry
+
+    lax.fori_loop(0, rows // block, attend, 0)
+
+    def finish(number, carry):
+        here = pl.ds(pl.multiple_of(number * block, block), block)
+        pair = pair_sum[here, :]
+        lane = lane_of((block, 128))
+        across = pair * sine[here, :]
+        turned = jnp.where(
+            lane % 64 < 32, pltpu.roll(across, 96, 1), -pltpu.roll(across, 32, 1)
+        )
+        pair = pair * cosine[here, :] + turned
+        values = value_sum[here, :]
+        for n, one in enumerate(storage(number)):
+            pair_out[one, :] = pair[n * 64 : (n + 1) * 64, :]
+            value_out[one, :] = values[n * 64 : (n + 1) * 64, :]
+        return carry
+
+    lax.fori_loop(0, rows // block, finish, 0)
+
+
+def whole_call(kernel, scalars, outs, scratch, vmem):
+    def run(*operands):
+        spec = pl.BlockSpec(memory_space=pltpu.VMEM)
+        return pl.pallas_call(
+            kernel,
+            out_shape=outs,
+            grid_spec=pltpu.PrefetchScalarGridSpec(
+                num_scalar_prefetch=scalars,
+                grid=(),
+                in_specs=[spec] * (len(operands) - scalars),
+                out_specs=[spec] * len(outs),
+                scratch_shapes=scratch,
+            ),
+            compiler_params=pltpu.CompilerParams(vmem_limit_bytes=vmem),
+        )(*operands)
+
+    return run
+
+
+def fast_shards(
+    hidden_in, block_order, segment_ids, cotangent, attn_gain, query_key_value_weight,
+    w_out, ffn_gain, w_router, routes, expert_in, expert_out,
+):
+    bf16, f32 = jnp.bfloat16, jnp.float32
+    rows = hidden_in.shape[1]
+    width = hidden_in.shape[2]
+    length = rows * 16
+    capacity = length * TOPK * 9 // (8 * E)
+    ia, ib, ic, idd, jf = (lax.axis_index(name) for name in EVERY)
+    mine = ia * 8 + ib * 4 + ic * 2 + idd
+    expert = jf * 16 + mine
+    low_half = jf == 0
+
+    gain_one_f = join(attn_gain, "f").astype(f32)
+    inputs = hidden_in[0].astype(f32)
+    grad_out = cotangent[0].astype(f32)
+    scale_one = rms_scale(inputs)
+    norm_one = inputs * scale_one
+    h_one = (norm_one * gain_one_f).astype(bf16)
+    h_low, h_high = gather_ctx(
+        [h_one[:, :512], h_one[:, 512:]], [("a", "b", "c", "d"), ("c", "a", "b", "d")]
+    )
+    h_low = h_low.reshape(length, 512)
+    h_high = h_high.reshape(length, 512)
+
+    split_rows = query_key_value_weight.shape[0]
+    q_part = query_key_value_weight[:, :1024].reshape(split_rows, 16, 64)
+    k_part = query_key_value_weight[:, 1024:1536].reshape(split_rows, 8, 1, 64)
+    v_part = query_key_value_weight[:, 1536:].reshape(split_rows, 8, 1, 64)
+    kv_part = jnp.concatenate([k_part, v_part], 2).reshape(split_rows, 16, 64)
+    by_head = jnp.concatenate([q_part, kv_part], 2).reshape(split_rows, 2048)
+    my_slice = lax.dynamic_slice_in_dim(by_head, (mine // 2) * 256, 256, 1)
+    my_weight = join(my_slice, "f")
+    head_weight = jnp.concatenate(
+        [
+            jnp.where(idd == 0, my_weight[:, :64], my_weight[:, 128:192]),
+            my_weight[:, 64:128],
+            my_weight[:, 192:],
+            jnp.zeros((width, 64), bf16),
+        ],
+        1,
+    )
+    out_full = join(w_out, "f")
+    gain_two_f = join(ffn_gain, "f").astype(f32)
+    router_full = join(w_router, "f")
+    by_head_full = join(by_head, "f")
+
+    up_weight = lax.all_to_all(expert_in, CTX, split_axis=0, concat_axis=0, tiled=True).reshape(
+        width, 2 * F
+    )
+    down_weight = lax.all_to_all(
+        expert_out, CTX, split_axis=0, concat_axis=0, tiled=True
+    ).reshape(F, width)
+
+    order = block_order[0]
+    place = jnp.sum(
+        jnp.where(order[None, :] == jnp.arange(32, dtype=jnp.int32)[:, None],
+                  jnp.arange(32, dtype=jnp.int32)[None, :], 0),
+        axis=1,
+    )
+    document = segment_ids[0]
+    start = jnp.sum((document[:, None] < document[None, :]).astype(jnp.int32), axis=0)
+    first_key = start[::QUERY_BLOCK] // QUERY_BLOCK
+    start = start[None, :]
+    steps = jnp.arange(HEAD_SIZE // 2, dtype=f32)
+    frequency = jnp.power(THETA, -2.0 * steps / HEAD_SIZE)
+    coarse = (jnp.arange(length // 64, dtype=f32) * 64.0)[:, None] * frequency[None, :]
+    fine = jnp.arange(64, dtype=f32)[:, None] * frequency[None, :]
+    cos_a, sin_a = (jnp.cos(coarse)[:, None, :], jnp.sin(coarse)[:, None, :])
+    cos_b, sin_b = (jnp.cos(fine)[None], jnp.sin(fine)[None])
+    cosine = jnp.tile((cos_a * cos_b - sin_a * sin_b).reshape(length, 32), (1, 4))
+    sine = jnp.tile((sin_a * cos_b + cos_a * sin_b).reshape(length, 32), (1, 4))
+
+    query, key, value, mixed, attended_head = whole_call(
+        attention_forward,
+        2,
+        [
+            jax.ShapeDtypeStruct((length, 128), bf16),
+            jax.ShapeDtypeStruct((length, 128), bf16),
+            jax.ShapeDtypeStruct((length, 128), bf16),
+            jax.ShapeDtypeStruct((72, length), f32),
+            jax.ShapeDtypeStruct((length, 64), bf16),
+        ],
+        [pltpu.VMEM((128, length), bf16)],
+        32 << 20,
+    )(place, first_key, h_low, h_high, head_weight, cosine, sine, start)
+
+    def to_tokens(value_heads):
+        got = lax.all_to_all(
+            value_heads.reshape(16, rows, -1), CTX, split_axis=0, concat_axis=0, tiled=True
+        )
+        return got
+
+    attended = to_tokens(attended_head).transpose(1, 0, 2).reshape(rows, 1024)
+    middle_state = inputs + jnp.dot(attended, out_full, preferred_element_type=f32)
+    scale_two = rms_scale(middle_state)
+    norm_two = middle_state * scale_two
+    h_two = (norm_two * gain_two_f).astype(bf16)
+    logits = jnp.dot(h_two, router_full, preferred_element_type=f32)
+    route = routes[0]
+    named = jnp.any(route[:, :, None] == jnp.arange(E, dtype=jnp.int32)[None, None, :], axis=1)
+    top = jnp.max(jnp.where(named, logits, MASK_FILL_VALUE), axis=-1, keepdims=True)
+    weights = jnp.where(named, jnp.exp(logits - top), 0.0)
+    gates = weights / jnp.sum(weights, axis=-1, keepdims=True)
+
+    named_b = named.astype(bf16)
+    earlier = (
+        jnp.arange(rows)[:, None] > jnp.arange(rows)[None, :]
+    ).astype(bf16)
+    rank = jnp.dot(earlier, named_b, preferred_element_type=f32)
+    row_of = jnp.where(named, rank, -1.0)
+    row_pair = jnp.stack([row_of, swap(row_of, "a")])
+    half = row_pair.reshape(2, rows, 2, 2, 8)
+    half = jnp.where(ia == 0, half[:, :, :, 0], half[:, :, :, 1])
+    half = half.transpose(0, 3, 2, 1).reshape(2, 16, 1, rows)
+    pick = (half == jnp.arange(MOST, dtype=f32)[None, None, :, None]).astype(bf16)
+
+    def send_rows(choice, tokens):
+        built = lax.dot_general(
+            choice, tokens, (((2,), (0,)), ((), ())), preferred_element_type=f32
+        ).astype(bf16)
+        return lax.all_to_all(built, HALF, split_axis=0, concat_axis=0, tiled=True)
+
+    def take_rows(choice, sent):
+        got = lax.all_to_all(sent, HALF, split_axis=0, concat_axis=0, tiled=True)
+        return lax.dot_general(
+            choice, got, (((0, 1), (0, 1)), ((), ())), preferred_element_type=f32
+        )
+
+    extended = jnp.concatenate(
+        [h_two] + exact_parts(gates) + [jnp.zeros((rows, EXTRA - 3 * E), bf16)], 1
+    )
+    other_extended = swap(extended, "a")
+    rows_mine = send_rows(pick[0], extended)
+    rows_other = send_rows(pick[1], other_extended)
+    received = in_order(rows_mine[None], rows_other[None], "a", 0).reshape(
+        32 * MOST, width + EXTRA
+    )
+
+    columns = row_of.T.reshape(2, 16, rows).transpose(1, 0, 2).reshape(32, rows)
+    their_row = lax.all_to_all(columns, EVERY, split_axis=0, concat_axis=0, tiled=True)
+    their_count = jnp.sum((their_row >= 0).astype(f32), axis=1).reshape(16, 2)
+    before_me = (jnp.arange(16)[:, None] > jnp.arange(16)[None, :]).astype(f32)
+    offset = jnp.dot(before_me, their_count, precision=HIGHEST).reshape(32, 1)
+    their_count = their_count.reshape(32, 1)
+    row_number = jnp.arange(MOST, dtype=f32)[None, :]
+    kept = (row_number < their_count) & (row_number + offset < capacity)
+    kept = kept.astype(f32).reshape(32 * MOST, 1)
+    their_pick = (their_row[:, None, :] == row_number[:, :, None]).astype(bf16)
+    all_cotangent = lax.all_gather(cotangent[0], EVERY, axis=0, tiled=True).reshape(
+        32, rows, width
+    )
+    grad_rows = jnp.einsum(
+        "srt,stc->src", their_pick, all_cotangent, preferred_element_type=f32
+    ).astype(bf16).reshape(32 * MOST, width)
+
+    x_rows = received[:, :width]
+    lane = jnp.arange(EXTRA, dtype=jnp.int32)[None, :]
+    my_lane = ((lane % E) == expert) & (lane < 3 * E)
+    gate_rows = jnp.sum(
+        jnp.where(my_lane, received[:, width:].astype(f32), 0.0), axis=1, keepdims=True
+    )
+    before = jnp.dot(x_rows, up_weight, preferred_element_type=f32)
+    gate_pre = before[:, :F]
+    up_pre = before[:, F:]
+    sigma = jax.nn.sigmoid(gate_pre)
+    activation = (gate_pre * sigma * up_pre).astype(bf16)
+    result = jnp.dot(activation, down_weight, preferred_element_type=f32).astype(bf16)
+    result_f = result.astype(f32) * kept
+    grad_pair = (gate_rows * grad_rows.astype(f32) * kept).astype(bf16)
+    grad_gate_rows = jnp.sum(grad_rows.astype(f32) * result_f, axis=1, keepdims=True)
+    grad_activation = contract_columns(grad_pair, down_weight)
+    grad_down = contract_rows(activation, grad_pair)
+    grad_gate = grad_activation * up_pre * sigma * (1.0 + gate_pre * (1.0 - sigma))
+    grad_up = grad_activation * gate_pre * sigma
+    grad_pre = jnp.concatenate([grad_gate, grad_up], axis=-1).astype(bf16)
+    grad_copy = contract_columns(grad_pre, up_weight).astype(bf16)
+    grad_up_weight = contract_rows(x_rows, grad_pre)
+    gate_parts = exact_parts(grad_gate_rows)
+    extra = jnp.zeros((32 * MOST, EXTRA), bf16)
+    for number, part in enumerate(gate_parts):
+        extra = jnp.where(lane == expert + number * E, part, extra)
+    grad_copy = jnp.concatenate([grad_copy, extra], 1).reshape(2, 16, MOST, width + EXTRA)
+    gated_result = (gate_rows * result_f).astype(bf16).reshape(2, 16, MOST, width)
+
+    def give_back(by_half):
+        here = jnp.where(ia == 0, by_half[0], by_half[1])
+        there = jnp.where(ia == 0, by_half[1], by_half[0])
+        away = take_rows(pick[1], there).astype(bf16)
+        home = take_rows(pick[0], here)
+        return home + swap(away, "a").astype(f32)
+
+    back = give_back(grad_copy)
+    mixture = give_back(gated_result)
+    hidden_out = (middle_state + mixture).astype(bf16)
+    gate_grads = sum(
+        back[:, width + n * E : width + (n + 1) * E] for n in range(3)
+    )
+    grad_logits = gates * (gate_grads - jnp.sum(gates * gate_grads, axis=-1, keepdims=True))
+    grad_h_two = back[:, :width] + lax.dot_general(
+        grad_logits, router_full.astype(f32), (((1,), (1,)), ((), ())), precision=HIGHEST
+    )
+    grad_router_part = lax.dot_general(
+        grad_logits, h_two.astype(f32), (((0,), (0,)), ((), ())), precision=HIGHEST
+    )
+    grad_gain_two = jnp.sum(grad_h_two * norm_two, axis=0, keepdims=True)
+    scaled_two = grad_h_two * gain_two_f
+    grad_mid = grad_out + scale_two * (
+        scaled_two - norm_two * jnp.mean(scaled_two * norm_two, axis=-1, keepdims=True)
+    )
+    grad_branch = grad_mid.astype(bf16)
+    attended_gradient = contract_columns(grad_branch, out_full).astype(bf16)
+    grad_heads = to_tokens(
+        attended_gradient.reshape(rows, 16, 64).transpose(1, 0, 2)
+    ).reshape(length, 64)
+
+    all_branch = lax.all_gather(grad_branch, CTX, axis=0, tiled=True)
+    out_part = contract_rows(attended_head, all_branch)
+    out_part = (out_part + swap(out_part, "f")).astype(bf16)
+    out_all = gather_ctx(
+        [out_part[:, :512], out_part[:, 512:]], [("a", "b", "c", "d"), ("c", "a", "b", "d")]
+    )
+    out_all = jnp.concatenate(out_all, 2).reshape(2, 512, width)
+    share_out = jnp.where(low_half, out_all[0], out_all[1]).astype(f32)
+
+    small = sum_everywhere(
+        jnp.concatenate([grad_router_part, jnp.broadcast_to(grad_gain_two, (8, width))], 0)
+    )
+    small = jnp.where(low_half, small[:, :512], small[:, 512:])
+    share_router = small[:E].T
+    share_two = small[E]
+
+    pair_grad, value_grad = whole_call(
+        attention_backward,
+        2,
+        [jax.ShapeDtypeStruct((length, 128), f32), jax.ShapeDtypeStruct((length, 64), f32)],
+        [
+            pltpu.VMEM((64, length), bf16),
+            pltpu.VMEM((length, 128), f32),
+            pltpu.VMEM((length, 64), f32),
+        ],
+        32 << 20,
+    )(place, first_key, query, key, value, mixed, grad_heads, cosine, sine, start)
+    key_grad = pair_grad[:, 64:]
+    sent = jnp.where(idd == 0, value_grad, key_grad)
+    stays = jnp.where(idd == 0, key_grad, value_grad)
+    grad_columns = jnp.concatenate([pair_grad[:, :64], stays + swap(sent, "d")], 1).astype(bf16)
+
+    low_part = contract_rows(h_low, grad_columns)
+    high_part = contract_rows(h_high, grad_columns)
+    columns_grad = jnp.where(low_half, low_part, high_part) + swap(
+        jnp.where(low_half, high_part, low_part), "f"
+    )
+    columns_grad = columns_grad.astype(bf16)
+    qkv_all = gather_ctx(
+        [columns_grad[:256], columns_grad[256:]], [("a", "b", "c", "d"), ("c", "a", "b", "d")]
+    )
+    qkv_all = jnp.concatenate(qkv_all, 1).transpose(1, 0, 2).astype(f32)
+    kv_all = qkv_all[:, :, 64:].reshape(512, 8, 2, 64)
+    share_qkv = jnp.concatenate(
+        [
+            qkv_all[:, :, :64].reshape(512, 1024),
+            kv_all[:, :, 0].reshape(512, 512),
+            kv_all[:, :, 1].reshape(512, 512),
+        ],
+        1,
+    )
+
+    grad_projected = to_tokens(grad_columns)
+    grad_projected = grad_projected.transpose(1, 0, 2).reshape(rows, 2048)
+    grad_h_one = contract_columns(grad_projected, by_head_full)
+    grad_gain_one = sum_everywhere(jnp.sum(grad_h_one * norm_one, axis=0))
+    share_one = jnp.where(low_half, grad_gain_one[:512], grad_gain_one[512:])
+    scaled_one = grad_h_one * gain_one_f
+    grad_inputs = grad_mid + scale_one * (
+        scaled_one - norm_one * jnp.mean(scaled_one * norm_one, axis=-1, keepdims=True)
+    )
+
+    grad_expert_in = lax.all_to_all(
+        grad_up_weight.astype(bf16).reshape(16, 64, 2 * F), CTX,
+        split_axis=0, concat_axis=0, tiled=True,
+    ).astype(f32)
+    grad_expert_out = lax.all_to_all(
+        grad_down.astype(bf16).reshape(16, 32, width), CTX,
+        split_axis=0, concat_axis=0, tiled=True,
+    ).astype(f32)
+    return (
+        hidden_out[None],
+        grad_inputs[None],
+        share_one,
+        share_qkv,
+        share_out,
+        share_two,
+        share_router,
+        grad_expert_in,
+        grad_expert_out,
+    )
+
+
+def fast_solution(mesh):
+    fine = Mesh(mesh.devices.reshape(2, 2, 2, 2, 2), EVERY)
+    placed = (
+        P("f", CTX, None),
+        P("f", None),
+        P("f", None),
+        P("f", CTX, None),
+        P("f"),
+        P("f", None),
+        P("f", None),
+        P("f"),
+        P("f", None),
+        P("f", CTX, None),
+        P("f", CTX, None),
+        P("f", CTX, None),
+    )
+    return jax.shard_map(
+        fast_shards,
+        mesh=fine,
+        in_specs=placed,
+        out_specs=(
+            P("f", CTX, None),
+            P("f", CTX, None),
+            P("f"),
+            P("f", None),
+            P("f", None),
+            P("f"),
+            P("f", None),
+            P("f", CTX, None),
+            P("f", CTX, None),
+        ),
+        check_vma=False,
+    )
+
+
+def solution(mesh):
+    if mesh.shape["ctx"] == QUERY_HEADS and mesh.shape["fsdp"] * mesh.shape["ctx"] == E:
+        return fast_solution(mesh)
+    return general_solution(mesh)

time: 1510 us -> 704 us (0.47)
  waiting for transfers between devices: 1020 us -> 294 us
  starting transfers between devices: 20.4 us -> 119 us
  matrix products: 149 us -> 79.2 us
  local copies, waits for them, and re-layouts: 128 us -> 59.1 us
  blocking collectives: 100 us -> 45.3 us
  Pallas kernels: 0 us -> 27 us
    reduce_scatter x2 -> x0, waiting for transfers between devices: 506 us -> none  [the longest x1 333 us: shards(): lax.psum_scatter(grad_up_weight.astype(jnp.bfloat16), 'ctx', scatter_dime...]
    ppermute x0 -> x47, waiting for transfers between devices: none -> 219 us  [swap(): return lax.ppermute(value, axis, [(0, 1), (1, 0)])]
    all_gather x5 -> x2, waiting for transfers between devices: 196 us -> 0.02 us  [the longest x1 0.02 us: fast_shards(): all_branch = lax.all_gather(grad_branch, CTX, axis=0, tiled=True)]
    psum x1 -> x0, waiting for transfers between devices: 158 us -> none  [shards(): lax.psum((grad_gain_one, grad_qkv_weight, grad_out_weight, grad_gain_two,...]
    dot_general x25 -> x15, matrix products: 137 us -> 40.5 us  [the longest x1 8.68 us: fast_shards(): before = jnp.dot(x_rows, up_weight, preferred_element_type=f32)]
    unnamed x10 -> x2, waiting for transfers between devices: 67.9 us -> 1.17 us
    ppermute x0 -> x47, starting transfers between devices: none -> 54.2 us  [swap(): return lax.ppermute(value, axis, [(0, 1), (1, 0)])]
    all_gather x3 -> x0, blocking collectives: 46.8 us -> none  [the longest x1 37.2 us: shards(): lax.all_gather(w_router, 'fsdp', axis=0, tiled=True)]
  transfers between devices with their start and end apart: 13 -> 61, of which waited for: 11 -> 34; matrix products, arithmetic and copies ran while one was open for 13% -> 22% of each run, Pallas kernels for 0% -> 4%
where the time goes in v1:
time: 704 us; the launch traced here: 693 us
  waiting for transfers between devices  294 us (42%)
  starting transfers between devices  119 us (17%)
  matrix products  79.2 us (11%)
  local copies, waits for them, and re-layouts  59.1 us (8%)
  other arithmetic  53.7 us (8%)
  blocking collectives  45.3 us (6%)
  Pallas kernels  27 us (4%)
  between operations  15.9 us (2%)
    ppermute x47, waiting for transfers between devices, swap(): return lax.ppermute(value, axis, [(0, 1), (1, 0)])  219 us
    ppermute x47, starting transfers between devices, swap(): return lax.ppermute(value, axis, [(0, 1), (1, 0)])  54.2 us
    all_to_all x3, waiting for transfers between devices, take_rows(): got = lax.all_to_all(sent, HALF, split_axis=0, concat_axis=0, tiled=True)  28.8 us
    all_to_all x1, blocking collectives, take_rows(): got = lax.all_to_all(sent, HALF, split_axis=0, concat_axis=0, tiled=True)  28.2 us
    pallas_call x2, Pallas kernels, run(): pl.pallas_call(kernel, out_shape=outs, grid_spec=pltpu.PrefetchScalarGrid...  27 us
    unnamed x116, local copies, waits for them, and re-layouts  24.2 us
    all_to_all x2, waiting for transfers between devices, send_rows(): return lax.all_to_all(built, HALF, split_axis=0, concat_axis=0, tiled=True)  22.8 us
    dot_general x4, matrix products, contract_columns(): lax.dot_general(left, right, (((1,), (1,)), ((), ())), preferred_element_...  22.7 us
  transfers between devices with their start and end apart: 61, of which 34 were waited for; matrix products, arithmetic and copies ran while one was open for 22% of the time, Pallas kernels for 4%

profile of v1, /device:TPU:0, one launch (start us, length us, event | category | flops | bytes accessed | tf_op | source)
XLA Modules:
  0.0 693.1 jit_solution(2154625473813975026)
XLA Ops:
  7.2 3.0 collective-permute-start
  19.7 6.4 all-to-all-start.5
  29.1 2.7 collective-permute-start.1
  33.5 5.0 collective-permute-done.1
  39.3 3.4 collective-permute-start.6
  44.3 12.1 %collective-permute-done.2 = bf16[2,1,1,1,128,512]{5,4,3,2,1,0:T(8,128)(2,1)S(1)} collective-permute-done((bf16[2,1,1,1,128,512]{5,4,3,2,1,0:T(8,128)(2,1)S(1)}, bf16[2,1,1,1,128,512]{5,4,3,2,1,0:T(8,128)(2,1)S(1)}, u32[]{:S(2)}, u32[]{:S(2)}) %collective-permute-start.2) | collective-permute-done | bytes 262176 | tf_op jit(solution)/shard_map/ppermute | solution.py:466
  65.7 7.0 %collective-permute-done.3 = bf16[2,2,1,1,128,512]{5,4,3,2,1,0:T(8,128)(2,1)} collective-permute-done((bf16[2,2,1,1,128,512]{5,4,3,2,1,0:T(8,128)(2,1)}, bf16[2,2,1,1,128,512]{5,4,3,2,1,0:T(8,128)(2,1)}, u32[]{:S(2)}, u32[]{:S(2)}) %collective-permute-start.3) | collective-permute-done | bytes 524320 | tf_op jit(solution)/shard_map/ppermute | solution.py:466
  74.3 9.2 %collective-permute-done.7 = bf16[2,1,2,1,128,512]{5,4,3,2,1,0:T(8,128)(2,1)} collective-permute-done((bf16[2,1,2,1,128,512]{5,4,3,2,1,0:T(8,128)(2,1)}, bf16[2,1,2,1,128,512]{5,4,3,2,1,0:T(8,128)(2,1)}, u32[]{:S(2)}, u32[]{:S(2)}) %collective-permute-start.7) | collective-permute-done | bytes 524320 | tf_op jit(solution)/shard_map/ppermute | solution.py:466
  88.1 14.5 %shard_map.187 = (bf16[2048,128]{1,0:T(8,128)(2,1)S(1)}, bf16[2048,128]{1,0:T(8,128)(2,1)S(1)}, bf16[2048,128]{1,0:T(8,128)(2,1)S(1)}, f32[72,2048]{1,0:T(8,128)S(1)}, bf16[2048,64]{1,0:T(8,128)(2,1)S(1)}) custom-call(s32[32]{0:T(128)S(1)} %select_reduce_fusion.2.place, s32[8]{0:T(128)S(1)} %and_select_fusion.1.first_key, bf16[2048,512]{1,0:T(8,128)(2,1)S(1)} %bitcast.263, ...), custom_call_target="tpu_custom_call" | custom-call | tf_op jit(solution)/shard_map/pallas_call | solution.py:681
  107.9 17.1 %all_to_all.77 = bf16[16,128,64]{1,2,0:T(8,128)(2,1)} all-to-all(bf16[16,128,64]{1,2,0:T(8,128)(2,1)S(1)} %copy.145), channel_id=1, replica_groups=mesh['a'=2,'b'=2,'c'=2,'d'=2,'f'=2] {'a','b','c','d'}, dimensions={0} | all-to-all | bytes 524288 | tf_op jit(solution)/shard_map/all_to_all | solution.py:786
  125.0 4.4 all-to-all-start.3
  131.6 2.6 collective-permute-start.11
  135.9 19.6 %collective-permute-done.12 = bf16[512]{0:T(512)(128)(2,1)S(1)} collective-permute-done((bf16[512]{0:T(512)(128)(2,1)S(1)}, bf16[512]{0:T(512)(128)(2,1)S(1)}, u32[]{:S(2)}, u32[]{:S(2)}) %collective-permute-start.12) | collective-permute-done | bytes 1056 | tf_op jit(solution)/shard_map/ppermute | solution.py:466
  155.5 23.6 %collective-permute-done.11 = f32[128,32]{0,1:T(8,128)S(1)} collective-permute-done((f32[128,32]{0,1:T(8,128)S(1)}, f32[128,32]{0,1:T(8,128)S(1)}, u32[]{:S(2)}, u32[]{:S(2)}) %collective-permute-start.11) | collective-permute-done | bytes 16416 | tf_op jit(solution)/shard_map/ppermute | solution.py:466
  179.3 3.3 multiply_reduce_fusion.2
  188.7 2.8 convolution_convert_fusion.3
  191.4 4.9 all-to-all-start.1
  197.3 27.6 %collective-permute-done.14 = bf16[128,1152]{1,0:T(8,128)(2,1)S(1)} collective-permute-done((bf16[128,1152]{1,0:T(8,128)(2,1)}, bf16[128,1152]{1,0:T(8,128)(2,1)S(1)}, u32[]{:S(2)}, u32[]{:S(2)}) %collective-permute-start.14) | collective-permute-done | bytes 294944 | tf_op jit(solution)/shard_map/ppermute | solution.py:466
  226.7 5.5 all-to-all-start.2
  232.8 22.8 %all-to-all-done.2 = bf16[16,48,1152]{2,1,0:T(8,128)(2,1)} async-done(((bf16[16,48,1152]{2,1,0:T(8,128)(2,1)}), bf16[16,48,1152]{2,1,0:T(8,128)(2,1)}, u32[]{:S(2)}, u32[]{:S(2)}) %all-to-all-start.2) | async-done | bytes 1769504 | tf_op jit(solution)/shard_map/all_to_all | solution.py:819
  255.6 6.0 all-to-all-start.4
  261.6 3.8 maximum_select_fusion.2
  267.4 8.7 %fusion.14 = f32[1536,1024]{0,1:T(8,128)} fusion(bf16[1024,1024]{1,0:T(8,128)(2,1)} %bitcast.47, bf16[1536,1152]{1,0:T(8,128)(2,1)} %bitcast.282), kind=kOutput, calls=%fused_computation.35 | convolution fusion | flops 3221225472 | bytes 11534336 | tf_op jit(solution)/shard_map/dot_general | solution.py:860
  276.1 7.6 %fusion.1 = (bf16[32,48,1024]{2,1,0:T(8,128)(2,1)}, bf16[32,48,1024]{2,1,0:T(8,128)(2,1)}) fusion(f32[32,48]{1,0:T(8,128)S(1)} %fusion.64, f32[32,48]{1,0:T(8,128)S(1)} %mul.402, bf16[32,128,1024]{2,1,0:T(8,128)(2,1)} %bitcast.271, f32[32,128]{1,0:T(8,128)S(1)} %bitcast.317), kind=kOutput, calls=%fused_computation.5 | convolution fusion | flops 410714112 | bytes 14708736 | tf_op jit(solution)/shard_map/srt,stc->src/dot_general | solution.py:850
  284.6 8.7 %multiply_convert_fusion.2 = (bf16[1536,512]{0,1:T(8,128)(2,1)}, bf16[1536,512]{0,1:T(8,128)(2,1)}, bf16[1536,512]{0,1:T(8,128)(2,1)S(1)}) fusion(f32[1536,1024]{0,1:T(8,128)} %fusion.14, bf16[1536,1024]{1,0:T(8,128)(2,1)} %bitcast.294, bf16[512,1024]{1,0:T(8,128)(2,1)} %bitcast.48), kind=kOutput, calls=%fused_computation.30 | convolution fusion | flops 1623195648 | bytes 15204352 | tf_op jit(solution)/shard_map/dot_general | solution.py:68
  293.3 5.6 fusion.4
  298.9 2.8 convolution_convert_fusion.5
  301.7 6.9 all-to-all-start.13
  308.6 3.8 broadcast_select_fusion.3
  312.4 19.2 %all-to-all-done.13 = bf16[16,32,1024]{2,1,0:T(8,128)(2,1)} async-done(((bf16[16,32,1024]{2,1,0:T(8,128)(2,1)}), bf16[16,32,1024]{2,1,0:T(8,128)(2,1)}, u32[]{:S(2)}, u32[]{:S(2)}) %all-to-all-start.13) | async-done | bytes 1048608 | tf_op jit(solution)/shard_map/all_to_all | solution.py:980
  331.6 6.2 all-to-all-start.7
  338.0 5.9 convolution_convert_fusion.1
  346.1 3.9 copy.153
  350.0 9.1 %all-to-all-done.7 = bf16[16,48,1024]{2,1,0:T(8,128)(2,1)} async-done(((bf16[16,48,1024]{2,1,0:T(8,128)(2,1)}), bf16[16,48,1024]{2,1,0:T(8,128)(2,1)}, u32[]{:S(2)}, u32[]{:S(2)}) %all-to-all-start.7) | async-done | bytes 1572896 | tf_op jit(solution)/shard_map/all_to_all | solution.py:822
  359.1 4.4 all-to-all-start.9
  363.5 3.9 copy.152
  367.4 19.7 %all-to-all-done.9 = bf16[16,48,1152]{2,1,0:T(8,128)(2,1)} async-done(((bf16[16,48,1152]{2,1,0:T(8,128)(2,1)}), bf16[16,48,1152]{2,1,0:T(8,128)(2,1)}, u32[]{:S(2)}, u32[]{:S(2)}) %all-to-all-start.9) | async-done | bytes 1769504 | tf_op jit(solution)/shard_map/all_to_all | solution.py:822
  387.1 28.2 %all_to_all.78 = bf16[16,48,1152]{2,1,0:T(8,128)(2,1)} all-to-all(bf16[16,48,1152]{2,1,0:T(8,128)(2,1)} %bitcast.278), channel_id=1, replica_groups=mesh['a'=2,'b'=2,'c'=2,'d'=2,'f'=2] {'b','c','d','f'}, dimensions={0} | all-to-all | bytes 3538944 | tf_op jit(solution)/shard_map/all_to_all | solution.py:822
  415.3 4.4 all-to-all-start.6
  421.8 3.3 collective-permute-start.16
  425.1 20.8 %collective-permute-done.16 = bf16[128,1152]{1,0:T(8,128)(2,1)S(1)} collective-permute-done((bf16[128,1152]{1,0:T(8,128)(2,1)S(1)}, bf16[128,1152]{1,0:T(8,128)(2,1)S(1)}, u32[]{:S(2)}, u32[]{:S(2)}) %collective-permute-start.16) | collective-permute-done | bytes 294944 | tf_op jit(solution)/shard_map/ppermute | solution.py:466
  450.4 3.9 convolution_convert_fusion.6
  456.1 6.3 all-to-all-start.10
  462.4 7.6 %fusion.17 = bf16[1024,1024]{1,0:T(8,128)(2,1)} fusion(bf16[1536,512]{0,1:T(8,128)(2,1)} %get-tuple-element.59, bf16[1536,512]{0,1:T(8,128)(2,1)} %get-tuple-element.58, bf16[1536,1152]{1,0:T(8,128)(2,1)} %bitcast.283), kind=kOutput, calls=%fused_computation.47 | convolution fusion | flops 3228565504 | bytes 8388608 | tf_op jit(solution)/shard_map/dot_general | solution.py:62
  472.5 4.4 all-to-all-start.12
  482.5 4.6 collective-permute-done.43
  497.3 12.4 %shard_map.188 = (f32[2048,128]{1,0:T(8,128)S(1)}, f32[2048,64]{1,0:T(8,128)S(1)}) custom-call(s32[32]{0:T(128)S(1)} %select_reduce_fusion.2.place, s32[8]{0:T(128)S(1)} %and_select_fusion.1.first_key, bf16[2048,128]{1,0:T(8,128)(2,1)S(1)} %copy-done.13, bf16[2048,128]{1,0:T(8,128)(2,1)S(1)} %copy-done.15, bf16[2048,128]{1,0:T(8,128)(2,1)S(1)} %copy-done.17, ...), custom_call_target="tpu_custom_call" | custom-call | tf_op jit(solution)/shard_map/pallas_call | solution.py:681
  521.5 2.8 convert_element_type.236
  524.3 8.6 %collective-permute-done.45 = f32[40,1024]{1,0:T(8,128)S(1)} collective-permute-done((f32[40,1024]{1,0:T(8,128)S(1)}, f32[40,1024]{1,0:T(8,128)S(1)}, u32[]{:S(2)}, u32[]{:S(2)}) %collective-permute-start.45) | collective-permute-done | bytes 163872 | tf_op jit(solution)/shard_map/ppermute | solution.py:466
  532.9 4.9 collective-permute-start.46
  537.8 28.5 %collective-permute-done.15 = bf16[128,1024]{1,0:T(8,128)(2,1)S(1)} collective-permute-done((bf16[128,1024]{1,0:T(8,128)(2,1)S(1)}, bf16[128,1024]{1,0:T(8,128)(2,1)S(1)}, u32[]{:S(2)}, u32[]{:S(2)}) %collective-permute-start.15) | collective-permute-done | bytes 262176 | tf_op jit(solution)/shard_map/ppermute | solution.py:466
  566.3 2.5 fusion.41
  568.9 4.2 convert_element_type.233
  588.3 4.6 all-to-all-start.11
  602.6 11.5 %collective-permute-done.25 = bf16[1,1,1,1,256,128]{5,4,3,2,1,0:T(8,128)(2,1)S(1)} collective-permute-done((bf16[1,1,1,1,256,128]{5,4,3,2,1,0:T(8,128)(2,1)S(1)}, bf16[1,1,1,1,256,128]{5,4,3,2,1,0:T(8,128)(2,1)S(1)}, u32[]{:S(2)}, u32[]{:S(2)}) %collective-permute-start.25) | collective-permute-done | bytes 65568 | tf_op jit(solution)/shard_map/ppermute | solution.py:466
  621.0 4.1 fusion.34
  630.7 2.9 collective-permute-done.21
  633.6 3.6 collective-permute-done.22
  638.3 3.4 collective-permute-done.23
  642.5 3.0 fusion.96
  654.3 6.1 collective-permute-done.34
  662.8 5.5 collective-permute-done.35
  669.2 5.5 collective-permute-done.36
  678.3 5.3 copy.174
  (350 shorter events, 150.5 us)
Async XLA Ops:
  7.2 21.7 %collective-permute-start = (bf16[512]{0:T(512)(128)(2,1)}, bf16[512]{0:T(512)(128)(2,1)S(1)}, u32[]{:S(2)}, u32[]{:S(2)}) collective-permute-start(bf16[512]{0:T(512)(128)(2,1)} %param.16), channel_id=1, source_target_pairs={{0,1},{1,0},{2,3},{3,2},{4,5},{5,4},{6,7},{7,6},{8,9},{9,8},{10,11... | collective-permute-start | bytes 3080 | tf_op jit(solution)/shard_map/ppermute | solution.py:466
  18.8 66.1 %collective-permute-start.9 = (bf16[512,256]{1,0:T(8,128)(2,1)S(1)}, bf16[512,256]{1,0:T(8,128)(2,1)}, u32[]{:S(2)}, u32[]{:S(2)}) collective-permute-start(bf16[512,256]{1,0:T(8,128)(2,1)S(1)} %constant_dynamic-slice_fusion), channel_id=1, source_target_pairs={{0,1},{1,0},{2,3},{3,2},{4,5},{5,4},{6,7},{7,6},{8,9},{9,8},{10,11... | collective-permute-start | bytes 786440 | tf_op jit(solution)/shard_map/ppermute | solution.py:466
  19.7 88.2 %all-to-all-start.5 = ((f32[32,1,128]{2,1,0:T(1,128)}), f32[32,1,128]{2,1,0:T(1,128)S(1)}, u32[]{:S(2)}, u32[]{:S(2)}) async-start(f32[32,1,128]{2,1,0:T(1,128)} %bitcast.53), calls=%async_computation.5 | async-start | bytes 32768 | tf_op jit(solution)/shard_map/all_to_all | solution.py:838
  26.1 250.0 %all-gather.6.cloned.1.call-start = ((), (), s32[]{:S(2)}) async-start(), calls=%async_computation.15 | async-start | bytes 8650752 | tf_op jit(solution)/shard_map/all_gather | solution.py:847
  29.1 9.4 %collective-permute-start.1 = (bf16[1,1,1,1,128,512]{5,4,3,2,1,0:T(8,128)(2,1)S(1)}, bf16[1,1,1,1,128,512]{5,4,3,2,1,0:T(8,128)(2,1)S(1)}, u32[]{:S(2)}, u32[]{:S(2)}) collective-permute-start(bf16[1,1,1,1,128,512]{5,4,3,2,1,0:T(8,128)(2,1)S(1)} %get-tuple-element.81), channel_id=1, source_target_pairs={{0,16},{16,0},{1,17},{17,1},{2,18},{18,2},{3,19},{19,3},{4,20},{20... | collective-permute-start | bytes 393224 | tf_op jit(solution)/shard_map/ppermute | solution.py:466
  31.8 7.4 %collective-permute-start.5 = (bf16[1,1,1,1,128,512]{5,4,3,2,1,0:T(8,128)(2,1)S(1)}, bf16[1,1,1,1,128,512]{5,4,3,2,1,0:T(8,128)(2,1)S(1)}, u32[]{:S(2)}, u32[]{:S(2)}) collective-permute-start(bf16[1,1,1,1,128,512]{5,4,3,2,1,0:T(8,128)(2,1)S(1)} %get-tuple-element.82), channel_id=1, source_target_pairs={{0,4},{4,0},{1,5},{5,1},{2,6},{6,2},{3,7},{7,3},{8,12},{12,8},{9,1... | collective-permute-start | bytes 393224 | tf_op jit(solution)/shard_map/ppermute | solution.py:466
  38.6 17.8 %collective-permute-start.2 = (bf16[2,1,1,1,128,512]{5,4,3,2,1,0:T(8,128)(2,1)S(1)}, bf16[2,1,1,1,128,512]{5,4,3,2,1,0:T(8,128)(2,1)S(1)}, u32[]{:S(2)}, u32[]{:S(2)}) collective-permute-start(bf16[2,1,1,1,128,512]{5,4,3,2,1,0:T(8,128)(2,1)S(1)} %maximum_select_fusion.23), channel_id=1, source_target_pairs={{0,8},{8,0},{1,9},{9,1},{2,10},{10,2},{3,11},{11,3},{4,12},{12,4},... | collective-permute-start | bytes 786440 | tf_op jit(solution)/shard_map/ppermute | solution.py:466
  39.3 20.9 %collective-permute-start.6 = (bf16[1,1,2,1,128,512]{5,4,3,2,1,0:T(8,128)(2,1)S(1)}, bf16[1,1,2,1,128,512]{5,4,3,2,1,0:T(8,128)(2,1)S(1)}, u32[]{:S(2)}, u32[]{:S(2)}) collective-permute-start(bf16[1,1,2,1,128,512]{5,4,3,2,1,0:T(8,128)(2,1)S(1)} %maximum_select_fusion.25), channel_id=1, source_target_pairs={{0,16},{16,0},{1,17},{17,1},{2,18},{18,2},{3,19},{19,3},{4,20},{20... | collective-permute-start | bytes 786440 | tf_op jit(solution)/shard_map/ppermute | solution.py:466
  57.3 15.5 %collective-permute-start.3 = (bf16[2,2,1,1,128,512]{5,4,3,2,1,0:T(8,128)(2,1)}, bf16[2,2,1,1,128,512]{5,4,3,2,1,0:T(8,128)(2,1)}, u32[]{:S(2)}, u32[]{:S(2)}) collective-permute-start(bf16[2,2,1,1,128,512]{5,4,3,2,1,0:T(8,128)(2,1)} %maximum_select_fusion.13), channel_id=1, source_target_pairs={{0,4},{4,0},{1,5},{5,1},{2,6},{6,2},{3,7},{7,3},{8,12},{12,8},{9,1... | collective-permute-start | bytes 1572872 | tf_op jit(solution)/shard_map/ppermute | solution.py:466
  61.1 22.3 %collective-permute-start.7 = (bf16[2,1,2,1,128,512]{5,4,3,2,1,0:T(8,128)(2,1)}, bf16[2,1,2,1,128,512]{5,4,3,2,1,0:T(8,128)(2,1)}, u32[]{:S(2)}, u32[]{:S(2)}) collective-permute-start(bf16[2,1,2,1,128,512]{5,4,3,2,1,0:T(8,128)(2,1)} %fusion.37), channel_id=1, source_target_pairs={{0,8},{8,0},{1,9},{9,1},{2,10},{10,2},{3,11},{11,3},{4,12},{12,4},... | collective-permute-start | bytes 1572872 | tf_op jit(solution)/shard_map/ppermute | solution.py:466
  74.1 12.5 %collective-permute-start.4 = (bf16[2,2,2,1,128,512]{5,4,3,2,1,0:T(8,128)(2,1)S(1)}, bf16[2,2,2,1,128,512]{5,4,3,2,1,0:T(8,128)(2,1)S(1)}, u32[]{:S(2)}, u32[]{:S(2)}) collective-permute-start(bf16[2,2,2,1,128,512]{5,4,3,2,1,0:T(8,128)(2,1)S(1)} %maximum_select_fusion.6), channel_id=1, source_target_pairs={{0,2},{2,0},{1,3},{3,1},{4,6},{6,4},{5,7},{7,5},{8,10},{10,8},{9,1... | collective-permute-start | bytes 3145736 | tf_op jit(solution)/shard_map/ppermute | solution.py:466
  84.8 2.7 collective-permute-start.8
  125.0 66.4 %all-to-all-start.3 = ((bf16[16,64,1024]{2,1,0:T(8,128)(2,1)}), bf16[16,64,1024]{2,1,0:T(8,128)(2,1)}, u32[]{:S(2)}, u32[]{:S(2)}) async-start(bf16[16,64,1024]{2,1,0:T(8,128)(2,1)} %param.22), calls=%async_computation.3 | async-start | bytes 4194304 | tf_op jit(solution)/shard_map/all_to_all | solution.py:745
  129.5 49.8 %collective-permute-start.10 = (bf16[512,1024]{1,0:T(8,128)(2,1)}, bf16[512,1024]{1,0:T(8,128)(2,1)}, u32[]{:S(2)}, u32[]{:S(2)}) collective-permute-start(bf16[512,1024]{1,0:T(8,128)(2,1)} %param.18), channel_id=1, source_target_pairs={{0,1},{1,0},{2,3},{3,2},{4,5},{5,4},{6,7},{7,6},{8,9},{9,8},{10,11... | collective-permute-start | bytes 3145736 | tf_op jit(solution)/shard_map/ppermute | solution.py:466
  131.1 24.3 %collective-permute-start.12 = (bf16[512]{0:T(512)(128)(2,1)S(1)}, bf16[512]{0:T(512)(128)(2,1)S(1)}, u32[]{:S(2)}, u32[]{:S(2)}) collective-permute-start(bf16[512]{0:T(512)(128)(2,1)S(1)} %copy-done.53), channel_id=1, source_target_pairs={{0,1},{1,0},{2,3},{3,2},{4,5},{5,4},{6,7},{7,6},{8,9},{9,8},{10,11... | collective-permute-start | bytes 3080 | tf_op jit(solution)/shard_map/ppermute | solution.py:466
  131.6 47.5 %collective-permute-start.11 = (f32[128,32]{0,1:T(8,128)S(1)}, f32[128,32]{0,1:T(8,128)S(1)}, u32[]{:S(2)}, u32[]{:S(2)}) collective-permute-start(f32[128,32]{0,1:T(8,128)S(1)} %convolution_select_fusion), channel_id=1, source_target_pairs={{0,16},{16,0},{1,17},{17,1},{2,18},{18,2},{3,19},{19,3},{4,20},{20... | collective-permute-start | bytes 49160 | tf_op jit(solution)/shard_map/ppermute | solution.py:466
  134.2 49.3 %collective-permute-start.13 = (bf16[512,32]{0,1:T(8,128)(2,1)S(1)}, bf16[512,32]{0,1:T(8,128)(2,1)S(1)}, u32[]{:S(2)}, u32[]{:S(2)}) collective-permute-start(bf16[512,32]{0,1:T(8,128)(2,1)S(1)} %copy-done.42), channel_id=1, source_target_pairs={{0,1},{1,0},{2,3},{3,2},{4,5},{5,4},{6,7},{7,6},{8,9},{9,8},{10,11... | collective-permute-start | bytes 98312 | tf_op jit(solution)/shard_map/ppermute | solution.py:466
  191.4 35.3 %all-to-all-start.1 = ((bf16[16,48,1152]{2,1,0:T(8,128)(2,1)}), bf16[16,48,1152]{2,1,0:T(8,128)(2,1)}, u32[]{:S(2)}, u32[]{:S(2)}) async-start(bf16[16,48,1152]{2,1,0:T(8,128)(2,1)} %convolution_convert_fusion.3), calls=%async_computation.1 | async-start | bytes 3538944 | tf_op jit(solution)/shard_map/all_to_all | solution.py:819
  196.3 28.5 %collective-permute-start.14 = (bf16[128,1152]{1,0:T(8,128)(2,1)}, bf16[128,1152]{1,0:T(8,128)(2,1)S(1)}, u32[]{:S(2)}, u32[]{:S(2)}) collective-permute-start(bf16[128,1152]{1,0:T(8,128)(2,1)} %concatenate.1219), channel_id=1, source_target_pairs={{0,16},{16,0},{1,17},{17,1},{2,18},{18,2},{3,19},{19,3},{4,20},{20... | collective-permute-start | bytes 884744 | tf_op jit(solution)/shard_map/ppermute | solution.py:466
  226.7 28.9 %all-to-all-start.2 = ((bf16[16,48,1152]{2,1,0:T(8,128)(2,1)}), bf16[16,48,1152]{2,1,0:T(8,128)(2,1)}, u32[]{:S(2)}, u32[]{:S(2)}) async-start(bf16[16,48,1152]{2,1,0:T(8,128)(2,1)} %convolution_convert_fusion.2), calls=%async_computation.2 | async-start | bytes 3538944 | tf_op jit(solution)/shard_map/all_to_all | solution.py:819
  255.6 29.0 %all-to-all-start.4 = ((bf16[16,32,1024]{2,1,0:T(8,128)(2,1)}), bf16[16,32,1024]{2,1,0:T(8,128)(2,1)}, u32[]{:S(2)}, u32[]{:S(2)}) async-start(bf16[16,32,1024]{2,1,0:T(8,128)(2,1)} %param.23), calls=%async_computation.4 | async-start | bytes 2097152 | tf_op jit(solution)/shard_map/all_to_all | solution.py:748
  301.7 29.9 %all-to-all-start.13 = ((bf16[16,32,1024]{2,1,0:T(8,128)(2,1)}), bf16[16,32,1024]{2,1,0:T(8,128)(2,1)}, u32[]{:S(2)}, u32[]{:S(2)}) async-start(bf16[16,32,1024]{2,1,0:T(8,128)(2,1)} %bitcast.304), calls=%async_computation.13 | async-start | bytes 2097152 | tf_op jit(solution)/shard_map/all_to_all | solution.py:980
  331.6 27.5 %all-to-all-start.7 = ((bf16[16,48,1024]{2,1,0:T(8,128)(2,1)}), bf16[16,48,1024]{2,1,0:T(8,128)(2,1)}, u32[]{:S(2)}, u32[]{:S(2)}) async-start(bf16[16,48,1024]{2,1,0:T(8,128)(2,1)} %bitcast.280), calls=%async_computation.7 | async-start | bytes 3145728 | tf_op jit(solution)/shard_map/all_to_all | solution.py:822
  359.1 28.0 %all-to-all-start.9 = ((bf16[16,48,1152]{2,1,0:T(8,128)(2,1)}), bf16[16,48,1152]{2,1,0:T(8,128)(2,1)}, u32[]{:S(2)}, u32[]{:S(2)}) async-start(bf16[16,48,1152]{2,1,0:T(8,128)(2,1)} %bitcast.277), calls=%async_computation.9 | async-start | bytes 3538944 | tf_op jit(solution)/shard_map/all_to_all | solution.py:822
  415.3 40.8 %all-to-all-start.6 = ((bf16[16,48,1024]{2,1,0:T(8,128)(2,1)}), bf16[16,48,1024]{2,1,0:T(8,128)(2,1)}, u32[]{:S(2)}, u32[]{:S(2)}) async-start(bf16[16,48,1024]{2,1,0:T(8,128)(2,1)} %bitcast.279), calls=%async_computation.6 | async-start | bytes 3145728 | tf_op jit(solution)/shard_map/all_to_all | solution.py:822
  421.8 24.1 %collective-permute-start.16 = (bf16[128,1152]{1,0:T(8,128)(2,1)S(1)}, bf16[128,1152]{1,0:T(8,128)(2,1)S(1)}, u32[]{:S(2)}, u32[]{:S(2)}) collective-permute-start(bf16[128,1152]{1,0:T(8,128)(2,1)S(1)} %fusion.16), channel_id=1, source_target_pairs={{0,16},{16,0},{1,17},{17,1},{2,18},{18,2},{3,19},{19,3},{4,20},{20... | collective-permute-start | bytes 884744 | tf_op jit(solution)/shard_map/ppermute | solution.py:466
  456.1 16.4 %all-to-all-start.10 = ((bf16[16,128,64]{1,2,0:T(8,128)(2,1)}), bf16[16,128,64]{1,2,0:T(8,128)(2,1)}, u32[]{:S(2)}, u32[]{:S(2)}) async-start(bf16[16,128,64]{1,2,0:T(8,128)(2,1)} %bitcast.305), calls=%async_computation.10 | async-start | bytes 524288 | tf_op jit(solution)/shard_map/all_to_all | solution.py:786
  472.5 96.4 %all-to-all-start.12 = ((bf16[16,64,1024]{2,1,0:T(8,128)(2,1)}), bf16[16,64,1024]{2,1,0:T(8,128)(2,1)}, u32[]{:S(2)}, u32[]{:S(2)}) async-start(bf16[16,64,1024]{2,1,0:T(8,128)(2,1)} %bitcast.297), calls=%async_computation.12 | async-start | bytes 4194304 | tf_op jit(solution)/shard_map/all_to_all | solution.py:976
  476.9 165.5 %all-gather.4.cloned.1.call-start = ((), (), s32[]{:S(2)}) async-start(), calls=%async_computation.14 | async-start | bytes 4456448 | tf_op jit(solution)/shard_map/all_gather | solution.py:914
  479.0 1.5 collective-permute-start.42
  480.5 6.6 collective-permute-start.43
  487.1 29.8 %collective-permute-start.44 = (f32[40,1024]{1,0:T(8,128)S(1)}, f32[40,1024]{1,0:T(8,128)}, u32[]{:S(2)}, u32[]{:S(2)}) collective-permute-start(f32[40,1024]{1,0:T(8,128)S(1)} %add.190), channel_id=1, source_target_pairs={{0,4},{4,0},{1,5},{5,1},{2,6},{6,2},{3,7},{7,3},{8,12},{12,8},{9,1... | collective-permute-start | bytes 491528 | tf_op jit(solution)/shard_map/ppermute | solution.py:466
  512.5 53.8 %copy-start.20 = (f32[128,1024]{1,0:T(8,128)S(1)}, f32[128,1024]{1,0:T(8,128)}, u32[]{:S(2)}) copy-start(f32[128,1024]{1,0:T(8,128)} %copy-done.18) | copy-start | bytes 1572868
  512.5 64.9 %collective-permute-start.17 = (f32[2048,64]{0,1:T(8,128)}, f32[2048,64]{0,1:T(8,128)}, u32[]{:S(2)}, u32[]{:S(2)}) collective-permute-start(f32[2048,64]{0,1:T(8,128)} %copy.158), channel_id=1, source_target_pairs={{0,2},{2,0},{1,3},{3,1},{4,6},{6,4},{5,7},{7,5},{8,10},{10,8},{9,1... | collective-permute-start | bytes 1572872 | tf_op jit(solution)/shard_map/ppermute | solution.py:466
  514.4 51.9 %collective-permute-start.15 = (bf16[128,1024]{1,0:T(8,128)(2,1)S(1)}, bf16[128,1024]{1,0:T(8,128)(2,1)S(1)}, u32[]{:S(2)}, u32[]{:S(2)}) collective-permute-start(bf16[128,1024]{1,0:T(8,128)(2,1)S(1)} %fusion.21), channel_id=1, source_target_pairs={{0,16},{16,0},{1,17},{17,1},{2,18},{18,2},{3,19},{19,3},{4,20},{20... | collective-permute-start | bytes 786440 | tf_op jit(solution)/shard_map/ppermute | solution.py:466
  517.9 15.0 %collective-permute-start.45 = (f32[40,1024]{1,0:T(8,128)S(1)}, f32[40,1024]{1,0:T(8,128)S(1)}, u32[]{:S(2)}, u32[]{:S(2)}) collective-permute-start(f32[40,1024]{1,0:T(8,128)S(1)} %add.191), channel_id=1, source_target_pairs={{0,8},{8,0},{1,9},{9,1},{2,10},{10,2},{3,11},{11,3},{4,12},{12,4},... | collective-permute-start | bytes 491528 | tf_op jit(solution)/shard_map/ppermute | solution.py:466
  519.4 101.5 %collective-permute-start.18 = (bf16[512,2048]{1,0:T(8,128)(2,1)}, bf16[512,2048]{1,0:T(8,128)(2,1)}, u32[]{:S(2)}, u32[]{:S(2)}) collective-permute-start(bf16[512,2048]{1,0:T(8,128)(2,1)} %copy.176), channel_id=1, source_target_pairs={{0,1},{1,0},{2,3},{3,2},{4,5},{5,4},{6,7},{7,6},{8,9},{9,8},{10,11... | collective-permute-start | bytes 6291464 | tf_op jit(solution)/shard_map/ppermute | solution.py:466
  532.9 42.9 %collective-permute-start.46 = (f32[40,1024]{1,0:T(8,128)S(1)}, f32[40,1024]{1,0:T(8,128)}, u32[]{:S(2)}, u32[]{:S(2)}) collective-permute-start(f32[40,1024]{1,0:T(8,128)S(1)} %add.192), channel_id=1, source_target_pairs={{0,16},{16,0},{1,17},{17,1},{2,18},{18,2},{3,19},{19,3},{4,20},{20... | collective-permute-start | bytes 491528 | tf_op jit(solution)/shard_map/ppermute | solution.py:466
  584.2 8.7 %collective-permute-start.24 = (f32[512,128]{1,0:T(8,128)}, f32[512,128]{1,0:T(8,128)}, u32[]{:S(2)}, u32[]{:S(2)}) collective-permute-start(f32[512,128]{1,0:T(8,128)} %get-tuple-element.123), channel_id=1, source_target_pairs={{0,1},{1,0},{2,3},{3,2},{4,5},{5,4},{6,7},{7,6},{8,9},{9,8},{10,11... | collective-permute-start | bytes 786440 | tf_op jit(solution)/shard_map/ppermute | solution.py:466
  588.3 32.7 %copy-start.41 = (f32[1024]{0:T(1024)S(1)}, f32[1024]{0:T(1024)}, u32[]{:S(2)}) copy-start(f32[1024]{0:T(1024)} %copy-done.40) | copy-start | bytes 12292
  588.3 32.7 %copy-start.50 = (f32[128]{0:T(128)S(1)}, f32[128]{0:T(128)}, u32[]{:S(2)}) copy-start(f32[128]{0:T(128)} %copy-done.49) | copy-start | bytes 1540
  588.3 32.6 %all-to-all-start.11 = ((bf16[16,128,128]{1,2,0:T(8,128)(2,1)}), bf16[16,128,128]{1,2,0:T(8,128)(2,1)}, u32[]{:S(2)}, u32[]{:S(2)}) async-start(bf16[16,128,128]{1,2,0:T(8,128)(2,1)} %pad_maximum_fusion.10), calls=%async_computation.11 | async-start | bytes 1048576 | tf_op jit(solution)/shard_map/all_to_all | solution.py:786
  594.0 6.4 collective-permute-start.29
  597.2 17.0 %collective-permute-start.25 = (bf16[1,1,1,1,256,128]{5,4,3,2,1,0:T(8,128)(2,1)S(1)}, bf16[1,1,1,1,256,128]{5,4,3,2,1,0:T(8,128)(2,1)S(1)}, u32[]{:S(2)}, u32[]{:S(2)}) collective-permute-start(bf16[1,1,1,1,256,128]{5,4,3,2,1,0:T(8,128)(2,1)S(1)} %get-tuple-element.98), channel_id=1, source_target_pairs={{0,16},{16,0},{1,17},{17,1},{2,18},{18,2},{3,19},{19,3},{4,20},{20... | collective-permute-start | bytes 196616 | tf_op jit(solution)/shard_map/ppermute | solution.py:466
  600.4 16.1 %collective-permute-start.30 = (bf16[1,1,2,1,256,128]{5,4,3,2,1,0:T(8,128)(2,1)S(1)}, bf16[1,1,2,1,256,128]{5,4,3,2,1,0:T(8,128)(2,1)S(1)}, u32[]{:S(2)}, u32[]{:S(2)}) collective-permute-start(bf16[1,1,2,1,256,128]{5,4,3,2,1,0:T(8,128)(2,1)S(1)} %maximum_select_fusion.35), channel_id=1, source_target_pairs={{0,16},{16,0},{1,17},{17,1},{2,18},{18,2},{3,19},{19,3},{4,20},{20... | collective-permute-start | bytes 393224 | tf_op jit(solution)/shard_map/ppermute | solution.py:466
  614.2 5.1 collective-permute-start.26
  617.3 9.1 %collective-permute-start.31 = (bf16[2,1,2,1,256,128]{5,4,3,2,1,0:T(8,128)(2,1)}, bf16[2,1,2,1,256,128]{5,4,3,2,1,0:T(8,128)(2,1)}, u32[]{:S(2)}, u32[]{:S(2)}) collective-permute-start(bf16[2,1,2,1,256,128]{5,4,3,2,1,0:T(8,128)(2,1)} %fusion.43), channel_id=1, source_target_pairs={{0,8},{8,0},{1,9},{9,1},{2,10},{10,2},{3,11},{11,3},{4,12},{12,4},... | collective-permute-start | bytes 786440 | tf_op jit(solution)/shard_map/ppermute | solution.py:466
  619.3 11.2 %collective-permute-start.27 = (bf16[2,2,1,1,256,128]{5,4,3,2,1,0:T(8,128)(2,1)S(1)}, bf16[2,2,1,1,256,128]{5,4,3,2,1,0:T(8,128)(2,1)S(1)}, u32[]{:S(2)}, u32[]{:S(2)}) collective-permute-start(bf16[2,2,1,1,256,128]{5,4,3,2,1,0:T(8,128)(2,1)S(1)} %maximum_select_fusion.27), channel_id=1, source_target_pairs={{0,4},{4,0},{1,5},{5,1},{2,6},{6,2},{3,7},{7,3},{8,12},{12,8},{9,1... | collective-permute-start | bytes 786440 | tf_op jit(solution)/shard_map/ppermute | solution.py:466
  625.1 1.2 collective-permute-start.19
  626.4 3.6 collective-permute-start.20
  627.6 14.7 %collective-permute-start.32 = (bf16[2,2,2,1,256,128]{5,4,3,2,1,0:T(8,128)(2,1)S(1)}, bf16[2,2,2,1,256,128]{5,4,3,2,1,0:T(8,128)(2,1)S(1)}, u32[]{:S(2)}, u32[]{:S(2)}) collective-permute-start(bf16[2,2,2,1,256,128]{5,4,3,2,1,0:T(8,128)(2,1)S(1)} %maximum_select_fusion.17), channel_id=1, source_target_pairs={{0,2},{2,0},{1,3},{3,1},{4,6},{6,4},{5,7},{7,5},{8,10},{10,8},{9,1... | collective-permute-start | bytes 1572872 | tf_op jit(solution)/shard_map/ppermute | solution.py:466
  630.0 3.6 collective-permute-start.21
  630.6 15.0 %collective-permute-start.28 = (bf16[2,2,2,1,256,128]{5,4,3,2,1,0:T(8,128)(2,1)S(1)}, bf16[2,2,2,1,256,128]{5,4,3,2,1,0:T(8,128)(2,1)}, u32[]{:S(2)}, u32[]{:S(2)}) collective-permute-start(bf16[2,2,2,1,256,128]{5,4,3,2,1,0:T(8,128)(2,1)S(1)} %maximum_select_fusion.16), channel_id=1, source_target_pairs={{0,2},{2,0},{1,3},{3,1},{4,6},{6,4},{5,7},{7,5},{8,10},{10,8},{9,1... | collective-permute-start | bytes 1572872 | tf_op jit(solution)/shard_map/ppermute | solution.py:466
  633.6 3.6 collective-permute-start.22
  637.2 4.5 collective-permute-start.23
  645.5 6.5 collective-permute-start.33
  653.1 7.4 %collective-permute-start.34 = (bf16[1,1,1,1,64,512]{5,4,3,2,1,0:T(8,128)(2,1)S(1)}, bf16[1,1,1,1,64,512]{5,4,3,2,1,0:T(8,128)(2,1)S(1)}, u32[]{:S(2)}, u32[]{:S(2)}) collective-permute-start(bf16[1,1,1,1,64,512]{5,4,3,2,1,0:T(8,128)(2,1)S(1)} %get-tuple-element.90), channel_id=1, source_target_pairs={{0,16},{16,0},{1,17},{17,1},{2,18},{18,2},{3,19},{19,3},{4,20},{20... | collective-permute-start | bytes 196616 | tf_op jit(solution)/shard_map/ppermute | solution.py:466
  653.7 6.8 collective-permute-start.38
  660.4 7.8 %collective-permute-start.35 = (bf16[2,1,1,1,64,512]{5,4,3,2,1,0:T(8,128)(2,1)S(1)}, bf16[2,1,1,1,64,512]{5,4,3,2,1,0:T(8,128)(2,1)S(1)}, u32[]{:S(2)}, u32[]{:S(2)}) collective-permute-start(bf16[2,1,1,1,64,512]{5,4,3,2,1,0:T(8,128)(2,1)S(1)} %maximum_select_fusion.37), channel_id=1, source_target_pairs={{0,8},{8,0},{1,9},{9,1},{2,10},{10,2},{3,11},{11,3},{4,12},{12,4},... | collective-permute-start | bytes 393224 | tf_op jit(solution)/shard_map/ppermute | solution.py:466
  660.6 8.5 %collective-permute-start.39 = (bf16[1,1,2,1,64,512]{5,4,3,2,1,0:T(8,128)(2,1)S(1)}, bf16[1,1,2,1,64,512]{5,4,3,2,1,0:T(8,128)(2,1)S(1)}, u32[]{:S(2)}, u32[]{:S(2)}) collective-permute-start(bf16[1,1,2,1,64,512]{5,4,3,2,1,0:T(8,128)(2,1)S(1)} %maximum_select_fusion.39), channel_id=1, source_target_pairs={{0,16},{16,0},{1,17},{17,1},{2,18},{18,2},{3,19},{19,3},{4,20},{20... | collective-permute-start | bytes 393224 | tf_op jit(solution)/shard_map/ppermute | solution.py:466
  668.3 6.4 collective-permute-start.36
  669.1 6.4 collective-permute-start.40
  674.8 8.9 %collective-permute-start.37 = (bf16[2,2,2,1,64,512]{5,4,3,2,1,0:T(8,128)(2,1)S(1)}, bf16[2,2,2,1,64,512]{5,4,3,2,1,0:T(8,128)(2,1)S(1)}, u32[]{:S(2)}, u32[]{:S(2)}) collective-permute-start(bf16[2,2,2,1,64,512]{5,4,3,2,1,0:T(8,128)(2,1)S(1)} %maximum_select_fusion.18), channel_id=1, source_target_pairs={{0,2},{2,0},{1,3},{3,1},{4,6},{6,4},{5,7},{7,5},{8,10},{10,8},{9,1... | collective-permute-start | bytes 1572872 | tf_op jit(solution)/shard_map/ppermute | solution.py:466
  675.6 8.2 %collective-permute-start.41 = (bf16[2,2,2,1,64,512]{5,4,3,2,1,0:T(8,128)(2,1)S(1)}, bf16[2,2,2,1,64,512]{5,4,3,2,1,0:T(8,128)(2,1)S(1)}, u32[]{:S(2)}, u32[]{:S(2)}) collective-permute-start(bf16[2,2,2,1,64,512]{5,4,3,2,1,0:T(8,128)(2,1)S(1)} %maximum_select_fusion.19), channel_id=1, source_target_pairs={{0,2},{2,0},{1,3},{3,1},{4,6},{6,4},{5,7},{7,5},{8,10},{10,8},{9,1... | collective-permute-start | bytes 1572872 | tf_op jit(solution)/shard_map/ppermute | solution.py:466
  (54 other events, 512.4 us)
Sparse Core Ops, SparseCore 0:
  29.9 90.6 all-gather.5
  479.9 80.3 all-gather.3

commit v2 on v1

--- a/solution.py
+++ b/solution.py
@@ -477,15 +477,22 @@
     return in_order(value, swap(value, axis), axis, dim)
 
 
-def gather_ctx(parts, orders):
-    held = [part[(None,) * 4] for part in parts]
-    for step in range(4):
-        others = [swap(held[i], orders[i][step]) for i in range(len(held))]
-        held = [
-            in_order(held[i], others[i], orders[i][step], CTX.index(orders[i][step]))
-            for i in range(len(held))
-        ]
-    return [value.reshape((16,) + value.shape[4:]) for value in held]
+def spread(value):
+    return value[(None,) * 4]
+
+
+def gather_step(held, axis):
+    return in_order(held, swap(held, axis), axis, CTX.index(axis))
+
+
+def share_swap(value):
+    half = value.shape[0] // 2
+    part = swap(jnp.where(lax.axis_index("d") == 0, value[:half], value[half:]), "f")
+    return part
+
+
+def share_join(value, part):
+    return in_order(value, join(part, "d"), "f", 0)
 
 
 def sum_everywhere(value):
@@ -494,11 +501,28 @@
     return value
 
 
-def exact_parts(value):
+def together(*values):
+    return lax.optimization_barrier(values)
+
+
+def two_parts(value):
     high = lax.reduce_precision(value, 8, 7)
-    rest = value - high
-    middle = lax.reduce_precision(rest, 8, 7)
-    return [part.astype(jnp.bfloat16) for part in (high, middle, rest - middle)]
+    return [high.astype(jnp.bfloat16), (value - high).astype(jnp.bfloat16)]
+
+
+def angles(number, fine, coarse):
+    cos_b, sin_b = fine[0], fine[1]
+    cos_a = coarse[0, pl.ds(number, 1), :]
+    sin_a = coarse[1, pl.ds(number, 1), :]
+    return cos_a * cos_b - sin_a * sin_b, sin_a * cos_b + cos_a * sin_b
+
+
+def block_angles(chunk, pieces, fine, coarse):
+    pairs = [angles(chunk * pieces + n, fine, coarse) for n in range(pieces)]
+    return (
+        jnp.concatenate([one[0] for one in pairs], 0),
+        jnp.concatenate([one[1] for one in pairs], 0),
+    )
 
 
 def lane_of(shape):
@@ -506,19 +530,24 @@
 
 
 def attention_forward(
-    place, first_key, h_low, h_high, weight, cosine, sine, start,
-    query_out, key_out, value_out, mixed_out, attended_out, value_t,
+    place, h_place, first_key, low_own, high_own, low_next, high_next, weight, fine, coarse,
+    start, query_out, key_out, value_out, mixed_out, attended_out, value_t,
 ):
-    rows = h_low.shape[0]
+    rows = query_out.shape[0]
     block = QUERY_BLOCK
     pieces = block // 64
 
     def project(chunk, carry):
-        storage = [
-            pl.ds(pl.multiple_of(place[chunk * pieces + n] * 64, 64), 64) for n in range(pieces)
-        ]
-        low = jnp.concatenate([h_low[one, :] for one in storage], 0)
-        high = jnp.concatenate([h_high[one, :] for one in storage], 0)
+        def rows_of(own, following):
+            found = []
+            for n in range(pieces):
+                spot = h_place[chunk * pieces + n]
+                at = pl.ds(pl.multiple_of((spot % 16) * 64, 64), 64)
+                found.append(jnp.where(spot < 16, own[at, :], following[at, :]))
+            return jnp.concatenate(found, 0)
+
+        low = rows_of(low_own, low_next)
+        high = rows_of(high_own, high_next)
         here = pl.ds(pl.multiple_of(chunk * block, block), block)
         both = jnp.dot(low, weight[:512, :], preferred_element_type=jnp.float32) + jnp.dot(
             high, weight[512:, :], preferred_element_type=jnp.float32
@@ -529,7 +558,8 @@
         turned = jnp.where(
             lane % 64 < 32, -pltpu.roll(pair, 96, 1), pltpu.roll(pair, 32, 1)
         )
-        pair = pair * cosine[here, :] + turned * sine[here, :]
+        cosine, sine = block_angles(chunk, pieces, fine, coarse)
+        pair = pair * cosine + turned * sine
         pair = pair.astype(jnp.bfloat16).astype(jnp.float32)
         key_out[here, :] = jnp.where(lane >= 64, pair, 0.0).astype(jnp.bfloat16)
         query_out[here, :] = jnp.where(
@@ -590,8 +620,8 @@
 
 
 def attention_backward(
-    place, first_key, query, key, value, mixed, grad, cosine, sine, start,
-    pair_out, value_out, key_t, pair_sum, value_sum,
+    place, first_key, core, query, key, value, mixed, grad, fine, coarse, start,
+    keep_out, send_out, key_t, pair_sum, value_sum,
 ):
     rows = query.shape[0]
     block = QUERY_BLOCK
@@ -603,7 +633,7 @@
         turned = jnp.transpose(key[here, :].astype(jnp.float32))
         key_t[:, here] = turned[64:, :].astype(jnp.bfloat16)
         pair_sum[here, :] = jnp.zeros((block, 128), jnp.float32)
-        value_sum[here, :] = jnp.zeros((block, 64), jnp.float32)
+        value_sum[here, :] = jnp.zeros((block, 128), jnp.float32)
         return carry
 
     lax.fori_loop(0, rows // block, prepare, 0)
@@ -617,7 +647,9 @@
         here = pl.ds(pl.multiple_of(number * block, block), block)
         queries = query[here, :]
         incoming = jnp.concatenate([grad[one, :] for one in storage(number)], 0)
-        padded = jnp.concatenate([incoming, jnp.zeros((block, 64), jnp.bfloat16)], 1)
+        nothing = jnp.zeros((block, 64), jnp.bfloat16)
+        padded = jnp.concatenate([incoming, nothing], 1)
+        upper = jnp.concatenate([nothing, incoming], 1)
         incoming_t = jnp.transpose(padded.astype(jnp.float32))[:64, :]
         log_total = mixed[64:65, here]
         delta = jnp.sum(incoming_t * mixed[:64, here], axis=0, keepdims=True)
@@ -639,7 +671,7 @@
             )
             grad_scores = (probs * (grad_probs - delta)).astype(jnp.bfloat16)
             value_sum[there, :] += jnp.dot(
-                probs.astype(jnp.bfloat16), incoming, preferred_element_type=jnp.float32
+                probs.astype(jnp.bfloat16), upper, preferred_element_type=jnp.float32
             )
             pair_sum[there, :] += jnp.dot(
                 grad_scores, queries, preferred_element_type=jnp.float32
@@ -661,18 +693,116 @@
         here = pl.ds(pl.multiple_of(number * block, block), block)
         pair = pair_sum[here, :]
         lane = lane_of((block, 128))
-        across = pair * sine[here, :]
+        cosine, sine = block_angles(number, pieces, fine, coarse)
+        across = pair * sine
         turned = jnp.where(
             lane % 64 < 32, pltpu.roll(across, 96, 1), -pltpu.roll(across, 32, 1)
         )
-        pair = pair * cosine[here, :] + turned
+        pair = pair * cosine + turned
         values = value_sum[here, :]
+        keys_stay = core[0] == 0
+        keep = jnp.where((lane < 64) | keys_stay, pair, values)
+        send = jnp.where(lane < 64, 0.0, jnp.where(keys_stay, values, pair)).astype(jnp.bfloat16)
         for n, one in enumerate(storage(number)):
-            pair_out[one, :] = pair[n * 64 : (n + 1) * 64, :]
-            value_out[one, :] = values[n * 64 : (n + 1) * 64, :]
+            keep_out[one, :] = keep[n * 64 : (n + 1) * 64, :]
+            send_out[one, :] = send[n * 64 : (n + 1) * 64, :]
         return carry
 
     lax.fori_loop(0, rows // block, finish, 0)
+
+
+def expert_rows(
+    where, rows, grad, up_weight, down_weight,
+    copy_out, result_out, activation_out, pair_out, pre_out,
+):
+    f32, bf16 = jnp.float32, jnp.bfloat16
+    width = grad.shape[3]
+    count = rows.shape[0]
+    expert = where[0]
+    extra = rows[:, width:].astype(f32)
+    lane = lane_of((count, EXTRA))
+    gate = jnp.sum(
+        jnp.where((lane == expert) | (lane == expert + E), extra, 0.0), axis=1, keepdims=True
+    )
+    before = jnp.dot(rows[:, :width], up_weight[...], preferred_element_type=f32)
+    gate_pre = before[:, :F]
+    up_pre = before[:, F:]
+    sigma = jax.nn.sigmoid(gate_pre)
+    swish = gate_pre * sigma
+    activation = (swish * up_pre).astype(bf16)
+    activation_out[...] = activation
+    result = jnp.dot(activation, down_weight[...], preferred_element_type=f32).astype(bf16)
+    result = result.astype(f32)
+    grads = grad[...].reshape(count, width).astype(f32)
+    grad_gate = jnp.sum(grads * result, axis=1, keepdims=True)
+    result_out[...] = (gate * result).astype(bf16)
+    pair = (gate * grads).astype(bf16)
+    pair_out[...] = pair
+    grad_activation = lax.dot_general(
+        pair, down_weight[...], (((1,), (1,)), ((), ())), preferred_element_type=f32
+    )
+    pre_out[:, :F] = (
+        grad_activation * up_pre * sigma * (1.0 + gate_pre * (1.0 - sigma))
+    ).astype(bf16)
+    pre_out[:, F:] = (grad_activation * swish).astype(bf16)
+    copy_out[:, :width] = lax.dot_general(
+        pre_out[...], up_weight[...], (((1,), (1,)), ((), ())), preferred_element_type=f32
+    ).astype(bf16)
+    high = grad_gate.astype(bf16).astype(f32)
+    copy_out[:, width:] = jnp.where(
+        lane == expert, high, jnp.where(lane == expert + E, grad_gate - high, 0.0)
+    ).astype(bf16)
+
+
+def expert_call(half, where, rows, grads, up_weight, down_weight):
+    count, full = rows.shape
+    width = grads.shape[3]
+    steps = 2
+    block = count // steps
+    bf16 = jnp.bfloat16
+    row_spec = lambda columns: pl.BlockSpec((block, columns), lambda i, w: (i, 0))
+    whole = lambda a: pl.BlockSpec(a.shape, lambda i, w: (0, 0), pipeline_mode=pl.Buffered(1))
+    columns = (full, width, F, width, 2 * F)
+    return pl.pallas_call(
+        expert_rows,
+        out_shape=[jax.ShapeDtypeStruct((count, n), bf16) for n in columns],
+        grid_spec=pltpu.PrefetchScalarGridSpec(
+            num_scalar_prefetch=1,
+            grid=(steps,),
+            in_specs=[
+                row_spec(full),
+                pl.BlockSpec((16 // steps, 1, MOST, width), lambda i, w: (i, half, 0, 0)),
+                whole(up_weight),
+                whole(down_weight),
+            ],
+            out_specs=[row_spec(n) for n in columns],
+        ),
+        compiler_params=pltpu.CompilerParams(vmem_limit_bytes=48 << 20),
+    )(where, rows, grads, up_weight, down_weight)
+
+
+def assemble(first, second, qkv_out, out_out, gain_out):
+    f32 = jnp.float32
+    for pair in range(8):
+        for source, rows, at in ((first, 384, 0), (second, 128, 384)):
+            left = source[2 * pair, :rows, :].astype(f32)
+            right = source[2 * pair + 1, :rows, :].astype(f32)
+            here = slice(at, at + rows)
+            qkv_out[here, pair * 128 : (pair + 1) * 128] = jnp.concatenate(
+                [left[:, :64], right[:, :64]], 1
+            )
+            qkv_out[here, 1024 + pair * 64 : 1024 + (pair + 1) * 64] = left[:, 64:]
+            qkv_out[here, 1536 + pair * 64 : 1536 + (pair + 1) * 64] = right[:, 64:]
+    total = jnp.zeros((16, 128), f32)
+    for device in range(16):
+        bits = [(device >> n) & 1 for n in range(4)]
+        at = bits[0] * 256 + bits[1] * 128 + bits[2] * 64 + bits[3] * 32
+        for part in range(8):
+            out_out[at : at + 32, part * 128 : (part + 1) * 128] = second[
+                device, 128 + part * 32 : 160 + part * 32, :
+            ].astype(f32)
+        total = total + second[device, 384:400, :].astype(f32)
+    gain_out[...] = total[:8, :] + total[8:, :]
 
 
 def whole_call(kernel, scalars, outs, scratch, vmem):
@@ -708,51 +838,93 @@
     expert = jf * 16 + mine
     low_half = jf == 0
 
-    gain_one_f = join(attn_gain, "f").astype(f32)
     inputs = hidden_in[0].astype(f32)
-    grad_out = cotangent[0].astype(f32)
     scale_one = rms_scale(inputs)
     norm_one = inputs * scale_one
+    gain_one_f = join(attn_gain, "f").astype(f32)
     h_one = (norm_one * gain_one_f).astype(bf16)
-    h_low, h_high = gather_ctx(
-        [h_one[:, :512], h_one[:, 512:]], [("a", "b", "c", "d"), ("c", "a", "b", "d")]
-    )
-    h_low = h_low.reshape(length, 512)
-    h_high = h_high.reshape(length, 512)
-
-    split_rows = query_key_value_weight.shape[0]
-    q_part = query_key_value_weight[:, :1024].reshape(split_rows, 16, 64)
-    k_part = query_key_value_weight[:, 1024:1536].reshape(split_rows, 8, 1, 64)
-    v_part = query_key_value_weight[:, 1536:].reshape(split_rows, 8, 1, 64)
-    kv_part = jnp.concatenate([k_part, v_part], 2).reshape(split_rows, 16, 64)
-    by_head = jnp.concatenate([q_part, kv_part], 2).reshape(split_rows, 2048)
-    my_slice = lax.dynamic_slice_in_dim(by_head, (mine // 2) * 256, 256, 1)
-    my_weight = join(my_slice, "f")
-    head_weight = jnp.concatenate(
+
+    (
+        h_one, block_order, segment_ids, query_key_value_weight, w_out, ffn_gain, w_router,
+        routes, cotangent,
+    ) = together(
+        h_one, block_order, segment_ids, query_key_value_weight, w_out, ffn_gain, w_router,
+        routes, cotangent,
+    )
+    both = gather_step(spread(h_one), "a")
+
+    def columns_of(start, number, low_first):
+        pair = lax.dynamic_slice_in_dim(query_key_value_weight, start + number * 128, 128, 1)
+        return jnp.where(low_first, pair[:, :64], pair[:, 64:])
+
+    my_columns = jnp.concatenate(
         [
-            jnp.where(idd == 0, my_weight[:, :64], my_weight[:, 128:192]),
-            my_weight[:, 64:128],
-            my_weight[:, 192:],
-            jnp.zeros((width, 64), bf16),
+            columns_of(0, mine // 2, idd == 0),
+            columns_of(1024, mine // 4, ic == 0),
+            columns_of(1536, mine // 4, ic == 0),
+            jnp.zeros((512, 64), bf16),
         ],
         1,
     )
-    out_full = join(w_out, "f")
-    gain_two_f = join(ffn_gain, "f").astype(f32)
-    router_full = join(w_router, "f")
-    by_head_full = join(by_head, "f")
-
-    up_weight = lax.all_to_all(expert_in, CTX, split_axis=0, concat_axis=0, tiled=True).reshape(
-        width, 2 * F
-    )
-    down_weight = lax.all_to_all(
-        expert_out, CTX, split_axis=0, concat_axis=0, tiled=True
-    ).reshape(F, width)
+    other_columns = swap(my_columns, "f")
+
+    route = routes[0]
+    named = jnp.any(route[:, :, None] == jnp.arange(E, dtype=jnp.int32)[None, None, :], axis=1)
+    counts = spread(jnp.sum(named.astype(f32), axis=0, keepdims=True))
+    named_b = named.astype(bf16)
+    earlier = (jnp.arange(rows)[:, None] > jnp.arange(rows)[None, :]).astype(bf16)
+    rank = jnp.dot(earlier, named_b, preferred_element_type=f32)
+    row_of = jnp.where(named, rank, -1.0)
+    counts = gather_step(counts, "a")
+    expert_weights = jnp.concatenate([expert_in, expert_out], 1)
+    both, row_of, cotangent, counts, expert_weights = together(
+        both, row_of, cotangent, counts, expert_weights
+    )
+    low = gather_step(both[..., :512], "b")
+    high = gather_step(both[..., 512:], "c")
+    other_row_of = swap(row_of, "a")
+    other_cotangent = swap(cotangent[0], "a")
+    counts = gather_step(counts, "c")
+
+    def picks(rows_of):
+        half = rows_of.reshape(rows, 2, 2, 8)
+        half = jnp.where(ia == 0, half[:, :, 0], half[:, :, 1])
+        half = half.transpose(2, 1, 0).reshape(16, 1, rows)
+        return (half == jnp.arange(MOST, dtype=f32)[None, :, None]).astype(bf16)
+
+    def build_rows(choice, tokens):
+        return lax.dot_general(
+            choice, tokens, (((2,), (0,)), ((), ())), preferred_element_type=f32
+        ).astype(bf16)
+
+    def exchange(sent):
+        return lax.all_to_all(sent, HALF, split_axis=0, concat_axis=0, tiled=True)
+
+    low, high, other_columns, counts = together(low, high, other_columns, counts)
+    low = gather_step(low, "c")
+    high = gather_step(high, "b")
+    counts = gather_step(counts, "b")
+    out_part = share_swap(w_out)
+    other_gain_two = swap(ffn_gain, "f")
+    other_router = swap(w_router, "f")
+    low, high, other_cotangent, other_row_of, counts, expert_weights, out_part = together(
+        low, high, other_cotangent, other_row_of, counts, expert_weights, out_part
+    )
+    low_own = low.reshape(length // 2, 512)
+    high_own = high.reshape(length // 2, 512)
+    low_next = swap(low_own, "d")
+    high_next = swap(high_own, "d")
+    expert_weights = lax.all_to_all(
+        expert_weights, CTX, split_axis=0, concat_axis=0, tiled=True
+    )
+    counts = gather_step(counts, "d")
+    head_weight = in_order(my_columns, other_columns, "f", 0)
 
     order = block_order[0]
+    blocks = order.shape[0]
     place = jnp.sum(
-        jnp.where(order[None, :] == jnp.arange(32, dtype=jnp.int32)[:, None],
-                  jnp.arange(32, dtype=jnp.int32)[None, :], 0),
+        jnp.where(order[None, :] == jnp.arange(blocks, dtype=jnp.int32)[:, None],
+                  jnp.arange(blocks, dtype=jnp.int32)[None, :], 0),
         axis=1,
     )
     document = segment_ids[0]
@@ -761,16 +933,23 @@
     start = start[None, :]
     steps = jnp.arange(HEAD_SIZE // 2, dtype=f32)
     frequency = jnp.power(THETA, -2.0 * steps / HEAD_SIZE)
-    coarse = (jnp.arange(length // 64, dtype=f32) * 64.0)[:, None] * frequency[None, :]
-    fine = jnp.arange(64, dtype=f32)[:, None] * frequency[None, :]
-    cos_a, sin_a = (jnp.cos(coarse)[:, None, :], jnp.sin(coarse)[:, None, :])
-    cos_b, sin_b = (jnp.cos(fine)[None], jnp.sin(fine)[None])
-    cosine = jnp.tile((cos_a * cos_b - sin_a * sin_b).reshape(length, 32), (1, 4))
-    sine = jnp.tile((sin_a * cos_b + cos_a * sin_b).reshape(length, 32), (1, 4))
-
+    angle_a = (jnp.arange(length // 64, dtype=f32) * 64.0)[:, None] * frequency[None, :]
+    angle_b = jnp.arange(64, dtype=f32)[:, None] * frequency[None, :]
+    coarse = jnp.tile(jnp.stack([jnp.cos(angle_a), jnp.sin(angle_a)]), (1, 1, 4))
+    fine = jnp.tile(jnp.stack([jnp.cos(angle_b), jnp.sin(angle_b)]), (1, 1, 4))
+    storage = jnp.arange(blocks, dtype=jnp.int32)
+    held = (((storage // 2) % 2) ^ idd) * (blocks // 2) + (storage // 4) * 2 + storage % 2
+    h_place = jnp.sum(jnp.where(place[:, None] == storage[None, :], held[None, :], 0), axis=1)
+    storage = jnp.arange(blocks, dtype=jnp.int32)
+    held = (((storage // 2) % 2) ^ idd) * (blocks // 2) + (storage // 4) * 2 + storage % 2
+    h_place = jnp.sum(jnp.where(place[:, None] == storage[None, :], held[None, :], 0), axis=1)
+    head_weight, out_part, other_gain_two, other_router, query_key_value_weight = together(
+        head_weight, out_part, other_gain_two, other_router, query_key_value_weight
+    )
+    weight_part = share_swap(query_key_value_weight)
     query, key, value, mixed, attended_head = whole_call(
         attention_forward,
-        2,
+        3,
         [
             jax.ShapeDtypeStruct((length, 128), bf16),
             jax.ShapeDtypeStruct((length, 128), bf16),
@@ -780,207 +959,225 @@
         ],
         [pltpu.VMEM((128, length), bf16)],
         32 << 20,
-    )(place, first_key, h_low, h_high, head_weight, cosine, sine, start)
+    )(
+        place, h_place, first_key, low_own, high_own, low_next, high_next, head_weight, fine,
+        coarse, start,
+    )
 
     def to_tokens(value_heads):
-        got = lax.all_to_all(
+        return lax.all_to_all(
             value_heads.reshape(16, rows, -1), CTX, split_axis=0, concat_axis=0, tiled=True
         )
-        return got
-
-    attended = to_tokens(attended_head).transpose(1, 0, 2).reshape(rows, 1024)
+
+    pick_mine = picks(row_of)
+    pick_other = picks(other_row_of)
+    grad_rows = jnp.concatenate(
+        [build_rows(pick_mine, cotangent[0]), build_rows(pick_other, other_cotangent)], 1
+    )
+    out_full = share_join(w_out, out_part)
+    gain_two_f = in_order(ffn_gain, other_gain_two, "f", 0).astype(f32)
+    router_full = in_order(w_router, other_router, "f", 0)
+    attended_head, expert_weights, grad_rows, out_full, weight_part, counts = together(
+        attended_head, expert_weights, grad_rows, out_full, weight_part, counts
+    )
+    attended = to_tokens(attended_head)
+    weight_full = share_join(query_key_value_weight, weight_part)
+    attended, grad_rows = together(attended, grad_rows)
+    grad_rows = exchange(grad_rows)
+    attended = attended.transpose(1, 0, 2).reshape(rows, 1024)
     middle_state = inputs + jnp.dot(attended, out_full, preferred_element_type=f32)
     scale_two = rms_scale(middle_state)
     norm_two = middle_state * scale_two
     h_two = (norm_two * gain_two_f).astype(bf16)
     logits = jnp.dot(h_two, router_full, preferred_element_type=f32)
-    route = routes[0]
-    named = jnp.any(route[:, :, None] == jnp.arange(E, dtype=jnp.int32)[None, None, :], axis=1)
     top = jnp.max(jnp.where(named, logits, MASK_FILL_VALUE), axis=-1, keepdims=True)
     weights = jnp.where(named, jnp.exp(logits - top), 0.0)
     gates = weights / jnp.sum(weights, axis=-1, keepdims=True)
-
-    named_b = named.astype(bf16)
-    earlier = (
-        jnp.arange(rows)[:, None] > jnp.arange(rows)[None, :]
-    ).astype(bf16)
-    rank = jnp.dot(earlier, named_b, preferred_element_type=f32)
-    row_of = jnp.where(named, rank, -1.0)
-    row_pair = jnp.stack([row_of, swap(row_of, "a")])
-    half = row_pair.reshape(2, rows, 2, 2, 8)
-    half = jnp.where(ia == 0, half[:, :, :, 0], half[:, :, :, 1])
-    half = half.transpose(0, 3, 2, 1).reshape(2, 16, 1, rows)
-    pick = (half == jnp.arange(MOST, dtype=f32)[None, None, :, None]).astype(bf16)
-
-    def send_rows(choice, tokens):
-        built = lax.dot_general(
-            choice, tokens, (((2,), (0,)), ((), ())), preferred_element_type=f32
-        ).astype(bf16)
-        return lax.all_to_all(built, HALF, split_axis=0, concat_axis=0, tiled=True)
-
-    def take_rows(choice, sent):
-        got = lax.all_to_all(sent, HALF, split_axis=0, concat_axis=0, tiled=True)
+    passed = (jnp.arange(16)[:, None] < mine).astype(f32)
+    offset = jnp.sum(counts.reshape(16, E) * passed, axis=0, keepdims=True)
+    kept = (named & (rank + offset < capacity)).astype(f32)
+    extended = jnp.concatenate(
+        [h_two] + two_parts(gates * kept) + [jnp.zeros((rows, 2 * E), bf16)], 1
+    )
+    other_extended = swap(extended, "a")
+    rows_mine = build_rows(pick_mine, extended)
+    rows_mine, grad_rows, weight_full, other_extended = together(
+        rows_mine, grad_rows, weight_full, other_extended
+    )
+    rows_mine = exchange(rows_mine)
+    up_weight = expert_weights[:, :64].reshape(width, 2 * F)
+    down_weight = expert_weights[:, 64:].reshape(F, width)
+    grad_rows = grad_rows.reshape(16, 2, MOST, width)
+    rows_other = build_rows(pick_other, other_extended)
+    rows_mine, rows_other, up_weight, down_weight = together(
+        rows_mine, rows_other, up_weight, down_weight
+    )
+    rows_other = exchange(rows_other)
+    rows_mine = rows_mine.reshape(16 * MOST, width + EXTRA)
+    number = expert.astype(jnp.int32)[None]
+    copy_mine, result_mine, act_mine, pair_mine, pre_mine = expert_call(
+        0, number, rows_mine, grad_rows, up_weight, down_weight
+    )
+    rows_other, copy_mine = together(rows_other, copy_mine)
+    rows_other = rows_other.reshape(16 * MOST, width + EXTRA)
+    copy_other, result_other, act_other, pair_other, pre_other = expert_call(
+        1, number, rows_other, grad_rows, up_weight, down_weight
+    )
+
+    def sum_rows(choice, got):
         return lax.dot_general(
             choice, got, (((0, 1), (0, 1)), ((), ())), preferred_element_type=f32
         )
 
-    extended = jnp.concatenate(
-        [h_two] + exact_parts(gates) + [jnp.zeros((rows, EXTRA - 3 * E), bf16)], 1
-    )
-    other_extended = swap(extended, "a")
-    rows_mine = send_rows(pick[0], extended)
-    rows_other = send_rows(pick[1], other_extended)
-    received = in_order(rows_mine[None], rows_other[None], "a", 0).reshape(
-        32 * MOST, width + EXTRA
-    )
-
-    columns = row_of.T.reshape(2, 16, rows).transpose(1, 0, 2).reshape(32, rows)
-    their_row = lax.all_to_all(columns, EVERY, split_axis=0, concat_axis=0, tiled=True)
-    their_count = jnp.sum((their_row >= 0).astype(f32), axis=1).reshape(16, 2)
-    before_me = (jnp.arange(16)[:, None] > jnp.arange(16)[None, :]).astype(f32)
-    offset = jnp.dot(before_me, their_count, precision=HIGHEST).reshape(32, 1)
-    their_count = their_count.reshape(32, 1)
-    row_number = jnp.arange(MOST, dtype=f32)[None, :]
-    kept = (row_number < their_count) & (row_number + offset < capacity)
-    kept = kept.astype(f32).reshape(32 * MOST, 1)
-    their_pick = (their_row[:, None, :] == row_number[:, :, None]).astype(bf16)
-    all_cotangent = lax.all_gather(cotangent[0], EVERY, axis=0, tiled=True).reshape(
-        32, rows, width
-    )
-    grad_rows = jnp.einsum(
-        "srt,stc->src", their_pick, all_cotangent, preferred_element_type=f32
-    ).astype(bf16).reshape(32 * MOST, width)
-
-    x_rows = received[:, :width]
-    lane = jnp.arange(EXTRA, dtype=jnp.int32)[None, :]
-    my_lane = ((lane % E) == expert) & (lane < 3 * E)
-    gate_rows = jnp.sum(
-        jnp.where(my_lane, received[:, width:].astype(f32), 0.0), axis=1, keepdims=True
-    )
-    before = jnp.dot(x_rows, up_weight, preferred_element_type=f32)
-    gate_pre = before[:, :F]
-    up_pre = before[:, F:]
-    sigma = jax.nn.sigmoid(gate_pre)
-    activation = (gate_pre * sigma * up_pre).astype(bf16)
-    result = jnp.dot(activation, down_weight, preferred_element_type=f32).astype(bf16)
-    result_f = result.astype(f32) * kept
-    grad_pair = (gate_rows * grad_rows.astype(f32) * kept).astype(bf16)
-    grad_gate_rows = jnp.sum(grad_rows.astype(f32) * result_f, axis=1, keepdims=True)
-    grad_activation = contract_columns(grad_pair, down_weight)
-    grad_down = contract_rows(activation, grad_pair)
-    grad_gate = grad_activation * up_pre * sigma * (1.0 + gate_pre * (1.0 - sigma))
-    grad_up = grad_activation * gate_pre * sigma
-    grad_pre = jnp.concatenate([grad_gate, grad_up], axis=-1).astype(bf16)
-    grad_copy = contract_columns(grad_pre, up_weight).astype(bf16)
-    grad_up_weight = contract_rows(x_rows, grad_pre)
-    gate_parts = exact_parts(grad_gate_rows)
-    extra = jnp.zeros((32 * MOST, EXTRA), bf16)
-    for number, part in enumerate(gate_parts):
-        extra = jnp.where(lane == expert + number * E, part, extra)
-    grad_copy = jnp.concatenate([grad_copy, extra], 1).reshape(2, 16, MOST, width + EXTRA)
-    gated_result = (gate_rows * result_f).astype(bf16).reshape(2, 16, MOST, width)
-
-    def give_back(by_half):
-        here = jnp.where(ia == 0, by_half[0], by_half[1])
-        there = jnp.where(ia == 0, by_half[1], by_half[0])
-        away = take_rows(pick[1], there).astype(bf16)
-        home = take_rows(pick[0], here)
-        return home + swap(away, "a").astype(f32)
-
-    back = give_back(grad_copy)
-    mixture = give_back(gated_result)
-    hidden_out = (middle_state + mixture).astype(bf16)
-    gate_grads = sum(
-        back[:, width + n * E : width + (n + 1) * E] for n in range(3)
-    )
+    away = exchange(copy_other.reshape(16, MOST, width + EXTRA))
+    away, copy_mine = together(away, copy_mine)
+    home = exchange(copy_mine.reshape(16, MOST, width + EXTRA))
+    grad_up_weight = contract_rows(rows_mine[:, :width], pre_mine) + contract_rows(
+        rows_other[:, :width], pre_other
+    )
+    grad_down = contract_rows(act_mine, pair_mine) + contract_rows(act_other, pair_other)
+    expert_grads = jnp.concatenate(
+        [
+            grad_up_weight.astype(bf16).reshape(16, 64, 2 * F),
+            grad_down.astype(bf16).reshape(16, 32, width),
+        ],
+        1,
+    )
+    away_sum = swap(sum_rows(pick_other, away).astype(bf16), "a")
+    home, away_sum, expert_grads = together(home, away_sum, expert_grads)
+    back = sum_rows(pick_mine, home) + away_sum.astype(f32)
+
+    gate_grads = (back[:, width : width + E] + back[:, width + E : width + 2 * E]) * kept
     grad_logits = gates * (gate_grads - jnp.sum(gates * gate_grads, axis=-1, keepdims=True))
     grad_h_two = back[:, :width] + lax.dot_general(
         grad_logits, router_full.astype(f32), (((1,), (1,)), ((), ())), precision=HIGHEST
     )
-    grad_router_part = lax.dot_general(
-        grad_logits, h_two.astype(f32), (((0,), (0,)), ((), ())), precision=HIGHEST
-    )
-    grad_gain_two = jnp.sum(grad_h_two * norm_two, axis=0, keepdims=True)
+    grad_out = cotangent[0].astype(f32)
     scaled_two = grad_h_two * gain_two_f
     grad_mid = grad_out + scale_two * (
         scaled_two - norm_two * jnp.mean(scaled_two * norm_two, axis=-1, keepdims=True)
     )
     grad_branch = grad_mid.astype(bf16)
     attended_gradient = contract_columns(grad_branch, out_full).astype(bf16)
-    grad_heads = to_tokens(
-        attended_gradient.reshape(rows, 16, 64).transpose(1, 0, 2)
-    ).reshape(length, 64)
-
-    all_branch = lax.all_gather(grad_branch, CTX, axis=0, tiled=True)
-    out_part = contract_rows(attended_head, all_branch)
-    out_part = (out_part + swap(out_part, "f")).astype(bf16)
-    out_all = gather_ctx(
-        [out_part[:, :512], out_part[:, 512:]], [("a", "b", "c", "d"), ("c", "a", "b", "d")]
-    )
-    out_all = jnp.concatenate(out_all, 2).reshape(2, 512, width)
-    share_out = jnp.where(low_half, out_all[0], out_all[1]).astype(f32)
-
-    small = sum_everywhere(
-        jnp.concatenate([grad_router_part, jnp.broadcast_to(grad_gain_two, (8, width))], 0)
+    grad_heads = to_tokens(attended_gradient.reshape(rows, 16, 64).transpose(1, 0, 2))
+    grad_heads = grad_heads.reshape(length, 64)
+
+    by_core = attended.reshape(rows, 2, 2, 256)
+    keep = lax.dynamic_slice_in_dim(by_core, idd, 1, 2).reshape(rows, 512)
+    send = lax.dynamic_slice_in_dim(by_core, 1 - idd, 1, 2).reshape(rows, 512)
+    out_sum = contract_rows(keep, grad_branch) + swap(
+        contract_rows(send, grad_branch).astype(bf16), "d"
+    ).astype(f32)
+
+    def halve(total, axis):
+        count = total.shape[0] // 2
+        index = lax.axis_index(axis)
+        keep = lax.dynamic_slice_in_dim(total, index * count, count, 0)
+        send = lax.dynamic_slice_in_dim(total, (1 - index) * count, count, 0)
+        return keep + swap(send.astype(bf16), axis).astype(f32)
+
+    grad_router_part = lax.dot_general(
+        grad_logits, h_two.astype(f32), (((0,), (0,)), ((), ())), precision=HIGHEST
+    )
+    grad_gain_two = jnp.sum(grad_h_two * norm_two, axis=0, keepdims=True)
+    small = jnp.concatenate([grad_router_part, jnp.broadcast_to(grad_gain_two, (8, width))], 0)
+    grad_heads, expert_grads = together(grad_heads, expert_grads)
+    expert_grads = lax.all_to_all(expert_grads, CTX, split_axis=0, concat_axis=0, tiled=True)
+
+    keep, send = whole_call(
+        attention_backward,
+        3,
+        [jax.ShapeDtypeStruct((length, 128), f32), jax.ShapeDtypeStruct((length, 128), bf16)],
+        [
+            pltpu.VMEM((64, length), bf16),
+            pltpu.VMEM((length, 128), f32),
+            pltpu.VMEM((length, 128), f32),
+        ],
+        32 << 20,
+    )(
+        place, first_key, idd.astype(jnp.int32)[None], query, key, value, mixed, grad_heads,
+        fine, coarse, start,
+    )
+    keep, send, out_sum, small = together(keep, send, out_sum, small)
+    grad_columns = (keep + swap(send, "d").astype(f32)).astype(bf16)
+    out_sum = halve(out_sum, "f")
+    small = small + swap(small, "d")
+    small = small + swap(small, "f")
+    ready, expert_grads, out_sum = together(grad_columns, expert_grads, out_sum)
+    grad_projected = to_tokens(ready)
+    for axis in ("c", "b", "a"):
+        out_sum = halve(out_sum, axis)
+    out_rows = out_sum.reshape(32, 8, 128).transpose(1, 0, 2).reshape(256, 128).astype(bf16)
+
+    by_core = grad_columns.reshape(8, 2, rows, 128)
+    own = jnp.where(idd == 0, by_core[:, 0], by_core[:, 1]).reshape(length // 2, 128)
+    following = jnp.where(idd == 0, by_core[:, 1], by_core[:, 0]).reshape(length // 2, 128)
+    low_part = contract_rows(low_own, own) + contract_rows(low_next, following)
+    high_part = contract_rows(high_own, own) + contract_rows(high_next, following)
+    columns_grad = jnp.where(low_half, low_part, high_part) + swap(
+        jnp.where(low_half, high_part, low_part), "f"
+    )
+    my_weight = jnp.concatenate(
+        [my_columns[:, :64], jnp.where(idd == 0, my_columns[:, 64:128], my_columns[:, 128:192])], 1
+    )
+    gain_part = jnp.sum(columns_grad * my_weight.astype(f32), axis=1).reshape(4, 128)
+    gain_part = jnp.concatenate([gain_part, jnp.zeros((4, 128), f32)], 0)
+    columns_grad = jnp.concatenate(
+        [columns_grad.astype(bf16), out_rows] + two_parts(gain_part), 0
+    )
+    gathered = gather_step(spread(columns_grad), "a")
+    first = gather_step(gathered[..., :384, :], "b")
+    second = gather_step(gathered[..., 384:, :], "c")
+    first = gather_step(first, "c")
+    second = gather_step(second, "b")
+    results = jnp.concatenate(
+        [result_mine.reshape(16, MOST, width), result_other.reshape(16, MOST, width)], 1
+    )
+    grad_expert_in = expert_grads[:, :64].astype(f32)
+    grad_expert_out = expert_grads[:, 64:].astype(f32)
+    grad_projected, results, small, grad_expert_in, grad_expert_out, first, second = together(
+        grad_projected, results, small, grad_expert_in, grad_expert_out, first, second
+    )
+    results = exchange(results)
+    first = gather_step(first, "d")
+    second = gather_step(second, "d")
+    for axis in ("c", "b", "a"):
+        small = small + swap(small, axis)
+
+    grad_projected = grad_projected.transpose(1, 0, 2)
+    grad_kv = grad_projected[:, :, 64:].reshape(rows, 8, 2, 64)
+    grad_projected = jnp.concatenate(
+        [
+            grad_projected[:, :, :64].reshape(rows, 1024),
+            grad_kv[:, :, 0].reshape(rows, 512),
+            grad_kv[:, :, 1].reshape(rows, 512),
+        ],
+        1,
+    )
+    grad_h_one = contract_columns(grad_projected, weight_full)
+    scaled_one = grad_h_one * gain_one_f
+    grad_inputs = grad_mid + scale_one * (
+        scaled_one - norm_one * jnp.mean(scaled_one * norm_one, axis=-1, keepdims=True)
     )
     small = jnp.where(low_half, small[:, :512], small[:, 512:])
     share_router = small[:E].T
     share_two = small[E]
-
-    pair_grad, value_grad = whole_call(
-        attention_backward,
-        2,
-        [jax.ShapeDtypeStruct((length, 128), f32), jax.ShapeDtypeStruct((length, 64), f32)],
+    share_qkv, share_out, gain_sum = whole_call(
+        assemble,
+        0,
         [
-            pltpu.VMEM((64, length), bf16),
-            pltpu.VMEM((length, 128), f32),
-            pltpu.VMEM((length, 64), f32),
+            jax.ShapeDtypeStruct((512, 2048), f32),
+            jax.ShapeDtypeStruct((512, 1024), f32),
+            jax.ShapeDtypeStruct((8, 128), f32),
         ],
+        [],
         32 << 20,
-    )(place, first_key, query, key, value, mixed, grad_heads, cosine, sine, start)
-    key_grad = pair_grad[:, 64:]
-    sent = jnp.where(idd == 0, value_grad, key_grad)
-    stays = jnp.where(idd == 0, key_grad, value_grad)
-    grad_columns = jnp.concatenate([pair_grad[:, :64], stays + swap(sent, "d")], 1).astype(bf16)
-
-    low_part = contract_rows(h_low, grad_columns)
-    high_part = contract_rows(h_high, grad_columns)
-    columns_grad = jnp.where(low_half, low_part, high_part) + swap(
-        jnp.where(low_half, high_part, low_part), "f"
-    )
-    columns_grad = columns_grad.astype(bf16)
-    qkv_all = gather_ctx(
-        [columns_grad[:256], columns_grad[256:]], [("a", "b", "c", "d"), ("c", "a", "b", "d")]
-    )
-    qkv_all = jnp.concatenate(qkv_all, 1).transpose(1, 0, 2).astype(f32)
-    kv_all = qkv_all[:, :, 64:].reshape(512, 8, 2, 64)
-    share_qkv = jnp.concatenate(
-        [
-            qkv_all[:, :, :64].reshape(512, 1024),
-            kv_all[:, :, 0].reshape(512, 512),
-            kv_all[:, :, 1].reshape(512, 512),
-        ],
-        1,
-    )
-
-    grad_projected = to_tokens(grad_columns)
-    grad_projected = grad_projected.transpose(1, 0, 2).reshape(rows, 2048)
-    grad_h_one = contract_columns(grad_projected, by_head_full)
-    grad_gain_one = sum_everywhere(jnp.sum(grad_h_one * norm_one, axis=0))
-    share_one = jnp.where(low_half, grad_gain_one[:512], grad_gain_one[512:])
-    scaled_one = grad_h_one * gain_one_f
-    grad_inputs = grad_mid + scale_one * (
-        scaled_one - norm_one * jnp.mean(scaled_one * norm_one, axis=-1, keepdims=True)
-    )
-
-    grad_expert_in = lax.all_to_all(
-        grad_up_weight.astype(bf16).reshape(16, 64, 2 * F), CTX,
-        split_axis=0, concat_axis=0, tiled=True,
+    )(first.reshape(16, 384, 128), second.reshape(16, 400, 128))
+    share_one = gain_sum[:4].reshape(512) / attn_gain.astype(f32)
+    mixture = sum_rows(pick_mine, results[:, :MOST]) + swap(
+        sum_rows(pick_other, results[:, MOST:]).astype(bf16), "a"
     ).astype(f32)
-    grad_expert_out = lax.all_to_all(
-        grad_down.astype(bf16).reshape(16, 32, width), CTX,
-        split_axis=0, concat_axis=0, tiled=True,
-    ).astype(f32)
+    hidden_out = (middle_state + mixture).astype(bf16)
     return (
         hidden_out[None],
         grad_inputs[None],

time: 704 us -> 587 us (0.83)
  waiting for transfers between devices: 294 us -> 236 us
  matrix products: 79.2 us -> 41.1 us
  local copies, waits for them, and re-layouts: 59.1 us -> 31.9 us
  starting transfers between devices: 119 us -> 95.4 us
  Pallas kernels: 27 us -> 50.2 us
  blocking collectives: 45.3 us -> 68.5 us
  between operations: 15.9 us -> 2.66 us
    ppermute x47 -> x43, waiting for transfers between devices: 219 us -> 162 us  [swap(): return lax.ppermute(value, axis, [(0, 1), (1, 0)])]
    all_to_all x1 -> x2, blocking collectives: 17.1 us -> 40.4 us  [to_tokens(): lax.all_to_all(value_heads.reshape(16, rows, -1), CTX, split_axis=0, conc...]
    dot_general x10 -> x8, matrix products: 34.9 us -> 13.4 us  [the longest x4 7.34 us: sum_rows(): lax.dot_general(choice, got, (((0, 1), (0, 1)), ((), ())), preferred_elem...]
    all_to_all x10 -> x7, starting transfers between devices: 53.6 us -> 34.2 us  [the longest x5 24.9 us: exchange(): return lax.all_to_all(sent, HALF, split_axis=0, concat_axis=0, tiled=True)]
    pallas_call x0 -> x2, Pallas kernels: none -> 18.3 us  [expert_call(): pl.pallas_call(expert_rows, out_shape=[jax.ShapeDtypeStruct((count, n), b...]
    dot_general x4 -> x2, matrix products: 22.7 us -> 4.34 us  [contract_columns(): lax.dot_general(left, right, (((1,), (1,)), ((), ())), preferred_element_...]
    select_n x5 -> x0, local copies, waits for them, and re-layouts: 10.7 us -> none  [the longest x1 3.87 us: give_back(): there = jnp.where(ia == 0, by_half[1], by_half[0])]
    convert_element_type x12 -> x10, other arithmetic: 14.8 us -> 8.98 us  [the longest x1 4.08 us: fast_shards(): grad_expert_in = expert_grads[:, :64].astype(f32)]
  transfers between devices with their start and end apart: 61 -> 51, of which waited for: 34 -> 27; matrix products, arithmetic and copies ran while one was open for 22% -> 17% of each run, Pallas kernels for 4% -> 7%
where the time goes in v2:
time: 587 us; the launch traced here: 577 us
  waiting for transfers between devices  236 us (40%)
  starting transfers between devices  95.4 us (16%)
  blocking collectives  68.5 us (12%)
  other arithmetic  51.1 us (9%)
  Pallas kernels  50.2 us (9%)
  matrix products  41.1 us (7%)
  local copies, waits for them, and re-layouts  31.9 us (5%)
    ppermute x43, waiting for transfers between devices, swap(): return lax.ppermute(value, axis, [(0, 1), (1, 0)])  162 us
    ppermute x43, starting transfers between devices, swap(): return lax.ppermute(value, axis, [(0, 1), (1, 0)])  57.1 us
    all_to_all x2, blocking collectives, to_tokens(): lax.all_to_all(value_heads.reshape(16, rows, -1), CTX, split_axis=0, conc...  40.4 us
    pallas_call x3, Pallas kernels, run(): pl.pallas_call(kernel, out_shape=outs, grid_spec=pltpu.PrefetchScalarGrid...  31.8 us
    all_to_all x5, waiting for transfers between devices, exchange(): return lax.all_to_all(sent, HALF, split_axis=0, concat_axis=0, tiled=True)  31.2 us
    all_to_all x1, blocking collectives, exchange(): return lax.all_to_all(sent, HALF, split_axis=0, concat_axis=0, tiled=True)  28 us
    all_to_all x5, starting transfers between devices, exchange(): return lax.all_to_all(sent, HALF, split_axis=0, concat_axis=0, tiled=True)  24.9 us
    all_to_all x1, waiting for transfers between devices, fast_shards(): lax.all_to_all(expert_weights, CTX, split_axis=0, concat_axis=0, tiled=True)  22.3 us
  transfers between devices with their start and end apart: 51, of which 27 were waited for; matrix products, arithmetic and copies ran while one was open for 17% of the time, Pallas kernels for 7%

profile of v2, /device:TPU:0, one launch (start us, length us, event | category | flops | bytes accessed | tf_op | source)
XLA Modules:
  0.0 576.7 jit_solution(738030142125781868)
XLA Ops:
  0.6 3.0 collective-permute-start
  5.0 4.0 pad_maximum_fusion
  9.6 2.6 collective-permute-start.1
  13.5 10.5 %collective-permute-done.2 = f32[1,1,1,1,1,32]{5,4,3,2,1,0:T(1,128)S(1)} collective-permute-done((f32[1,1,1,1,1,32]{5,4,3,2,1,0:T(1,128)S(1)}, f32[1,1,1,1,1,32]{5,4,3,2,1,0:T(1,128)S(1)}, u32[]{:S(2)}, u32[]{:S(2)}) %collective-permute-start.2) | collective-permute-done | bytes 160 | tf_op jit(solution)/shard_map/ppermute | solution.py:466
  25.7 2.2 broadcast_select_fusion.3
  29.9 2.2 collective-permute-done.6
  32.2 2.6 collective-permute-done.3
  41.9 3.4 collective-permute-start.9
  45.3 10.5 %collective-permute-done.11 = f32[2,1,2,1,1,32]{5,4,3,2,1,0:T(1,128)S(1)} collective-permute-done((f32[2,1,2,1,1,32]{5,4,3,2,1,0:T(1,128)S(1)}, f32[2,1,2,1,1,32]{5,4,3,2,1,0:T(1,128)S(1)}, u32[]{:S(2)}, u32[]{:S(2)}) %collective-permute-start.11) | collective-permute-done | bytes 544 | tf_op jit(solution)/shard_map/ppermute | solution.py:466
  59.0 2.3 maximum_select_fusion.6
  62.1 4.5 all-to-all-start
  79.4 2.1 pad_maximum_fusion.1
  83.3 2.3 maximum_select_fusion.1
  85.6 14.6 %shard_map.187 = (bf16[2048,128]{1,0:T(8,128)(2,1)S(1)}, bf16[2048,128]{1,0:T(8,128)(2,1)S(1)}, bf16[2048,128]{1,0:T(8,128)(2,1)S(1)}, f32[72,2048]{1,0:T(8,128)S(1)}, bf16[2048,64]{1,0:T(8,128)(2,1)S(1)}) custom-call(s32[32]{0:T(128)S(1)} %select_reduce_fusion.2.place, s32[32]{0:T(128)S(1)} %select_reduce_fusion.1.h_place, s32[8]{0:T(128)S(1)} %and_select_fusion.first_key, ...), custom_call_target="tpu_custom_call" | custom-call | tf_op jit(solution)/shard_map/pallas_call | solution.py:811
  103.7 22.3 %all-to-all-done = bf16[16,96,1024]{2,1,0:T(8,128)(2,1)} async-done(((bf16[16,96,1024]{2,1,0:T(8,128)(2,1)}), bf16[16,96,1024]{2,1,0:T(8,128)(2,1)}, u32[]{:S(2)}, u32[]{:S(2)}) %all-to-all-start) | async-done | bytes 3145760 | tf_op jit(solution)/shard_map/all_to_all | solution.py:917
  126.2 25.2 %all_to_all.55 = bf16[16,128,64]{1,2,0:T(8,128)(2,1)S(1)} all-to-all(bf16[16,128,64]{1,2,0:T(8,128)(2,1)S(1)} %copy.99), channel_id=1, replica_groups=mesh['a'=2,'b'=2,'c'=2,'d'=2,'f'=2] {'a','b','c','d'}, dimensions={0} | all-to-all | bytes 524288 | tf_op jit(solution)/shard_map/all_to_all | solution.py:968
  151.4 4.7 all-to-all-start.2
  157.4 2.6 multiply_reduce_fusion.2
  165.6 2.6 maximum_select_fusion.2
  168.2 3.6 maximum_select_fusion
  171.8 28.4 %collective-permute-done.21 = bf16[128,1152]{0,1:T(8,128)(2,1)S(1)} collective-permute-done((bf16[128,1152]{0,1:T(8,128)(2,1)S(1)}, bf16[128,1152]{0,1:T(8,128)(2,1)S(1)}, u32[]{:S(2)}, u32[]{:S(2)}) %collective-permute-start.21) | collective-permute-done | bytes 294944 | tf_op jit(solution)/shard_map/ppermute | solution.py:466
  202.0 5.7 all-to-all-start.3
  207.7 3.1 slice.142
  214.1 17.0 %all-to-all-done.3 = bf16[16,48,1152]{2,1,0:T(8,128)(2,1)} async-done(((bf16[16,48,1152]{2,1,0:T(8,128)(2,1)}), bf16[16,48,1152]{2,1,0:T(8,128)(2,1)}, u32[]{:S(2)}, u32[]{:S(2)}) %all-to-all-start.3) | async-done | bytes 1769504 | tf_op jit(solution)/shard_map/all_to_all | solution.py:901
  231.1 4.8 all-to-all-start.4
  236.0 9.2 %shard_map.188 = (bf16[768,1152]{1,0:T(8,128)(2,1)}, bf16[768,1024]{1,0:T(8,128)(2,1)S(1)}, bf16[768,512]{1,0:T(8,128)(2,1)S(1)}, bf16[768,1024]{1,0:T(8,128)(2,1)S(1)}, bf16[768,1024]{1,0:T(8,128)(2,1)}) custom-call(s32[1]{0:T(128)} %bitcast.27.where, bf16[768,1152]{1,0:T(8,128)(2,1)} %bitcast.32.rows, bf16[16,2,48,1024]{3,2,1,0:T(8,128)(2,1)} %bitcast.33.grad, ...), custom_call_target="tpu_custom_call" | custom-call | tf_op jit(solution)/shard_map/pallas_call | solution.py:766
  248.5 11.4 %all-to-all-done.4 = bf16[16,48,1152]{2,1,0:T(8,128)(2,1)} async-done(((bf16[16,48,1152]{2,1,0:T(8,128)(2,1)}), bf16[16,48,1152]{2,1,0:T(8,128)(2,1)}, u32[]{:S(2)}, u32[]{:S(2)}) %all-to-all-start.4) | async-done | bytes 1769504 | tf_op jit(solution)/shard_map/all_to_all | solution.py:901
  259.9 9.1 %shard_map.189 = (bf16[768,1152]{1,0:T(8,128)(2,1)}, bf16[768,1024]{1,0:T(8,128)(2,1)S(1)}, bf16[768,512]{1,0:T(8,128)(2,1)S(1)}, bf16[768,1024]{1,0:T(8,128)(2,1)S(1)}, bf16[768,1024]{1,0:T(8,128)(2,1)}) custom-call(s32[1]{0:T(128)} %bitcast.27.where, bf16[768,1152]{1,0:T(8,128)(2,1)} %bitcast.34.rows, bf16[16,2,48,1024]{3,2,1,0:T(8,128)(2,1)} %bitcast.33.grad, ...), custom_call_target="tpu_custom_call" | custom-call | tf_op jit(solution)/shard_map/pallas_call | solution.py:766
  272.2 28.0 %all_to_all.56 = bf16[16,48,1152]{2,1,0:T(8,128)(2,1)} all-to-all(bf16[16,48,1152]{2,1,0:T(8,128)(2,1)} %bitcast.196), channel_id=1, replica_groups=mesh['a'=2,'b'=2,'c'=2,'d'=2,'f'=2] {'b','c','d','f'}, dimensions={0} | all-to-all | bytes 3538944 | tf_op jit(solution)/shard_map/all_to_all | solution.py:901
  300.3 4.8 all-to-all-start.6
  305.0 2.5 fusion.93
  307.6 3.4 fusion.7
  311.1 3.5 add_convert_fusion
  319.8 13.8 %collective-permute-done.22 = bf16[128,1152]{0,1:T(8,128)(2,1)} collective-permute-done((bf16[128,1152]{0,1:T(8,128)(2,1)S(1)}, bf16[128,1152]{0,1:T(8,128)(2,1)}, u32[]{:S(2)}, u32[]{:S(2)}) %collective-permute-start.22) | collective-permute-done | bytes 294944 | tf_op jit(solution)/shard_map/ppermute | solution.py:466
  334.6 2.3 fusion
  336.9 2.2 multiply_reduce_fusion
  342.1 15.3 %all_to_all.57 = bf16[16,128,64]{1,2,0:T(8,128)(2,1)S(1)} all-to-all(bf16[16,128,64]{1,2,0:T(8,128)(2,1)S(1)} %bitcast.200), channel_id=1, replica_groups=mesh['a'=2,'b'=2,'c'=2,'d'=2,'f'=2] {'a','b','c','d'}, dimensions={0} | all-to-all | bytes 524288 | tf_op jit(solution)/shard_map/all_to_all | solution.py:968
  357.7 4.8 all-to-all-start.8
  369.1 13.6 %shard_map.190 = (f32[2048,128]{1,0:T(8,128)S(1)}, bf16[2048,128]{1,0:T(8,128)(2,1)}) custom-call(s32[32]{0:T(128)S(1)} %select_reduce_fusion.2.place, s32[8]{0:T(128)S(1)} %and_select_fusion.first_key, s32[1]{0:T(128)} %bitcast.26.core, bf16[2048,128]{1,0:T(8,128)(2,1)S(1)} %copy-done.13, bf16[2048,128]{1,0:T(8,128)(2,1)S(1)} %copy-done.15, ...), custom_call_target="tpu_custom_call" | custom-call | tf_op jit(solution)/shard_map/pallas_call | solution.py:811
  390.6 10.5 %collective-permute-done.25 = bf16[256,1024]{1,0:T(8,128)(2,1)S(1)} collective-permute-done((bf16[256,1024]{1,0:T(8,128)(2,1)S(1)}, bf16[256,1024]{1,0:T(8,128)(2,1)S(1)}, u32[]{:S(2)}, u32[]{:S(2)}) %collective-permute-start.25) | collective-permute-done | bytes 524320 | tf_op jit(solution)/shard_map/ppermute | solution.py:466
  401.8 20.0 %all-to-all-done.8 = bf16[16,96,1024]{2,1,0:T(8,128)(2,1)} async-done(((bf16[16,96,1024]{2,1,0:T(8,128)(2,1)}), bf16[16,96,1024]{2,1,0:T(8,128)(2,1)}, u32[]{:S(2)}, u32[]{:S(2)}) %all-to-all-start.8) | async-done | bytes 3145760 | tf_op jit(solution)/shard_map/all_to_all | solution.py:1085
  421.9 4.8 collective-permute-start.29
  427.8 6.0 %collective-permute-done.29 = bf16[128,1024]{1,0:T(8,128)(2,1)S(1)} collective-permute-done((bf16[128,1024]{1,0:T(8,128)(2,1)S(1)}, bf16[128,1024]{1,0:T(8,128)(2,1)S(1)}, u32[]{:S(2)}, u32[]{:S(2)}) %collective-permute-start.29) | collective-permute-done | bytes 262176 | tf_op jit(solution)/shard_map/ppermute | solution.py:466
  433.9 8.7 %collective-permute-start.30 = (bf16[64,1024]{1,0:T(8,128)(2,1)S(1)}, bf16[64,1024]{1,0:T(8,128)(2,1)S(1)}, u32[]{:S(2)}, u32[]{:S(2)}) collective-permute-start(bf16[64,1024]{1,0:T(8,128)(2,1)S(1)} %dynamic-slice_convert_fusion.2), channel_id=1, source_target_pairs={{0,8},{8,0},{1,9},{9,1},{2,10},{10,2},{3,11},{11,3},{4,12},{12,4},... | collective-permute-start | bytes 393224 | tf_op jit(solution)/shard_map/ppermute | solution.py:466
  443.0 3.2 collective-permute-done.30
  446.2 2.4 collective-permute-start.31
  448.6 2.8 collective-permute-done.31
  451.5 2.4 collective-permute-start.32
  457.4 2.8 collective-permute-done.27
  461.9 4.1 all-to-all-start.9
  469.7 4.1 slice_convert_fusion
  473.8 8.0 %collective-permute-done.33 = bf16[2,1,1,1,384,128]{5,4,0,3,2,1:T(8,128)(2,1)S(1)} collective-permute-done((bf16[2,1,1,1,384,128]{5,4,0,3,2,1:T(8,128)(2,1)S(1)}, bf16[2,1,1,1,384,128]{5,4,0,3,2,1:T(8,128)(2,1)S(1)}, u32[]{:S(2)}, u32[]{:S(2)}) %collective-permute-start.33) | collective-permute-done | bytes 196640 | tf_op jit(solution)/shard_map/ppermute | solution.py:466
  484.2 2.8 slice_convert_fusion.1
  487.1 5.5 collective-permute-done.34
  494.5 4.9 all-to-all-start.10
  501.7 3.5 fusion.22
  505.2 34.4 %collective-permute-done.40 = f32[40,1024]{1,0:T(8,128)S(1)} collective-permute-done((f32[40,1024]{1,0:T(8,128)S(1)}, f32[40,1024]{1,0:T(8,128)S(1)}, u32[]{:S(2)}, u32[]{:S(2)}) %collective-permute-start.40) | collective-permute-done | bytes 163872 | tf_op jit(solution)/shard_map/ppermute | solution.py:466
  541.1 4.4 collective-permute-done.41
  545.6 2.5 collective-permute-start.42
  549.3 5.8 %collective-permute-done.42 = f32[40,1024]{1,0:T(8,128)S(1)} collective-permute-done((f32[40,1024]{1,0:T(8,128)S(1)}, f32[40,1024]{1,0:T(8,128)S(1)}, u32[]{:S(2)}, u32[]{:S(2)}) %collective-permute-start.42) | collective-permute-done | bytes 163872 | tf_op jit(solution)/shard_map/ppermute | solution.py:466
  557.9 2.1 fusion.15
  561.8 3.6 shard_map.191
  566.1 7.2 %collective-permute-done.37 = bf16[128,1024]{0,1:T(8,128)(2,1)S(1)} collective-permute-done((bf16[128,1024]{0,1:T(8,128)(2,1)S(1)}, bf16[128,1024]{0,1:T(8,128)(2,1)S(1)}, u32[]{:S(2)}, u32[]{:S(2)}) %collective-permute-start.37) | collective-permute-done | bytes 262176 | tf_op jit(solution)/shard_map/ppermute | solution.py:466
  573.2 2.1 fusion.37
  (360 shorter events, 104.4 us)
Async XLA Ops:
  0.6 8.4 %collective-permute-start = (bf16[512]{0:T(512)(128)(2,1)}, bf16[512]{0:T(512)(128)(2,1)S(1)}, u32[]{:S(2)}, u32[]{:S(2)}) collective-permute-start(bf16[512]{0:T(512)(128)(2,1)} %param.16), channel_id=1, source_target_pairs={{0,1},{1,0},{2,3},{3,2},{4,5},{5,4},{6,7},{7,6},{8,9},{9,8},{10,11... | collective-permute-start | bytes 3080 | tf_op jit(solution)/shard_map/ppermute | solution.py:466
  9.6 14.4 %collective-permute-start.1 = (bf16[1,1,1,1,128,1024]{4,5,3,2,1,0:T(8,128)(2,1)S(1)}, bf16[1,1,1,1,128,1024]{4,5,3,2,1,0:T(8,128)(2,1)S(1)}, u32[]{:S(2)}, u32[]{:S(2)}) collective-permute-start(bf16[1,1,1,1,128,1024]{4,5,3,2,1,0:T(8,128)(2,1)S(1)} %bitcast.201), channel_id=1, source_target_pairs={{0,16},{16,0},{1,17},{17,1},{2,18},{18,2},{3,19},{19,3},{4,20},{20... | collective-permute-start | bytes 786440 | tf_op jit(solution)/shard_map/ppermute | solution.py:466
  13.1 10.9 %collective-permute-start.2 = (f32[1,1,1,1,1,32]{5,4,3,2,1,0:T(1,128)S(1)}, f32[1,1,1,1,1,32]{5,4,3,2,1,0:T(1,128)S(1)}, u32[]{:S(2)}, u32[]{:S(2)}) collective-permute-start(f32[1,1,1,1,1,32]{5,4,3,2,1,0:T(1,128)S(1)} %bitcast.224), channel_id=1, source_target_pairs={{0,16},{16,0},{1,17},{17,1},{2,18},{18,2},{3,19},{19,3},{4,20},{20... | collective-permute-start | bytes 392 | tf_op jit(solution)/shard_map/ppermute | solution.py:466
  24.1 8.0 %collective-permute-start.4 = (bf16[2,1,1,1,128,512]{4,5,3,2,1,0:T(8,128)(2,1)S(1)}, bf16[2,1,1,1,128,512]{4,5,3,2,1,0:T(8,128)(2,1)S(1)}, u32[]{:S(2)}, u32[]{:S(2)}) collective-permute-start(bf16[2,1,1,1,128,512]{4,5,3,2,1,0:T(8,128)(2,1)S(1)} %get-tuple-element.230), channel_id=1, source_target_pairs={{0,4},{4,0},{1,5},{5,1},{2,6},{6,2},{3,7},{7,3},{8,12},{12,8},{9,1... | collective-permute-start | bytes 786440 | tf_op jit(solution)/shard_map/ppermute | solution.py:466
  27.9 45.3 %copy-start.43 = (bf16[512,64]{1,0:T(8,128)(2,1)}, bf16[512,64]{1,0:T(8,128)(2,1)S(1)}, u32[]{:S(2)}) copy-start(bf16[512,64]{1,0:T(8,128)(2,1)S(1)} %get-tuple-element.225) | copy-start | bytes 196612
  27.9 6.9 %collective-permute-start.3 = (bf16[2,1,1,1,128,512]{4,5,3,2,1,0:T(8,128)(2,1)S(1)}, bf16[2,1,1,1,128,512]{4,5,3,2,1,0:T(8,128)(2,1)S(1)}, u32[]{:S(2)}, u32[]{:S(2)}) collective-permute-start(bf16[2,1,1,1,128,512]{4,5,3,2,1,0:T(8,128)(2,1)S(1)} %get-tuple-element.231), channel_id=1, source_target_pairs={{0,8},{8,0},{1,9},{9,1},{2,10},{10,2},{3,11},{11,3},{4,12},{12,4},... | collective-permute-start | bytes 786440 | tf_op jit(solution)/shard_map/ppermute | solution.py:466
  28.6 3.6 collective-permute-start.6
  29.3 7.5 %collective-permute-start.5 = (bf16[512,256]{1,0:T(8,128)(2,1)S(1)}, bf16[512,256]{1,0:T(8,128)(2,1)S(1)}, u32[]{:S(2)}, u32[]{:S(2)}) collective-permute-start(bf16[512,256]{1,0:T(8,128)(2,1)S(1)} %pad_maximum_fusion.6), channel_id=1, source_target_pairs={{0,1},{1,0},{2,3},{3,2},{4,5},{5,4},{6,7},{7,6},{8,9},{9,8},{10,11... | collective-permute-start | bytes 786440 | tf_op jit(solution)/shard_map/ppermute | solution.py:466
  36.8 20.9 %copy-start.52 = (bf16[512,256]{1,0:T(8,128)(2,1)}, bf16[512,256]{1,0:T(8,128)(2,1)S(1)}, u32[]{:S(2)}) copy-start(bf16[512,256]{1,0:T(8,128)(2,1)S(1)} %collective-permute-done.5) | copy-start | bytes 786436
  36.8 20.9 %collective-permute-start.7 = (bf16[2,2,1,1,128,512]{4,5,3,2,1,0:T(8,128)(2,1)S(1)}, bf16[2,2,1,1,128,512]{4,5,3,2,1,0:T(8,128)(2,1)}, u32[]{:S(2)}, u32[]{:S(2)}) collective-permute-start(bf16[2,2,1,1,128,512]{4,5,3,2,1,0:T(8,128)(2,1)S(1)} %maximum_select_fusion.11), channel_id=1, source_target_pairs={{0,4},{4,0},{1,5},{5,1},{2,6},{6,2},{3,7},{7,3},{8,12},{12,8},{9,1... | collective-permute-start | bytes 1572872 | tf_op jit(solution)/shard_map/ppermute | solution.py:466
  38.3 20.8 %collective-permute-start.8 = (bf16[2,1,2,1,128,512]{4,5,3,2,1,0:T(8,128)(2,1)S(1)}, bf16[2,1,2,1,128,512]{4,5,3,2,1,0:T(8,128)(2,1)}, u32[]{:S(2)}, u32[]{:S(2)}) collective-permute-start(bf16[2,1,2,1,128,512]{4,5,3,2,1,0:T(8,128)(2,1)S(1)} %maximum_select_fusion.12), channel_id=1, source_target_pairs={{0,8},{8,0},{1,9},{9,1},{2,10},{10,2},{3,11},{11,3},{4,12},{12,4},... | collective-permute-start | bytes 1572872 | tf_op jit(solution)/shard_map/ppermute | solution.py:466
  39.5 22.6 %collective-permute-start.12 = (bf16[256,1024]{1,0:T(8,128)(2,1)}, bf16[256,1024]{1,0:T(8,128)(2,1)}, u32[]{:S(2)}, u32[]{:S(2)}) collective-permute-start(bf16[256,1024]{1,0:T(8,128)(2,1)} %slice_select_fusion.1), channel_id=1, source_target_pairs={{0,1},{1,0},{2,3},{3,2},{4,5},{5,4},{6,7},{7,6},{8,9},{9,8},{10,11... | collective-permute-start | bytes 1572872 | tf_op jit(solution)/shard_map/ppermute | solution.py:466
  40.0 15.8 %collective-permute-start.11 = (f32[2,1,2,1,1,32]{5,4,3,2,1,0:T(1,128)S(1)}, f32[2,1,2,1,1,32]{5,4,3,2,1,0:T(1,128)S(1)}, u32[]{:S(2)}, u32[]{:S(2)}) collective-permute-start(f32[2,1,2,1,1,32]{5,4,3,2,1,0:T(1,128)S(1)} %broadcast_select_fusion.7), channel_id=1, source_target_pairs={{0,8},{8,0},{1,9},{9,1},{2,10},{10,2},{3,11},{11,3},{4,12},{12,4},... | collective-permute-start | bytes 1544 | tf_op jit(solution)/shard_map/ppermute | solution.py:466
  41.9 19.5 %copy-start.46 = (bf16[1,128,1024]{1,2,0:T(8,128)(2,1)}, bf16[1,128,1024]{1,2,0:T(8,128)(2,1)S(1)}, u32[]{:S(2)}) copy-start(bf16[1,128,1024]{1,2,0:T(8,128)(2,1)S(1)} %copy.89) | copy-start | bytes 786436
  41.9 19.5 %collective-permute-start.9 = (bf16[128,1024]{0,1:T(8,128)(2,1)S(1)}, bf16[128,1024]{0,1:T(8,128)(2,1)S(1)}, u32[]{:S(2)}, u32[]{:S(2)}) collective-permute-start(bf16[128,1024]{0,1:T(8,128)(2,1)S(1)} %bitcast.199), channel_id=1, source_target_pairs={{0,16},{16,0},{1,17},{17,1},{2,18},{18,2},{3,19},{19,3},{4,20},{20... | collective-permute-start | bytes 786440 | tf_op jit(solution)/shard_map/ppermute | solution.py:466
  55.8 5.6 collective-permute-start.10
  62.1 63.9 %all-to-all-start = ((bf16[16,96,1024]{2,1,0:T(8,128)(2,1)}), bf16[16,96,1024]{2,1,0:T(8,128)(2,1)}, u32[]{:S(2)}, u32[]{:S(2)}) async-start(bf16[16,96,1024]{2,1,0:T(8,128)(2,1)} %pad_maximum_fusion), calls=%async_computation | async-start | bytes 6291456 | tf_op jit(solution)/shard_map/all_to_all | solution.py:917
  69.1 7.2 %collective-permute-start.15 = (bf16[512]{0:T(512)(128)(2,1)}, bf16[512]{0:T(512)(128)(2,1)}, u32[]{:S(2)}, u32[]{:S(2)}) collective-permute-start(bf16[512]{0:T(512)(128)(2,1)} %param.19), channel_id=1, source_target_pairs={{0,1},{1,0},{2,3},{3,2},{4,5},{5,4},{6,7},{7,6},{8,9},{9,8},{10,11... | collective-permute-start | bytes 3080 | tf_op jit(solution)/shard_map/ppermute | solution.py:466
  69.6 6.6 %collective-permute-start.16 = (bf16[512,32]{0,1:T(8,128)(2,1)}, bf16[512,32]{0,1:T(8,128)(2,1)}, u32[]{:S(2)}, u32[]{:S(2)}) collective-permute-start(bf16[512,32]{0,1:T(8,128)(2,1)} %param.20), channel_id=1, source_target_pairs={{0,1},{1,0},{2,3},{3,2},{4,5},{5,4},{6,7},{7,6},{8,9},{9,8},{10,11... | collective-permute-start | bytes 98312 | tf_op jit(solution)/shard_map/ppermute | solution.py:466
  75.7 10.0 %collective-permute-start.13 = (bf16[1024,512]{1,0:T(8,128)(2,1)S(1)}, bf16[1024,512]{1,0:T(8,128)(2,1)S(1)}, u32[]{:S(2)}, u32[]{:S(2)}) collective-permute-start(bf16[1024,512]{1,0:T(8,128)(2,1)S(1)} %bitcast.167), channel_id=1, source_target_pairs={{0,2},{2,0},{1,3},{3,1},{4,6},{6,4},{5,7},{7,5},{8,10},{10,8},{9,1... | collective-permute-start | bytes 3145736 | tf_op jit(solution)/shard_map/ppermute | solution.py:466
  75.7 9.9 %collective-permute-start.14 = (bf16[1024,512]{1,0:T(8,128)(2,1)S(1)}, bf16[1024,512]{1,0:T(8,128)(2,1)S(1)}, u32[]{:S(2)}, u32[]{:S(2)}) collective-permute-start(bf16[1024,512]{1,0:T(8,128)(2,1)S(1)} %bitcast.170), channel_id=1, source_target_pairs={{0,2},{2,0},{1,3},{3,1},{4,6},{6,4},{5,7},{7,5},{8,10},{10,8},{9,1... | collective-permute-start | bytes 3145736 | tf_op jit(solution)/shard_map/ppermute | solution.py:466
  76.2 5.3 collective-permute-start.17
  78.0 25.7 %collective-permute-start.18 = (bf16[256,2048]{1,0:T(8,128)(2,1)S(1)}, bf16[256,2048]{1,0:T(8,128)(2,1)}, u32[]{:S(2)}, u32[]{:S(2)}) collective-permute-start(bf16[256,2048]{1,0:T(8,128)(2,1)S(1)} %slice_select_fusion), channel_id=1, source_target_pairs={{0,1},{1,0},{2,3},{3,2},{4,5},{5,4},{6,7},{7,6},{8,9},{9,8},{10,11... | collective-permute-start | bytes 3145736 | tf_op jit(solution)/shard_map/ppermute | solution.py:466
  78.6 2.9 collective-permute-start.19
  151.4 50.6 %all-to-all-start.2 = ((bf16[16,96,1024]{2,1,0:T(8,128)(2,1)}), bf16[16,96,1024]{2,1,0:T(8,128)(2,1)}, u32[]{:S(2)}, u32[]{:S(2)}) async-start(bf16[16,96,1024]{2,1,0:T(8,128)(2,1)} %pad_maximum_fusion.1), calls=%async_computation.2 | async-start | bytes 6291456 | tf_op jit(solution)/shard_map/all_to_all | solution.py:901
  156.9 8.7 %collective-permute-start.20 = (bf16[256,2048]{1,0:T(8,128)(2,1)}, bf16[256,2048]{1,0:T(8,128)(2,1)S(1)}, u32[]{:S(2)}, u32[]{:S(2)}) collective-permute-start(bf16[256,2048]{1,0:T(8,128)(2,1)} %collective-permute-done.18), channel_id=1, source_target_pairs={{0,2},{2,0},{1,3},{3,1},{4,6},{6,4},{5,7},{7,5},{8,10},{10,8},{9,1... | collective-permute-start | bytes 3145736 | tf_op jit(solution)/shard_map/ppermute | solution.py:466
  162.5 37.7 %collective-permute-start.21 = (bf16[128,1152]{0,1:T(8,128)(2,1)S(1)}, bf16[128,1152]{0,1:T(8,128)(2,1)S(1)}, u32[]{:S(2)}, u32[]{:S(2)}) collective-permute-start(bf16[128,1152]{0,1:T(8,128)(2,1)S(1)} %maximum_maximum_fusion), channel_id=1, source_target_pairs={{0,16},{16,0},{1,17},{17,1},{2,18},{18,2},{3,19},{19,3},{4,20},{20... | collective-permute-start | bytes 884744 | tf_op jit(solution)/shard_map/ppermute | solution.py:466
  202.0 29.1 %all-to-all-start.3 = ((bf16[16,48,1152]{2,1,0:T(8,128)(2,1)}), bf16[16,48,1152]{2,1,0:T(8,128)(2,1)}, u32[]{:S(2)}, u32[]{:S(2)}) async-start(bf16[16,48,1152]{2,1,0:T(8,128)(2,1)} %convolution_convert_fusion.1), calls=%async_computation.3 | async-start | bytes 3538944 | tf_op jit(solution)/shard_map/all_to_all | solution.py:901
  231.1 28.7 %all-to-all-start.4 = ((bf16[16,48,1152]{2,1,0:T(8,128)(2,1)}), bf16[16,48,1152]{2,1,0:T(8,128)(2,1)}, u32[]{:S(2)}, u32[]{:S(2)}) async-start(bf16[16,48,1152]{2,1,0:T(8,128)(2,1)} %convolution_convert_fusion), calls=%async_computation.4 | async-start | bytes 3538944 | tf_op jit(solution)/shard_map/all_to_all | solution.py:901
  300.3 34.3 %all-to-all-start.6 = ((bf16[16,48,1152]{2,1,0:T(8,128)(2,1)}), bf16[16,48,1152]{2,1,0:T(8,128)(2,1)}, u32[]{:S(2)}, u32[]{:S(2)}) async-start(bf16[16,48,1152]{2,1,0:T(8,128)(2,1)} %bitcast.195), calls=%async_computation.6 | async-start | bytes 3538944 | tf_op jit(solution)/shard_map/all_to_all | solution.py:901
  315.5 18.1 %collective-permute-start.22 = (bf16[128,1152]{0,1:T(8,128)(2,1)S(1)}, bf16[128,1152]{0,1:T(8,128)(2,1)}, u32[]{:S(2)}, u32[]{:S(2)}) collective-permute-start(bf16[128,1152]{0,1:T(8,128)(2,1)S(1)} %fusion.1), channel_id=1, source_target_pairs={{0,16},{16,0},{1,17},{17,1},{2,18},{18,2},{3,19},{19,3},{4,20},{20... | collective-permute-start | bytes 884744 | tf_op jit(solution)/shard_map/ppermute | solution.py:466
  319.8 17.1 %copy-start.69 = (f32[128]{0:T(128)S(1)}, f32[128]{0:T(128)}, u32[]{:S(2)}) copy-start(f32[128]{0:T(128)} %copy-done.68) | copy-start | bytes 1540
  319.8 17.2 %copy-start.27 = (f32[128,1024]{0,1:T(8,128)S(1)}, f32[128,1024]{0,1:T(8,128)}, u32[]{:S(2)}) copy-start(f32[128,1024]{0,1:T(8,128)} %copy-done.26) | copy-start | bytes 1572868
  357.7 64.1 %all-to-all-start.8 = ((bf16[16,96,1024]{2,1,0:T(8,128)(2,1)}), bf16[16,96,1024]{2,1,0:T(8,128)(2,1)}, u32[]{:S(2)}, u32[]{:S(2)}) async-start(bf16[16,96,1024]{2,1,0:T(8,128)(2,1)} %pad_maximum_fusion.2), calls=%async_computation.8 | async-start | bytes 6291456 | tf_op jit(solution)/shard_map/all_to_all | solution.py:1085
  365.1 18.5 %copy-start.30 = (f32[128,1024]{0,1:T(8,128)S(1)}, f32[128,1024]{0,1:T(8,128)}, u32[]{:S(2)}) copy-start(f32[128,1024]{0,1:T(8,128)} %copy-done.29) | copy-start | bytes 1572868
  365.2 18.5 %collective-permute-start.23 = (bf16[512,1024]{1,0:T(8,128)(2,1)S(1)}, bf16[512,1024]{1,0:T(8,128)(2,1)S(1)}, u32[]{:S(2)}, u32[]{:S(2)}) collective-permute-start(bf16[512,1024]{1,0:T(8,128)(2,1)S(1)} %convolution_convert_fusion.4), channel_id=1, source_target_pairs={{0,2},{2,0},{1,3},{3,1},{4,6},{6,4},{5,7},{7,5},{8,10},{10,8},{9,1... | collective-permute-start | bytes 3145736 | tf_op jit(solution)/shard_map/ppermute | solution.py:466
  385.4 2.3 collective-permute-start.24
  386.8 14.3 %collective-permute-start.25 = (bf16[256,1024]{1,0:T(8,128)(2,1)S(1)}, bf16[256,1024]{1,0:T(8,128)(2,1)S(1)}, u32[]{:S(2)}, u32[]{:S(2)}) collective-permute-start(bf16[256,1024]{1,0:T(8,128)(2,1)S(1)} %dynamic-slice_convert_fusion), channel_id=1, source_target_pairs={{0,1},{1,0},{2,3},{3,2},{4,5},{5,4},{6,7},{7,6},{8,9},{9,8},{10,11... | collective-permute-start | bytes 1572872 | tf_op jit(solution)/shard_map/ppermute | solution.py:466
  387.4 66.5 %collective-permute-start.26 = (f32[40,1024]{1,0:T(8,128)}, f32[40,1024]{1,0:T(8,128)}, u32[]{:S(2)}, u32[]{:S(2)}) collective-permute-start(f32[40,1024]{1,0:T(8,128)} %pad_maximum_fusion.7), channel_id=1, source_target_pairs={{0,2},{2,0},{1,3},{3,1},{4,6},{6,4},{5,7},{7,5},{8,10},{10,8},{9,1... | collective-permute-start | bytes 491528 | tf_op jit(solution)/shard_map/ppermute | solution.py:466
  390.6 36.1 %copy-start.1 = (bf16[1024,512]{1,0:T(8,128)(2,1)S(1)}, bf16[1024,512]{1,0:T(8,128)(2,1)}, u32[]{:S(2)}) copy-start(bf16[1024,512]{1,0:T(8,128)(2,1)} %copy-done) | copy-start | bytes 3145732
  421.8 20.9 %copy-start.44 = (bf16[512,64]{1,0:T(8,128)(2,1)S(1)}, bf16[512,64]{1,0:T(8,128)(2,1)}, u32[]{:S(2)}) copy-start(bf16[512,64]{1,0:T(8,128)(2,1)} %copy-done.43) | copy-start | bytes 196612
  421.9 20.9 %copy-start.49 = (bf16[512,64]{1,0:T(8,128)(2,1)S(1)}, bf16[512,64]{1,0:T(8,128)(2,1)}, u32[]{:S(2)}) copy-start(bf16[512,64]{1,0:T(8,128)(2,1)} %get-tuple-element.218) | copy-start | bytes 196612
  421.9 11.9 %collective-permute-start.29 = (bf16[128,1024]{1,0:T(8,128)(2,1)S(1)}, bf16[128,1024]{1,0:T(8,128)(2,1)S(1)}, u32[]{:S(2)}, u32[]{:S(2)}) collective-permute-start(bf16[128,1024]{1,0:T(8,128)(2,1)S(1)} %dynamic-slice_convert_fusion.1), channel_id=1, source_target_pairs={{0,4},{4,0},{1,5},{5,1},{2,6},{6,2},{3,7},{7,3},{8,12},{12,8},{9,1... | collective-permute-start | bytes 786440 | tf_op jit(solution)/shard_map/ppermute | solution.py:466
  427.2 26.7 %copy-start.47 = (f32[40,1024]{1,0:T(8,128)S(1)}, f32[40,1024]{1,0:T(8,128)}, u32[]{:S(2)}) copy-start(f32[40,1024]{1,0:T(8,128)} %pad_maximum_fusion.7) | copy-start | bytes 491524
  427.2 15.5 %collective-permute-start.28 = (f32[512,128]{1,0:T(8,128)S(1)}, f32[512,128]{1,0:T(8,128)S(1)}, u32[]{:S(2)}, u32[]{:S(2)}) collective-permute-start(f32[512,128]{1,0:T(8,128)S(1)} %get-tuple-element.260), channel_id=1, source_target_pairs={{0,1},{1,0},{2,3},{3,2},{4,5},{5,4},{6,7},{7,6},{8,9},{9,8},{10,11... | collective-permute-start | bytes 786440 | tf_op jit(solution)/shard_map/ppermute | solution.py:466
  433.9 21.6 %copy-start.5 = (bf16[768,1024]{1,0:T(8,128)(2,1)S(1)}, bf16[768,1024]{1,0:T(8,128)(2,1)}, u32[]{:S(2)}) copy-start(bf16[768,1024]{1,0:T(8,128)(2,1)} %copy-done.4) | copy-start | bytes 4718596
  433.9 21.6 %copy-start.7 = (bf16[768,1024]{1,0:T(8,128)(2,1)S(1)}, bf16[768,1024]{1,0:T(8,128)(2,1)}, u32[]{:S(2)}) copy-start(bf16[768,1024]{1,0:T(8,128)(2,1)} %copy-done.6) | copy-start | bytes 4718596
  433.9 12.2 %collective-permute-start.30 = (bf16[64,1024]{1,0:T(8,128)(2,1)S(1)}, bf16[64,1024]{1,0:T(8,128)(2,1)S(1)}, u32[]{:S(2)}, u32[]{:S(2)}) collective-permute-start(bf16[64,1024]{1,0:T(8,128)(2,1)S(1)} %dynamic-slice_convert_fusion.2), channel_id=1, source_target_pairs={{0,8},{8,0},{1,9},{9,1},{2,10},{10,2},{3,11},{11,3},{4,12},{12,4},... | collective-permute-start | bytes 393224 | tf_op jit(solution)/shard_map/ppermute | solution.py:466
  446.2 5.2 collective-permute-start.31
  451.5 14.5 %collective-permute-start.32 = (bf16[1,1,1,1,784,128]{5,4,3,2,1,0:T(8,128)(2,1)S(1)}, bf16[1,1,1,1,784,128]{5,4,3,2,1,0:T(8,128)(2,1)S(1)}, u32[]{:S(2)}, u32[]{:S(2)}) collective-permute-start(bf16[1,1,1,1,784,128]{5,4,3,2,1,0:T(8,128)(2,1)S(1)} %maximum_bitcast_fusion), channel_id=1, source_target_pairs={{0,16},{16,0},{1,17},{17,1},{2,18},{18,2},{3,19},{19,3},{4,20},{20... | collective-permute-start | bytes 602120 | tf_op jit(solution)/shard_map/ppermute | solution.py:466
  454.8 5.4 collective-permute-start.27
  461.9 32.5 %all-to-all-start.9 = ((bf16[16,128,128]{1,2,0:T(8,128)(2,1)}), bf16[16,128,128]{1,2,0:T(8,128)(2,1)S(1)}, u32[]{:S(2)}, u32[]{:S(2)}) async-start(bf16[16,128,128]{1,2,0:T(8,128)(2,1)} %copy.109), calls=%async_computation.9 | async-start | bytes 1048576 | tf_op jit(solution)/shard_map/all_to_all | solution.py:968
  466.2 15.5 %collective-permute-start.33 = (bf16[2,1,1,1,384,128]{5,4,0,3,2,1:T(8,128)(2,1)S(1)}, bf16[2,1,1,1,384,128]{5,4,0,3,2,1:T(8,128)(2,1)S(1)}, u32[]{:S(2)}, u32[]{:S(2)}) collective-permute-start(bf16[2,1,1,1,384,128]{5,4,0,3,2,1:T(8,128)(2,1)S(1)} %get-tuple-element.236), channel_id=1, source_target_pairs={{0,8},{8,0},{1,9},{9,1},{2,10},{10,2},{3,11},{11,3},{4,12},{12,4},... | collective-permute-start | bytes 589832 | tf_op jit(solution)/shard_map/ppermute | solution.py:466
  468.2 15.2 %collective-permute-start.35 = (bf16[2,1,1,1,400,128]{5,4,0,3,2,1:T(8,128)(2,1)S(1)}, bf16[2,1,1,1,400,128]{5,4,0,3,2,1:T(8,128)(2,1)S(1)}, u32[]{:S(2)}, u32[]{:S(2)}) collective-permute-start(bf16[2,1,1,1,400,128]{5,4,0,3,2,1:T(8,128)(2,1)S(1)} %get-tuple-element.233), channel_id=1, source_target_pairs={{0,4},{4,0},{1,5},{5,1},{2,6},{6,2},{3,7},{7,3},{8,12},{12,8},{9,1... | collective-permute-start | bytes 614408 | tf_op jit(solution)/shard_map/ppermute | solution.py:466
  481.9 10.7 %collective-permute-start.34 = (bf16[2,2,1,1,384,128]{5,4,3,2,1,0:T(8,128)(2,1)S(1)}, bf16[2,2,1,1,384,128]{5,4,3,2,1,0:T(8,128)(2,1)S(1)}, u32[]{:S(2)}, u32[]{:S(2)}) collective-permute-start(bf16[2,2,1,1,384,128]{5,4,3,2,1,0:T(8,128)(2,1)S(1)} %maximum_select_fusion.18), channel_id=1, source_target_pairs={{0,4},{4,0},{1,5},{5,1},{2,6},{6,2},{3,7},{7,3},{8,12},{12,8},{9,1... | collective-permute-start | bytes 1179656 | tf_op jit(solution)/shard_map/ppermute | solution.py:466
  483.5 10.8 %collective-permute-start.36 = (bf16[2,1,2,1,400,128]{5,4,3,2,1,0:T(8,128)(2,1)S(1)}, bf16[2,1,2,1,400,128]{5,4,3,2,1,0:T(8,128)(2,1)S(1)}, u32[]{:S(2)}, u32[]{:S(2)}) collective-permute-start(bf16[2,1,2,1,400,128]{5,4,3,2,1,0:T(8,128)(2,1)S(1)} %maximum_select_fusion.15), channel_id=1, source_target_pairs={{0,8},{8,0},{1,9},{9,1},{2,10},{10,2},{3,11},{11,3},{4,12},{12,4},... | collective-permute-start | bytes 1228808 | tf_op jit(solution)/shard_map/ppermute | solution.py:466
  494.5 63.4 %all-to-all-start.10 = ((bf16[16,96,1024]{2,1,0:T(8,128)(2,1)}), bf16[16,96,1024]{2,1,0:T(8,128)(2,1)}, u32[]{:S(2)}, u32[]{:S(2)}) async-start(bf16[16,96,1024]{2,1,0:T(8,128)(2,1)} %pad_maximum_fusion.3), calls=%async_computation.10 | async-start | bytes 6291456 | tf_op jit(solution)/shard_map/all_to_all | solution.py:901
  499.4 56.9 %collective-permute-start.38 = (bf16[2,2,2,1,384,128]{5,4,3,2,1,0:T(8,128)(2,1)S(1)}, bf16[2,2,2,1,384,128]{5,4,3,2,1,0:T(8,128)(2,1)}, u32[]{:S(2)}, u32[]{:S(2)}) collective-permute-start(bf16[2,2,2,1,384,128]{5,4,3,2,1,0:T(8,128)(2,1)S(1)} %maximum_select_fusion.9), channel_id=1, source_target_pairs={{0,2},{2,0},{1,3},{3,1},{4,6},{6,4},{5,7},{7,5},{8,10},{10,8},{9,1... | collective-permute-start | bytes 2359304 | tf_op jit(solution)/shard_map/ppermute | solution.py:466
  499.9 39.7 %collective-permute-start.40 = (f32[40,1024]{1,0:T(8,128)S(1)}, f32[40,1024]{1,0:T(8,128)S(1)}, u32[]{:S(2)}, u32[]{:S(2)}) collective-permute-start(f32[40,1024]{1,0:T(8,128)S(1)} %copy-done.48), channel_id=1, source_target_pairs={{0,4},{4,0},{1,5},{5,1},{2,6},{6,2},{3,7},{7,3},{8,12},{12,8},{9,1... | collective-permute-start | bytes 491528 | tf_op jit(solution)/shard_map/ppermute | solution.py:466
  501.7 46.5 %copy-start.31 = (f32[128,1024]{0,1:T(8,128)S(1)}, f32[128,1024]{0,1:T(8,128)}, u32[]{:S(2)}) copy-start(f32[128,1024]{0,1:T(8,128)} %copy-done.29) | copy-start | bytes 1572868
  539.6 5.9 %collective-permute-start.41 = (f32[40,1024]{1,0:T(8,128)S(1)}, f32[40,1024]{1,0:T(8,128)S(1)}, u32[]{:S(2)}, u32[]{:S(2)}) collective-permute-start(f32[40,1024]{1,0:T(8,128)S(1)} %add.248), channel_id=1, source_target_pairs={{0,8},{8,0},{1,9},{9,1},{2,10},{10,2},{3,11},{11,3},{4,12},{12,4},... | collective-permute-start | bytes 491528 | tf_op jit(solution)/shard_map/ppermute | solution.py:466
  545.6 9.4 %collective-permute-start.42 = (f32[40,1024]{1,0:T(8,128)S(1)}, f32[40,1024]{1,0:T(8,128)S(1)}, u32[]{:S(2)}, u32[]{:S(2)}) collective-permute-start(f32[40,1024]{1,0:T(8,128)S(1)} %add.249), channel_id=1, source_target_pairs={{0,16},{16,0},{1,17},{17,1},{2,18},{18,2},{3,19},{19,3},{4,20},{20... | collective-permute-start | bytes 491528 | tf_op jit(solution)/shard_map/ppermute | solution.py:466
  549.3 10.9 %collective-permute-start.39 = (bf16[2,2,2,1,400,128]{5,4,3,2,1,0:T(8,128)(2,1)S(1)}, bf16[2,2,2,1,400,128]{5,4,3,2,1,0:T(8,128)(2,1)}, u32[]{:S(2)}, u32[]{:S(2)}) collective-permute-start(bf16[2,2,2,1,400,128]{5,4,3,2,1,0:T(8,128)(2,1)S(1)} %maximum_select_fusion.8), channel_id=1, source_target_pairs={{0,2},{2,0},{1,3},{3,1},{4,6},{6,4},{5,7},{7,5},{8,10},{10,8},{9,1... | collective-permute-start | bytes 2457608 | tf_op jit(solution)/shard_map/ppermute | solution.py:466
  560.0 13.2 %collective-permute-start.37 = (bf16[128,1024]{0,1:T(8,128)(2,1)S(1)}, bf16[128,1024]{0,1:T(8,128)(2,1)S(1)}, u32[]{:S(2)}, u32[]{:S(2)}) collective-permute-start(bf16[128,1024]{0,1:T(8,128)(2,1)S(1)} %fusion.15), channel_id=1, source_target_pairs={{0,16},{16,0},{1,17},{17,1},{2,18},{18,2},{3,19},{19,3},{4,20},{20... | collective-permute-start | bytes 786440 | tf_op jit(solution)/shard_map/ppermute | solution.py:466
  (73 other events, 356.4 us)

commit v3 on v2

--- a/solution.py
+++ b/solution.py
@@ -781,10 +781,10 @@
     )(where, rows, grads, up_weight, down_weight)
 
 
-def assemble(first, second, qkv_out, out_out, gain_out):
+def assemble(first, second, qkv_out, out_out, beside_out, gain_out):
     f32 = jnp.float32
     for pair in range(8):
-        for source, rows, at in ((first, 384, 0), (second, 128, 384)):
+        for source, rows, at in ((first, 400, 0), (second, 112, 400)):
             left = source[2 * pair, :rows, :].astype(f32)
             right = source[2 * pair + 1, :rows, :].astype(f32)
             here = slice(at, at + rows)
@@ -799,9 +799,10 @@
         at = bits[0] * 256 + bits[1] * 128 + bits[2] * 64 + bits[3] * 32
         for part in range(8):
             out_out[at : at + 32, part * 128 : (part + 1) * 128] = second[
-                device, 128 + part * 32 : 160 + part * 32, :
+                device, 112 + part * 32 : 144 + part * 32, :
             ].astype(f32)
-        total = total + second[device, 384:400, :].astype(f32)
+        beside_out[at : at + 32, :] = second[device, 368:400, :].astype(f32)
+        total = total + second[device, 400:416, :].astype(f32)
     gain_out[...] = total[:8, :] + total[8:, :]
 
 
@@ -846,10 +847,10 @@
 
     (
         h_one, block_order, segment_ids, query_key_value_weight, w_out, ffn_gain, w_router,
-        routes, cotangent,
+        expert_in, expert_out,
     ) = together(
         h_one, block_order, segment_ids, query_key_value_weight, w_out, ffn_gain, w_router,
-        routes, cotangent,
+        expert_in, expert_out,
     )
     both = gather_step(spread(h_one), "a")
 
@@ -1062,12 +1063,22 @@
     grad_heads = to_tokens(attended_gradient.reshape(rows, 16, 64).transpose(1, 0, 2))
     grad_heads = grad_heads.reshape(length, 64)
 
+    grad_router_part = lax.dot_general(
+        h_two.astype(f32), grad_logits, (((0,), (0,)), ((), ())), precision=HIGHEST
+    )
+    grad_gain_two = jnp.sum(grad_h_two * norm_two, axis=0)
+    beside = jnp.concatenate(
+        [grad_router_part, grad_gain_two[:, None], jnp.zeros((width, 128 - E - 1), f32)], 1
+    ).reshape(2, 2, 256, 128)
     by_core = attended.reshape(rows, 2, 2, 256)
-    keep = lax.dynamic_slice_in_dim(by_core, idd, 1, 2).reshape(rows, 512)
-    send = lax.dynamic_slice_in_dim(by_core, 1 - idd, 1, 2).reshape(rows, 512)
-    out_sum = contract_rows(keep, grad_branch) + swap(
-        contract_rows(send, grad_branch).astype(bf16), "d"
-    ).astype(f32)
+
+    def rows_at(core):
+        columns = lax.dynamic_slice_in_dim(by_core, core, 1, 2).reshape(rows, 512)
+        others = lax.dynamic_slice_in_dim(beside, core, 1, 1).reshape(512, 128)
+        return jnp.concatenate([contract_rows(columns, grad_branch), others], 1)
+
+    out_sum = rows_at(idd)
+    leaving = rows_at(1 - idd).astype(bf16)
 
     def halve(total, axis):
         count = total.shape[0] // 2
@@ -1076,13 +1087,11 @@
         send = lax.dynamic_slice_in_dim(total, (1 - index) * count, count, 0)
         return keep + swap(send.astype(bf16), axis).astype(f32)
 
-    grad_router_part = lax.dot_general(
-        grad_logits, h_two.astype(f32), (((0,), (0,)), ((), ())), precision=HIGHEST
-    )
-    grad_gain_two = jnp.sum(grad_h_two * norm_two, axis=0, keepdims=True)
-    small = jnp.concatenate([grad_router_part, jnp.broadcast_to(grad_gain_two, (8, width))], 0)
-    grad_heads, expert_grads = together(grad_heads, expert_grads)
-    expert_grads = lax.all_to_all(expert_grads, CTX, split_axis=0, concat_axis=0, tiled=True)
+    results = jnp.concatenate(
+        [result_mine.reshape(16, MOST, width), result_other.reshape(16, MOST, width)], 1
+    )
+    grad_heads, results = together(grad_heads, results)
+    results = exchange(results)
 
     keep, send = whole_call(
         attention_backward,
@@ -1098,16 +1107,15 @@
         place, first_key, idd.astype(jnp.int32)[None], query, key, value, mixed, grad_heads,
         fine, coarse, start,
     )
-    keep, send, out_sum, small = together(keep, send, out_sum, small)
+    keep, send, out_sum, leaving = together(keep, send, out_sum, leaving)
+    out_sum = out_sum + swap(leaving, "d").astype(f32)
     grad_columns = (keep + swap(send, "d").astype(f32)).astype(bf16)
     out_sum = halve(out_sum, "f")
-    small = small + swap(small, "d")
-    small = small + swap(small, "f")
-    ready, expert_grads, out_sum = together(grad_columns, expert_grads, out_sum)
-    grad_projected = to_tokens(ready)
+    results, expert_grads = together(results, expert_grads)
+    expert_grads = lax.all_to_all(expert_grads, CTX, split_axis=0, concat_axis=0, tiled=True)
     for axis in ("c", "b", "a"):
         out_sum = halve(out_sum, axis)
-    out_rows = out_sum.reshape(32, 8, 128).transpose(1, 0, 2).reshape(256, 128).astype(bf16)
+    out_rows = out_sum.reshape(32, 9, 128).transpose(1, 0, 2).reshape(288, 128).astype(bf16)
 
     by_core = grad_columns.reshape(8, 2, rows, 128)
     own = jnp.where(idd == 0, by_core[:, 0], by_core[:, 1]).reshape(length // 2, 128)
@@ -1126,23 +1134,17 @@
         [columns_grad.astype(bf16), out_rows] + two_parts(gain_part), 0
     )
     gathered = gather_step(spread(columns_grad), "a")
-    first = gather_step(gathered[..., :384, :], "b")
-    second = gather_step(gathered[..., 384:, :], "c")
+    first = gather_step(gathered[..., :400, :], "b")
+    second = gather_step(gathered[..., 400:, :], "c")
     first = gather_step(first, "c")
     second = gather_step(second, "b")
-    results = jnp.concatenate(
-        [result_mine.reshape(16, MOST, width), result_other.reshape(16, MOST, width)], 1
-    )
+    ready, expert_grads = together(grad_columns, expert_grads)
+    grad_projected = to_tokens(ready)
     grad_expert_in = expert_grads[:, :64].astype(f32)
     grad_expert_out = expert_grads[:, 64:].astype(f32)
-    grad_projected, results, small, grad_expert_in, grad_expert_out, first, second = together(
-        grad_projected, results, small, grad_expert_in, grad_expert_out, first, second
-    )
-    results = exchange(results)
+    first, second, grad_projected = together(first, second, grad_projected)
     first = gather_step(first, "d")
     second = gather_step(second, "d")
-    for axis in ("c", "b", "a"):
-        small = small + swap(small, axis)
 
     grad_projected = grad_projected.transpose(1, 0, 2)
     grad_kv = grad_projected[:, :, 64:].reshape(rows, 8, 2, 64)
@@ -1159,20 +1161,20 @@
     grad_inputs = grad_mid + scale_one * (
         scaled_one - norm_one * jnp.mean(scaled_one * norm_one, axis=-1, keepdims=True)
     )
-    small = jnp.where(low_half, small[:, :512], small[:, 512:])
-    share_router = small[:E].T
-    share_two = small[E]
-    share_qkv, share_out, gain_sum = whole_call(
+    share_qkv, share_out, beside, gain_sum = whole_call(
         assemble,
         0,
         [
             jax.ShapeDtypeStruct((512, 2048), f32),
             jax.ShapeDtypeStruct((512, 1024), f32),
+            jax.ShapeDtypeStruct((512, 128), f32),
             jax.ShapeDtypeStruct((8, 128), f32),
         ],
         [],
         32 << 20,
-    )(first.reshape(16, 384, 128), second.reshape(16, 400, 128))
+    )(first.reshape(16, 400, 128), second.reshape(16, 416, 128))
+    share_router = beside[:, :E]
+    share_two = beside[:, E]
     share_one = gain_sum[:4].reshape(512) / attn_gain.astype(f32)
     mixture = sum_rows(pick_mine, results[:, :MOST]) + swap(
         sum_rows(pick_other, results[:, MOST:]).astype(bf16), "a"

time: 587 us -> 556 us (0.947)
  waiting for transfers between devices: 236 us -> 218 us
  blocking collectives: 68.5 us -> 53.2 us
  starting transfers between devices: 95.4 us -> 84.9 us
  other arithmetic: 51.1 us -> 60.7 us
    all_to_all x1, waiting for transfers between devices: 20 us -> 0.01 us  [fast_shards(): lax.all_to_all(expert_grads, CTX, split_axis=0, concat_axis=0, tiled=True)]
    ppermute x43 -> x38, starting transfers between devices: 57.1 us -> 38.5 us  [swap(): return lax.ppermute(value, axis, [(0, 1), (1, 0)])]
    all_to_all x2 -> x1, blocking collectives: 40.4 us -> 25.2 us  [to_tokens(): lax.all_to_all(value_heads.reshape(16, rows, -1), CTX, split_axis=0, conc...]
    all_to_all x1 -> x2, waiting for transfers between devices: 0.01 us -> 7.11 us  [to_tokens(): lax.all_to_all(value_heads.reshape(16, rows, -1), CTX, split_axis=0, conc...]
    concatenate x0 -> x5, local copies, waits for them, and re-layouts: none -> 6.57 us  [fast_shards(): jnp.concatenate([grad_router_part, grad_gain_two[:, None], jnp.zeros((wid...]
    all_to_all x1 -> x2, starting transfers between devices: 4.05 us -> 10.3 us  [to_tokens(): lax.all_to_all(value_heads.reshape(16, rows, -1), CTX, split_axis=0, conc...]
    ppermute x43 -> x38, waiting for transfers between devices: 162 us -> 157 us  [swap(): return lax.ppermute(value, axis, [(0, 1), (1, 0)])]
    unnamed x175 -> x174, local copies, waits for them, and re-layouts: 18.4 us -> 18 us
  transfers between devices with their start and end apart: 51 -> 47, of which waited for: 27 -> 24; matrix products, arithmetic and copies ran while one was open for 17% -> 21% of each run, Pallas kernels for 7% -> 6%
where the time goes in v3:
time: 556 us; the launch traced here: 546 us
  waiting for transfers between devices  218 us (39%)
  starting transfers between devices  84.9 us (15%)
  other arithmetic  60.7 us (11%)
  blocking collectives  53.2 us (10%)
  Pallas kernels  46.9 us (8%)
  matrix products  42.6 us (8%)
  local copies, waits for them, and re-layouts  37 us (7%)
    ppermute x38, waiting for transfers between devices, swap(): return lax.ppermute(value, axis, [(0, 1), (1, 0)])  157 us
    ppermute x38, starting transfers between devices, swap(): return lax.ppermute(value, axis, [(0, 1), (1, 0)])  38.5 us
    all_to_all x5, waiting for transfers between devices, exchange(): return lax.all_to_all(sent, HALF, split_axis=0, concat_axis=0, tiled=True)  31.4 us
    pallas_call x3, Pallas kernels, run(): pl.pallas_call(kernel, out_shape=outs, grid_spec=pltpu.PrefetchScalarGrid...  28.5 us
    all_to_all x1, blocking collectives, exchange(): return lax.all_to_all(sent, HALF, split_axis=0, concat_axis=0, tiled=True)  28 us
    all_to_all x1, blocking collectives, to_tokens(): lax.all_to_all(value_heads.reshape(16, rows, -1), CTX, split_axis=0, conc...  25.2 us
    all_to_all x5, starting transfers between devices, exchange(): return lax.all_to_all(sent, HALF, split_axis=0, concat_axis=0, tiled=True)  25.1 us
    all_to_all x1, waiting for transfers between devices, fast_shards(): lax.all_to_all(expert_weights, CTX, split_axis=0, concat_axis=0, tiled=True)  22.3 us
  transfers between devices with their start and end apart: 47, of which 24 were waited for; matrix products, arithmetic and copies ran while one was open for 21% of the time, Pallas kernels for 6%

profile of v3, /device:TPU:0, one launch (start us, length us, event | category | flops | bytes accessed | tf_op | source)
XLA Modules:
  0.0 545.9 jit_solution(18158464588652169633)
XLA Ops:
  0.7 3.0 collective-permute-start
  5.2 2.7 collective-permute-start.2
  11.0 3.7 pad_maximum_fusion
  14.7 9.9 %collective-permute-done.1 = bf16[1,1,1,1,128,1024]{4,5,3,2,1,0:T(8,128)(2,1)S(1)} collective-permute-done((bf16[1,1,1,1,128,1024]{4,5,3,2,1,0:T(8,128)(2,1)S(1)}, bf16[1,1,1,1,128,1024]{4,5,3,2,1,0:T(8,128)(2,1)S(1)}, u32[]{:S(2)}, u32[]{:S(2)}) %collective-permute-start.1) | collective-permute-done | bytes 262176 | tf_op jit(solution)/shard_map/ppermute | solution.py:466
  26.3 2.2 broadcast_select_fusion.3
  29.8 2.2 collective-permute-done.6
  32.2 3.2 collective-permute-done.3
  41.1 2.6 collective-permute-start.9
  43.7 10.6 %collective-permute-done.11 = f32[2,1,2,1,1,32]{5,4,3,2,1,0:T(1,128)S(1)} collective-permute-done((f32[2,1,2,1,1,32]{5,4,3,2,1,0:T(1,128)S(1)}, f32[2,1,2,1,1,32]{5,4,3,2,1,0:T(1,128)S(1)}, u32[]{:S(2)}, u32[]{:S(2)}) %collective-permute-start.11) | collective-permute-done | bytes 544 | tf_op jit(solution)/shard_map/ppermute | solution.py:466
  57.5 2.3 maximum_select_fusion.6
  60.6 4.5 all-to-all-start
  77.8 2.1 pad_maximum_fusion.1
  81.7 2.3 maximum_select_fusion.1
  84.1 13.4 %shard_map.187 = (bf16[2048,128]{1,0:T(8,128)(2,1)S(1)}, bf16[2048,128]{1,0:T(8,128)(2,1)S(1)}, bf16[2048,128]{1,0:T(8,128)(2,1)S(1)}, f32[72,2048]{1,0:T(8,128)S(1)}, bf16[2048,64]{1,0:T(8,128)(2,1)S(1)}) custom-call(s32[32]{0:T(128)S(1)} %select_reduce_fusion.2.place, s32[32]{0:T(128)S(1)} %select_reduce_fusion.1.h_place, s32[8]{0:T(128)S(1)} %and_select_fusion.first_key, ...), custom_call_target="tpu_custom_call" | custom-call | tf_op jit(solution)/shard_map/pallas_call | solution.py:812
  102.1 22.3 %all-to-all-done = bf16[16,96,1024]{2,1,0:T(8,128)(2,1)} async-done(((bf16[16,96,1024]{2,1,0:T(8,128)(2,1)}), bf16[16,96,1024]{2,1,0:T(8,128)(2,1)}, u32[]{:S(2)}, u32[]{:S(2)}) %all-to-all-start) | async-done | bytes 3145760 | tf_op jit(solution)/shard_map/all_to_all | solution.py:918
  124.7 25.2 %all_to_all.55 = bf16[16,128,64]{1,2,0:T(8,128)(2,1)S(1)} all-to-all(bf16[16,128,64]{1,2,0:T(8,128)(2,1)S(1)} %copy.104), channel_id=1, replica_groups=mesh['a'=2,'b'=2,'c'=2,'d'=2,'f'=2] {'a','b','c','d'}, dimensions={0} | all-to-all | bytes 524288 | tf_op jit(solution)/shard_map/all_to_all | solution.py:969
  149.8 4.7 all-to-all-start.2
  156.0 2.6 multiply_reduce_fusion.2
  162.1 2.0 convolution_convert_fusion.1
  164.2 2.5 maximum_select_fusion.2
  166.7 3.6 maximum_select_fusion
  170.4 28.3 %collective-permute-done.21 = bf16[128,1152]{0,1:T(8,128)(2,1)S(1)} collective-permute-done((bf16[128,1152]{0,1:T(8,128)(2,1)S(1)}, bf16[128,1152]{0,1:T(8,128)(2,1)S(1)}, u32[]{:S(2)}, u32[]{:S(2)}) %collective-permute-start.21) | collective-permute-done | bytes 294944 | tf_op jit(solution)/shard_map/ppermute | solution.py:466
  200.5 5.7 %all-to-all-start.3 = ((bf16[16,48,1152]{2,1,0:T(8,128)(2,1)}), bf16[16,48,1152]{2,1,0:T(8,128)(2,1)}, u32[]{:S(2)}, u32[]{:S(2)}) async-start(bf16[16,48,1152]{2,1,0:T(8,128)(2,1)} %convolution_convert_fusion.1), calls=%async_computation.3 | async-start | bytes 3538944 | tf_op jit(solution)/shard_map/all_to_all | solution.py:902
  206.2 3.1 slice.136
  212.6 17.0 %all-to-all-done.3 = bf16[16,48,1152]{2,1,0:T(8,128)(2,1)} async-done(((bf16[16,48,1152]{2,1,0:T(8,128)(2,1)}), bf16[16,48,1152]{2,1,0:T(8,128)(2,1)}, u32[]{:S(2)}, u32[]{:S(2)}) %all-to-all-start.3) | async-done | bytes 1769504 | tf_op jit(solution)/shard_map/all_to_all | solution.py:902
  229.6 4.8 all-to-all-start.4
  234.5 9.2 %shard_map.188 = (bf16[768,1152]{1,0:T(8,128)(2,1)}, bf16[768,1024]{1,0:T(8,128)(2,1)S(1)}, bf16[768,512]{1,0:T(8,128)(2,1)S(1)}, bf16[768,1024]{1,0:T(8,128)(2,1)S(1)}, bf16[768,1024]{1,0:T(8,128)(2,1)}) custom-call(s32[1]{0:T(128)} %bitcast.26.where, bf16[768,1152]{1,0:T(8,128)(2,1)} %bitcast.31.rows, bf16[16,2,48,1024]{3,2,1,0:T(8,128)(2,1)} %bitcast.32.grad, ...), custom_call_target="tpu_custom_call" | custom-call | tf_op jit(solution)/shard_map/pallas_call | solution.py:766
  246.8 11.5 %all-to-all-done.4 = bf16[16,48,1152]{2,1,0:T(8,128)(2,1)} async-done(((bf16[16,48,1152]{2,1,0:T(8,128)(2,1)}), bf16[16,48,1152]{2,1,0:T(8,128)(2,1)}, u32[]{:S(2)}, u32[]{:S(2)}) %all-to-all-start.4) | async-done | bytes 1769504 | tf_op jit(solution)/shard_map/all_to_all | solution.py:902
  258.4 9.1 %shard_map.189 = (bf16[768,1152]{1,0:T(8,128)(2,1)}, bf16[768,1024]{1,0:T(8,128)(2,1)S(1)}, bf16[768,512]{1,0:T(8,128)(2,1)S(1)}, bf16[768,1024]{1,0:T(8,128)(2,1)S(1)}, bf16[768,1024]{1,0:T(8,128)(2,1)}) custom-call(s32[1]{0:T(128)} %bitcast.26.where, bf16[768,1152]{1,0:T(8,128)(2,1)} %bitcast.33.rows, bf16[16,2,48,1024]{3,2,1,0:T(8,128)(2,1)} %bitcast.32.grad, ...), custom_call_target="tpu_custom_call" | custom-call | tf_op jit(solution)/shard_map/pallas_call | solution.py:766
  270.7 28.0 %all_to_all.56 = bf16[16,48,1152]{2,1,0:T(8,128)(2,1)} all-to-all(bf16[16,48,1152]{2,1,0:T(8,128)(2,1)} %bitcast.195), channel_id=1, replica_groups=mesh['a'=2,'b'=2,'c'=2,'d'=2,'f'=2] {'b','c','d','f'}, dimensions={0} | all-to-all | bytes 3538944 | tf_op jit(solution)/shard_map/all_to_all | solution.py:902
  298.8 4.9 all-to-all-start.6
  303.7 2.5 fusion.90
  306.3 3.4 fusion.3
  309.8 3.5 add_convert_fusion
  316.4 2.0 pad_maximum_fusion.2
  318.5 13.7 %collective-permute-done.22 = bf16[128,1152]{0,1:T(8,128)(2,1)} collective-permute-done((bf16[128,1152]{0,1:T(8,128)(2,1)S(1)}, bf16[128,1152]{0,1:T(8,128)(2,1)}, u32[]{:S(2)}, u32[]{:S(2)}) %collective-permute-start.22) | collective-permute-done | bytes 294944 | tf_op jit(solution)/shard_map/ppermute | solution.py:466
  333.2 2.3 fusion
  335.6 2.2 multiply_reduce_fusion
  341.5 5.4 all-to-all-start.7
  346.9 4.0 pad_maximum_fusion.3
  350.9 6.1 %all-to-all-done.7 = bf16[16,128,64]{1,2,0:T(8,128)(2,1)S(1)} async-done(((bf16[16,128,64]{1,2,0:T(8,128)(2,1)}), bf16[16,128,64]{1,2,0:T(8,128)(2,1)S(1)}, u32[]{:S(2)}, u32[]{:S(2)}) %all-to-all-start.7) | async-done | bytes 262176 | tf_op jit(solution)/shard_map/all_to_all | solution.py:969
  357.3 4.8 all-to-all-start.8
  377.3 11.6 %shard_map.190 = (f32[2048,128]{1,0:T(8,128)S(1)}, bf16[2048,128]{1,0:T(8,128)(2,1)S(1)}) custom-call(s32[32]{0:T(128)S(1)} %select_reduce_fusion.2.place, s32[8]{0:T(128)S(1)} %and_select_fusion.first_key, s32[1]{0:T(128)} %bitcast.48.core, bf16[2048,128]{1,0:T(8,128)(2,1)S(1)} %copy-done.10, bf16[2048,128]{1,0:T(8,128)(2,1)S(1)} %copy-done.12, ...), custom_call_target="tpu_custom_call" | custom-call | tf_op jit(solution)/shard_map/pallas_call | solution.py:812
  390.4 3.1 collective-permute-done.24
  394.9 2.4 convert_add_fusion
  398.2 3.1 collective-permute-start.27
  402.1 6.5 %all-to-all-start.9 = ((bf16[16,96,1024]{2,1,0:T(8,128)(2,1)}), bf16[16,96,1024]{2,1,0:T(8,128)(2,1)}, u32[]{:S(2)}, u32[]{:S(2)}) async-start(bf16[16,96,1024]{2,1,0:T(8,128)(2,1)} %pad_maximum_fusion.2), calls=%async_computation.9 | async-start | bytes 6291456 | tf_op jit(solution)/shard_map/all_to_all | solution.py:1115
  411.7 6.1 %collective-permute-done.27 = bf16[256,1152]{1,0:T(8,128)(2,1)} collective-permute-done((bf16[256,1152]{1,0:T(8,128)(2,1)}, bf16[256,1152]{1,0:T(8,128)(2,1)}, u32[]{:S(2)}, u32[]{:S(2)}) %collective-permute-start.27) | collective-permute-done | bytes 589856 | tf_op jit(solution)/shard_map/ppermute | solution.py:466
  420.8 20.4 %collective-permute-done.28 = bf16[128,1152]{1,0:T(8,128)(2,1)S(1)} collective-permute-done((bf16[128,1152]{1,0:T(8,128)(2,1)S(1)}, bf16[128,1152]{1,0:T(8,128)(2,1)S(1)}, u32[]{:S(2)}, u32[]{:S(2)}) %collective-permute-start.28) | collective-permute-done | bytes 294944 | tf_op jit(solution)/shard_map/ppermute | solution.py:466
  441.7 21.9 %collective-permute-done.29 = bf16[64,1152]{1,0:T(8,128)(2,1)S(1)} collective-permute-done((bf16[64,1152]{1,0:T(8,128)(2,1)S(1)}, bf16[64,1152]{1,0:T(8,128)(2,1)S(1)}, u32[]{:S(2)}, u32[]{:S(2)}) %collective-permute-start.29) | collective-permute-done | bytes 147488 | tf_op jit(solution)/shard_map/ppermute | solution.py:466
  463.7 4.6 collective-permute-start.30
  468.2 15.1 %collective-permute-done.30 = bf16[32,1152]{1,0:T(8,128)(2,1)S(1)} collective-permute-done((bf16[32,1152]{1,0:T(8,128)(2,1)S(1)}, bf16[32,1152]{1,0:T(8,128)(2,1)S(1)}, u32[]{:S(2)}, u32[]{:S(2)}) %collective-permute-start.30) | collective-permute-done | bytes 73760 | tf_op jit(solution)/shard_map/ppermute | solution.py:466
  483.6 10.9 %collective-permute-done.31 = bf16[1,1,1,1,816,128]{5,4,3,2,1,0:T(8,128)(2,1)S(1)} collective-permute-done((bf16[1,1,1,1,816,128]{5,4,3,2,1,0:T(8,128)(2,1)S(1)}, bf16[1,1,1,1,816,128]{5,4,3,2,1,0:T(8,128)(2,1)S(1)}, u32[]{:S(2)}, u32[]{:S(2)}) %collective-permute-start.31) | collective-permute-done | bytes 208928 | tf_op jit(solution)/shard_map/ppermute | solution.py:466
  496.2 5.5 %collective-permute-done.32 = bf16[2,1,1,1,400,128]{5,4,0,3,2,1:T(8,128)(2,1)S(1)} collective-permute-done((bf16[2,1,1,1,400,128]{5,4,0,3,2,1:T(8,128)(2,1)S(1)}, bf16[2,1,1,1,400,128]{5,4,0,3,2,1:T(8,128)(2,1)S(1)}, u32[]{:S(2)}, u32[]{:S(2)}) %collective-permute-start.32) | collective-permute-done | bytes 204832 | tf_op jit(solution)/shard_map/ppermute | solution.py:466
  504.7 2.9 fusion.15
  507.6 2.6 collective-permute-start.23
  510.2 2.2 collective-permute-done.33
  513.5 4.9 all-to-all-start.10
  518.4 2.3 collective-permute-done.35
  522.0 2.1 fusion.37
  524.9 2.8 slice_convert_fusion.1
  527.7 4.1 slice_convert_fusion
  533.5 3.5 fusion.22
  540.0 3.6 shard_map.191
  (355 shorter events, 101.7 us)
Async XLA Ops:
  0.6 10.3 %copy-start.47 = (bf16[16,32,1024]{2,1,0:T(8,128)(2,1)S(1)}, bf16[16,32,1024]{2,1,0:T(8,128)(2,1)}, u32[]{:S(2)}) copy-start(bf16[16,32,1024]{2,1,0:T(8,128)(2,1)} %param.23) | copy-start | bytes 3145732
  0.7 8.6 %collective-permute-start = (bf16[512]{0:T(512)(128)(2,1)}, bf16[512]{0:T(512)(128)(2,1)S(1)}, u32[]{:S(2)}, u32[]{:S(2)}) collective-permute-start(bf16[512]{0:T(512)(128)(2,1)} %param.16), channel_id=1, source_target_pairs={{0,1},{1,0},{2,3},{3,2},{4,5},{5,4},{6,7},{7,6},{8,9},{9,8},{10,11... | collective-permute-start | bytes 3080 | tf_op jit(solution)/shard_map/ppermute | solution.py:466
  5.2 5.7 %collective-permute-start.2 = (f32[1,1,1,1,1,32]{5,4,3,2,1,0:T(1,128)S(1)}, f32[1,1,1,1,1,32]{5,4,3,2,1,0:T(1,128)S(1)}, u32[]{:S(2)}, u32[]{:S(2)}) collective-permute-start(f32[1,1,1,1,1,32]{5,4,3,2,1,0:T(1,128)S(1)} %bitcast.223), channel_id=1, source_target_pairs={{0,16},{16,0},{1,17},{17,1},{2,18},{18,2},{3,19},{19,3},{4,20},{20... | collective-permute-start | bytes 392 | tf_op jit(solution)/shard_map/ppermute | solution.py:466
  10.6 14.0 %collective-permute-start.1 = (bf16[1,1,1,1,128,1024]{4,5,3,2,1,0:T(8,128)(2,1)S(1)}, bf16[1,1,1,1,128,1024]{4,5,3,2,1,0:T(8,128)(2,1)S(1)}, u32[]{:S(2)}, u32[]{:S(2)}) collective-permute-start(bf16[1,1,1,1,128,1024]{4,5,3,2,1,0:T(8,128)(2,1)S(1)} %bitcast.198), channel_id=1, source_target_pairs={{0,16},{16,0},{1,17},{17,1},{2,18},{18,2},{3,19},{19,3},{4,20},{20... | collective-permute-start | bytes 786440 | tf_op jit(solution)/shard_map/ppermute | solution.py:466
  24.7 14.5 %copy-start.36 = (bf16[512,1024]{1,0:T(8,128)(2,1)S(1)}, bf16[512,1024]{1,0:T(8,128)(2,1)}, u32[]{:S(2)}) copy-start(bf16[512,1024]{1,0:T(8,128)(2,1)} %param.18) | copy-start | bytes 3145732
  24.7 7.3 %collective-permute-start.4 = (bf16[2,1,1,1,128,512]{4,5,3,2,1,0:T(8,128)(2,1)S(1)}, bf16[2,1,1,1,128,512]{4,5,3,2,1,0:T(8,128)(2,1)S(1)}, u32[]{:S(2)}, u32[]{:S(2)}) collective-permute-start(bf16[2,1,1,1,128,512]{4,5,3,2,1,0:T(8,128)(2,1)S(1)} %get-tuple-element.226), channel_id=1, source_target_pairs={{0,4},{4,0},{1,5},{5,1},{2,6},{6,2},{3,7},{7,3},{8,12},{12,8},{9,1... | collective-permute-start | bytes 786440 | tf_op jit(solution)/shard_map/ppermute | solution.py:466
  28.5 43.1 %copy-start.43 = (bf16[512,64]{1,0:T(8,128)(2,1)}, bf16[512,64]{1,0:T(8,128)(2,1)S(1)}, u32[]{:S(2)}) copy-start(bf16[512,64]{1,0:T(8,128)(2,1)S(1)} %get-tuple-element.221) | copy-start | bytes 196612
  28.5 6.9 %collective-permute-start.3 = (bf16[2,1,1,1,128,512]{4,5,3,2,1,0:T(8,128)(2,1)S(1)}, bf16[2,1,1,1,128,512]{4,5,3,2,1,0:T(8,128)(2,1)S(1)}, u32[]{:S(2)}, u32[]{:S(2)}) collective-permute-start(bf16[2,1,1,1,128,512]{4,5,3,2,1,0:T(8,128)(2,1)S(1)} %get-tuple-element.227), channel_id=1, source_target_pairs={{0,8},{8,0},{1,9},{9,1},{2,10},{10,2},{3,11},{11,3},{4,12},{12,4},... | collective-permute-start | bytes 786440 | tf_op jit(solution)/shard_map/ppermute | solution.py:466
  28.5 3.6 collective-permute-start.6
  29.0 11.8 %copy-start.45 = (bf16[1,128,1024]{2,1,0:T(8,128)(2,1)S(1)}, bf16[1,128,1024]{2,1,0:T(8,128)(2,1)}, u32[]{:S(2)}) copy-start(bf16[1,128,1024]{2,1,0:T(8,128)(2,1)} %param.15) | copy-start | bytes 786436
  29.2 6.7 %collective-permute-start.5 = (bf16[512,256]{1,0:T(8,128)(2,1)S(1)}, bf16[512,256]{1,0:T(8,128)(2,1)S(1)}, u32[]{:S(2)}, u32[]{:S(2)}) collective-permute-start(bf16[512,256]{1,0:T(8,128)(2,1)S(1)} %pad_maximum_fusion.8), channel_id=1, source_target_pairs={{0,1},{1,0},{2,3},{3,2},{4,5},{5,4},{6,7},{7,6},{8,9},{9,8},{10,11... | collective-permute-start | bytes 786440 | tf_op jit(solution)/shard_map/ppermute | solution.py:466
  35.9 20.2 %collective-permute-start.7 = (bf16[2,2,1,1,128,512]{4,5,3,2,1,0:T(8,128)(2,1)S(1)}, bf16[2,2,1,1,128,512]{4,5,3,2,1,0:T(8,128)(2,1)}, u32[]{:S(2)}, u32[]{:S(2)}) collective-permute-start(bf16[2,2,1,1,128,512]{4,5,3,2,1,0:T(8,128)(2,1)S(1)} %maximum_select_fusion.11), channel_id=1, source_target_pairs={{0,4},{4,0},{1,5},{5,1},{2,6},{6,2},{3,7},{7,3},{8,12},{12,8},{9,1... | collective-permute-start | bytes 1572872 | tf_op jit(solution)/shard_map/ppermute | solution.py:466
  37.4 20.1 %collective-permute-start.8 = (bf16[2,1,2,1,128,512]{4,5,3,2,1,0:T(8,128)(2,1)S(1)}, bf16[2,1,2,1,128,512]{4,5,3,2,1,0:T(8,128)(2,1)}, u32[]{:S(2)}, u32[]{:S(2)}) collective-permute-start(bf16[2,1,2,1,128,512]{4,5,3,2,1,0:T(8,128)(2,1)S(1)} %maximum_select_fusion.12), channel_id=1, source_target_pairs={{0,8},{8,0},{1,9},{9,1},{2,10},{10,2},{3,11},{11,3},{4,12},{12,4},... | collective-permute-start | bytes 1572872 | tf_op jit(solution)/shard_map/ppermute | solution.py:466
  40.1 20.5 %collective-permute-start.12 = (bf16[256,1024]{1,0:T(8,128)(2,1)}, bf16[256,1024]{1,0:T(8,128)(2,1)}, u32[]{:S(2)}, u32[]{:S(2)}) collective-permute-start(bf16[256,1024]{1,0:T(8,128)(2,1)} %slice_select_fusion.1), channel_id=1, source_target_pairs={{0,1},{1,0},{2,3},{3,2},{4,5},{5,4},{6,7},{7,6},{8,9},{9,8},{10,11... | collective-permute-start | bytes 1572872 | tf_op jit(solution)/shard_map/ppermute | solution.py:466
  40.6 13.7 %collective-permute-start.11 = (f32[2,1,2,1,1,32]{5,4,3,2,1,0:T(1,128)S(1)}, f32[2,1,2,1,1,32]{5,4,3,2,1,0:T(1,128)S(1)}, u32[]{:S(2)}, u32[]{:S(2)}) collective-permute-start(f32[2,1,2,1,1,32]{5,4,3,2,1,0:T(1,128)S(1)} %broadcast_select_fusion.7), channel_id=1, source_target_pairs={{0,8},{8,0},{1,9},{9,1},{2,10},{10,2},{3,11},{11,3},{4,12},{12,4},... | collective-permute-start | bytes 1544 | tf_op jit(solution)/shard_map/ppermute | solution.py:466
  41.1 18.8 %copy-start.46 = (bf16[1,128,1024]{1,2,0:T(8,128)(2,1)}, bf16[1,128,1024]{1,2,0:T(8,128)(2,1)S(1)}, u32[]{:S(2)}) copy-start(bf16[1,128,1024]{1,2,0:T(8,128)(2,1)S(1)} %copy.94) | copy-start | bytes 786436
  41.1 18.8 %collective-permute-start.9 = (bf16[128,1024]{0,1:T(8,128)(2,1)S(1)}, bf16[128,1024]{0,1:T(8,128)(2,1)S(1)}, u32[]{:S(2)}, u32[]{:S(2)}) collective-permute-start(bf16[128,1024]{0,1:T(8,128)(2,1)S(1)} %bitcast.197), channel_id=1, source_target_pairs={{0,16},{16,0},{1,17},{17,1},{2,18},{18,2},{3,19},{19,3},{4,20},{20... | collective-permute-start | bytes 786440 | tf_op jit(solution)/shard_map/ppermute | solution.py:466
  54.3 5.5 %collective-permute-start.10 = (f32[128,32]{0,1:T(8,128)S(1)}, f32[128,32]{0,1:T(8,128)S(1)}, u32[]{:S(2)}, u32[]{:S(2)}) collective-permute-start(f32[128,32]{0,1:T(8,128)S(1)} %get-tuple-element.107), channel_id=1, source_target_pairs={{0,16},{16,0},{1,17},{17,1},{2,18},{18,2},{3,19},{19,3},{4,20},{20... | collective-permute-start | bytes 49160 | tf_op jit(solution)/shard_map/ppermute | solution.py:466
  59.9 9.7 %copy-start.84 = (s32[1,32]{1,0:T(1,128)S(1)}, s32[1,32]{1,0:T(1,128)}, u32[]{:S(2)}) copy-start(s32[1,32]{1,0:T(1,128)} %param.13) | copy-start | bytes 388
  60.6 63.8 %all-to-all-start = ((bf16[16,96,1024]{2,1,0:T(8,128)(2,1)}), bf16[16,96,1024]{2,1,0:T(8,128)(2,1)}, u32[]{:S(2)}, u32[]{:S(2)}) async-start(bf16[16,96,1024]{2,1,0:T(8,128)(2,1)} %pad_maximum_fusion), calls=%async_computation | async-start | bytes 6291456 | tf_op jit(solution)/shard_map/all_to_all | solution.py:918
  67.5 7.2 %collective-permute-start.15 = (bf16[512]{0:T(512)(128)(2,1)}, bf16[512]{0:T(512)(128)(2,1)}, u32[]{:S(2)}, u32[]{:S(2)}) collective-permute-start(bf16[512]{0:T(512)(128)(2,1)} %param.19), channel_id=1, source_target_pairs={{0,1},{1,0},{2,3},{3,2},{4,5},{5,4},{6,7},{7,6},{8,9},{9,8},{10,11... | collective-permute-start | bytes 3080 | tf_op jit(solution)/shard_map/ppermute | solution.py:466
  68.1 6.6 %collective-permute-start.16 = (bf16[512,32]{0,1:T(8,128)(2,1)}, bf16[512,32]{0,1:T(8,128)(2,1)}, u32[]{:S(2)}, u32[]{:S(2)}) collective-permute-start(bf16[512,32]{0,1:T(8,128)(2,1)} %param.20), channel_id=1, source_target_pairs={{0,1},{1,0},{2,3},{3,2},{4,5},{5,4},{6,7},{7,6},{8,9},{9,8},{10,11... | collective-permute-start | bytes 98312 | tf_op jit(solution)/shard_map/ppermute | solution.py:466
  74.1 10.0 %collective-permute-start.13 = (bf16[1024,512]{1,0:T(8,128)(2,1)S(1)}, bf16[1024,512]{1,0:T(8,128)(2,1)S(1)}, u32[]{:S(2)}, u32[]{:S(2)}) collective-permute-start(bf16[1024,512]{1,0:T(8,128)(2,1)S(1)} %bitcast.166), channel_id=1, source_target_pairs={{0,2},{2,0},{1,3},{3,1},{4,6},{6,4},{5,7},{7,5},{8,10},{10,8},{9,1... | collective-permute-start | bytes 3145736 | tf_op jit(solution)/shard_map/ppermute | solution.py:466
  74.2 9.9 %collective-permute-start.14 = (bf16[1024,512]{1,0:T(8,128)(2,1)S(1)}, bf16[1024,512]{1,0:T(8,128)(2,1)S(1)}, u32[]{:S(2)}, u32[]{:S(2)}) collective-permute-start(bf16[1024,512]{1,0:T(8,128)(2,1)S(1)} %bitcast.163), channel_id=1, source_target_pairs={{0,2},{2,0},{1,3},{3,1},{4,6},{6,4},{5,7},{7,5},{8,10},{10,8},{9,1... | collective-permute-start | bytes 3145736 | tf_op jit(solution)/shard_map/ppermute | solution.py:466
  74.7 5.3 collective-permute-start.17
  76.4 25.7 %collective-permute-start.18 = (bf16[256,2048]{1,0:T(8,128)(2,1)S(1)}, bf16[256,2048]{1,0:T(8,128)(2,1)}, u32[]{:S(2)}, u32[]{:S(2)}) collective-permute-start(bf16[256,2048]{1,0:T(8,128)(2,1)S(1)} %slice_select_fusion), channel_id=1, source_target_pairs={{0,1},{1,0},{2,3},{3,2},{4,5},{5,4},{6,7},{7,6},{8,9},{9,8},{10,11... | collective-permute-start | bytes 3145736 | tf_op jit(solution)/shard_map/ppermute | solution.py:466
  77.0 2.9 collective-permute-start.19
  84.0 13.4 %copy-start.2 = (bf16[1024,512]{1,0:T(8,128)(2,1)}, bf16[1024,512]{1,0:T(8,128)(2,1)S(1)}, u32[]{:S(2)}) copy-start(bf16[1024,512]{1,0:T(8,128)(2,1)S(1)} %collective-permute-done.13.low_next) | copy-start | bytes 3145732
  84.1 13.4 %copy-start = (bf16[1024,512]{1,0:T(8,128)(2,1)}, bf16[1024,512]{1,0:T(8,128)(2,1)S(1)}, u32[]{:S(2)}) copy-start(bf16[1024,512]{1,0:T(8,128)(2,1)S(1)} %collective-permute-done.14.high_next) | copy-start | bytes 3145732
  149.8 50.7 %all-to-all-start.2 = ((bf16[16,96,1024]{2,1,0:T(8,128)(2,1)}), bf16[16,96,1024]{2,1,0:T(8,128)(2,1)}, u32[]{:S(2)}, u32[]{:S(2)}) async-start(bf16[16,96,1024]{2,1,0:T(8,128)(2,1)} %pad_maximum_fusion.1), calls=%async_computation.2 | async-start | bytes 6291456 | tf_op jit(solution)/shard_map/all_to_all | solution.py:902
  155.4 8.8 %collective-permute-start.20 = (bf16[256,2048]{1,0:T(8,128)(2,1)}, bf16[256,2048]{1,0:T(8,128)(2,1)S(1)}, u32[]{:S(2)}, u32[]{:S(2)}) collective-permute-start(bf16[256,2048]{1,0:T(8,128)(2,1)} %collective-permute-done.18), channel_id=1, source_target_pairs={{0,2},{2,0},{1,3},{3,1},{4,6},{6,4},{5,7},{7,5},{8,10},{10,8},{9,1... | collective-permute-start | bytes 3145736 | tf_op jit(solution)/shard_map/ppermute | solution.py:466
  161.0 37.7 %collective-permute-start.21 = (bf16[128,1152]{0,1:T(8,128)(2,1)S(1)}, bf16[128,1152]{0,1:T(8,128)(2,1)S(1)}, u32[]{:S(2)}, u32[]{:S(2)}) collective-permute-start(bf16[128,1152]{0,1:T(8,128)(2,1)S(1)} %maximum_maximum_fusion.1), channel_id=1, source_target_pairs={{0,16},{16,0},{1,17},{17,1},{2,18},{18,2},{3,19},{19,3},{4,20},{20... | collective-permute-start | bytes 884744 | tf_op jit(solution)/shard_map/ppermute | solution.py:466
  200.5 29.1 %all-to-all-start.3 = ((bf16[16,48,1152]{2,1,0:T(8,128)(2,1)}), bf16[16,48,1152]{2,1,0:T(8,128)(2,1)}, u32[]{:S(2)}, u32[]{:S(2)}) async-start(bf16[16,48,1152]{2,1,0:T(8,128)(2,1)} %convolution_convert_fusion.1), calls=%async_computation.3 | async-start | bytes 3538944 | tf_op jit(solution)/shard_map/all_to_all | solution.py:902
  229.6 28.8 %all-to-all-start.4 = ((bf16[16,48,1152]{2,1,0:T(8,128)(2,1)}), bf16[16,48,1152]{2,1,0:T(8,128)(2,1)}, u32[]{:S(2)}, u32[]{:S(2)}) async-start(bf16[16,48,1152]{2,1,0:T(8,128)(2,1)} %convolution_convert_fusion), calls=%async_computation.4 | async-start | bytes 3538944 | tf_op jit(solution)/shard_map/all_to_all | solution.py:902
  298.8 34.5 %all-to-all-start.6 = ((bf16[16,48,1152]{2,1,0:T(8,128)(2,1)}), bf16[16,48,1152]{2,1,0:T(8,128)(2,1)}, u32[]{:S(2)}, u32[]{:S(2)}) async-start(bf16[16,48,1152]{2,1,0:T(8,128)(2,1)} %bitcast.194), calls=%async_computation.6 | async-start | bytes 3538944 | tf_op jit(solution)/shard_map/all_to_all | solution.py:902
  314.1 18.1 %collective-permute-start.22 = (bf16[128,1152]{0,1:T(8,128)(2,1)S(1)}, bf16[128,1152]{0,1:T(8,128)(2,1)}, u32[]{:S(2)}, u32[]{:S(2)}) collective-permute-start(bf16[128,1152]{0,1:T(8,128)(2,1)S(1)} %fusion.1), channel_id=1, source_target_pairs={{0,16},{16,0},{1,17},{17,1},{2,18},{18,2},{3,19},{19,3},{4,20},{20... | collective-permute-start | bytes 884744 | tf_op jit(solution)/shard_map/ppermute | solution.py:466
  318.5 17.0 %copy-start.64 = (pred[128,32]{0,1:T(8,128)(4,1)S(1)}, pred[128,32]{0,1:T(8,128)(4,1)}, u32[]{:S(2)}) copy-start(pred[128,32]{0,1:T(8,128)(4,1)} %copy-done.63) | copy-start | bytes 12292
  318.5 17.1 %copy-start.66 = (f32[128]{0:T(128)S(1)}, f32[128]{0:T(128)}, u32[]{:S(2)}) copy-start(f32[128]{0:T(128)} %copy-done.65) | copy-start | bytes 1540
  318.5 17.1 %copy-start.69 = (f32[128]{0:T(128)S(1)}, f32[128]{0:T(128)}, u32[]{:S(2)}) copy-start(f32[128]{0:T(128)} %copy-done.68) | copy-start | bytes 1540
  318.5 17.1 %copy-start.24 = (f32[128,1024]{0,1:T(8,128)S(1)}, f32[128,1024]{0,1:T(8,128)}, u32[]{:S(2)}) copy-start(f32[128,1024]{0,1:T(8,128)} %copy-done.23) | copy-start | bytes 1572868
  341.5 15.5 %all-to-all-start.7 = ((bf16[16,128,64]{1,2,0:T(8,128)(2,1)}), bf16[16,128,64]{1,2,0:T(8,128)(2,1)S(1)}, u32[]{:S(2)}, u32[]{:S(2)}) async-start(bf16[16,128,64]{1,2,0:T(8,128)(2,1)} %bitcast.41), calls=%async_computation.7 | async-start | bytes 524288 | tf_op jit(solution)/shard_map/all_to_all | solution.py:969
  357.3 44.8 %all-to-all-start.8 = ((bf16[16,96,1024]{2,1,0:T(8,128)(2,1)}), bf16[16,96,1024]{2,1,0:T(8,128)(2,1)}, u32[]{:S(2)}, u32[]{:S(2)}) async-start(bf16[16,96,1024]{2,1,0:T(8,128)(2,1)} %pad_maximum_fusion.3), calls=%async_computation.8 | async-start | bytes 6291456 | tf_op jit(solution)/shard_map/all_to_all | solution.py:902
  364.1 8.8 %copy-start.27 = (f32[128,1024]{0,1:T(8,128)S(1)}, f32[128,1024]{0,1:T(8,128)}, u32[]{:S(2)}) copy-start(f32[128,1024]{0,1:T(8,128)} %copy-done.26) | copy-start | bytes 1572868
  389.9 5.0 collective-permute-start.26
  390.3 3.2 collective-permute-start.24
  398.2 19.6 %collective-permute-start.27 = (bf16[256,1152]{1,0:T(8,128)(2,1)}, bf16[256,1152]{1,0:T(8,128)(2,1)}, u32[]{:S(2)}, u32[]{:S(2)}) collective-permute-start(bf16[256,1152]{1,0:T(8,128)(2,1)} %dynamic-slice_convert_fusion), channel_id=1, source_target_pairs={{0,1},{1,0},{2,3},{3,2},{4,5},{5,4},{6,7},{7,6},{8,9},{9,8},{10,11... | collective-permute-start | bytes 1769480 | tf_op jit(solution)/shard_map/ppermute | solution.py:466
  402.1 110.4 %all-to-all-start.9 = ((bf16[16,96,1024]{2,1,0:T(8,128)(2,1)}), bf16[16,96,1024]{2,1,0:T(8,128)(2,1)}, u32[]{:S(2)}, u32[]{:S(2)}) async-start(bf16[16,96,1024]{2,1,0:T(8,128)(2,1)} %pad_maximum_fusion.2), calls=%async_computation.9 | async-start | bytes 6291456 | tf_op jit(solution)/shard_map/all_to_all | solution.py:1115
  408.7 9.1 %copy-start.31 = (f32[512,1152]{1,0:T(8,128)S(1)}, f32[512,1152]{1,0:T(8,128)}, u32[]{:S(2)}) copy-start(f32[512,1152]{1,0:T(8,128)} %copy-done.30) | copy-start | bytes 7077892
  419.0 22.2 %collective-permute-start.28 = (bf16[128,1152]{1,0:T(8,128)(2,1)S(1)}, bf16[128,1152]{1,0:T(8,128)(2,1)S(1)}, u32[]{:S(2)}, u32[]{:S(2)}) collective-permute-start(bf16[128,1152]{1,0:T(8,128)(2,1)S(1)} %dynamic-slice_convert_fusion.1), channel_id=1, source_target_pairs={{0,4},{4,0},{1,5},{5,1},{2,6},{6,2},{3,7},{7,3},{8,12},{12,8},{9,1... | collective-permute-start | bytes 884744 | tf_op jit(solution)/shard_map/ppermute | solution.py:466
  419.6 21.9 %copy-start.44 = (bf16[512,64]{1,0:T(8,128)(2,1)S(1)}, bf16[512,64]{1,0:T(8,128)(2,1)}, u32[]{:S(2)}) copy-start(bf16[512,64]{1,0:T(8,128)(2,1)} %copy-done.43) | copy-start | bytes 196612
  419.6 21.9 %copy-start.48 = (bf16[512,64]{1,0:T(8,128)(2,1)S(1)}, bf16[512,64]{1,0:T(8,128)(2,1)}, u32[]{:S(2)}) copy-start(bf16[512,64]{1,0:T(8,128)(2,1)} %get-tuple-element.214) | copy-start | bytes 196612
  420.1 21.3 %collective-permute-start.25 = (f32[512,128]{1,0:T(8,128)S(1)}, f32[512,128]{1,0:T(8,128)S(1)}, u32[]{:S(2)}, u32[]{:S(2)}) collective-permute-start(f32[512,128]{1,0:T(8,128)S(1)} %get-tuple-element.256), channel_id=1, source_target_pairs={{0,1},{1,0},{2,3},{3,2},{4,5},{5,4},{6,7},{7,6},{8,9},{9,8},{10,11... | collective-permute-start | bytes 786440 | tf_op jit(solution)/shard_map/ppermute | solution.py:466
  441.3 22.3 %collective-permute-start.29 = (bf16[64,1152]{1,0:T(8,128)(2,1)S(1)}, bf16[64,1152]{1,0:T(8,128)(2,1)S(1)}, u32[]{:S(2)}, u32[]{:S(2)}) collective-permute-start(bf16[64,1152]{1,0:T(8,128)(2,1)S(1)} %dynamic-slice_convert_fusion.2), channel_id=1, source_target_pairs={{0,8},{8,0},{1,9},{9,1},{2,10},{10,2},{3,11},{11,3},{4,12},{12,4},... | collective-permute-start | bytes 442376 | tf_op jit(solution)/shard_map/ppermute | solution.py:466
  463.7 19.7 %collective-permute-start.30 = (bf16[32,1152]{1,0:T(8,128)(2,1)S(1)}, bf16[32,1152]{1,0:T(8,128)(2,1)S(1)}, u32[]{:S(2)}, u32[]{:S(2)}) collective-permute-start(bf16[32,1152]{1,0:T(8,128)(2,1)S(1)} %dynamic-slice_convert_fusion.4), channel_id=1, source_target_pairs={{0,16},{16,0},{1,17},{17,1},{2,18},{18,2},{3,19},{19,3},{4,20},{20... | collective-permute-start | bytes 221192 | tf_op jit(solution)/shard_map/ppermute | solution.py:466
  483.5 11.0 %collective-permute-start.31 = (bf16[1,1,1,1,816,128]{5,4,3,2,1,0:T(8,128)(2,1)S(1)}, bf16[1,1,1,1,816,128]{5,4,3,2,1,0:T(8,128)(2,1)S(1)}, u32[]{:S(2)}, u32[]{:S(2)}) collective-permute-start(bf16[1,1,1,1,816,128]{5,4,3,2,1,0:T(8,128)(2,1)S(1)} %maximum_bitcast_fusion), channel_id=1, source_target_pairs={{0,16},{16,0},{1,17},{17,1},{2,18},{18,2},{3,19},{19,3},{4,20},{20... | collective-permute-start | bytes 626696 | tf_op jit(solution)/shard_map/ppermute | solution.py:466
  494.6 7.1 %collective-permute-start.32 = (bf16[2,1,1,1,400,128]{5,4,0,3,2,1:T(8,128)(2,1)S(1)}, bf16[2,1,1,1,400,128]{5,4,0,3,2,1:T(8,128)(2,1)S(1)}, u32[]{:S(2)}, u32[]{:S(2)}) collective-permute-start(bf16[2,1,1,1,400,128]{5,4,0,3,2,1:T(8,128)(2,1)S(1)} %get-tuple-element.232), channel_id=1, source_target_pairs={{0,8},{8,0},{1,9},{9,1},{2,10},{10,2},{3,11},{11,3},{4,12},{12,4},... | collective-permute-start | bytes 614408 | tf_op jit(solution)/shard_map/ppermute | solution.py:466
  494.8 8.5 %collective-permute-start.34 = (bf16[2,1,1,1,416,128]{5,4,0,3,2,1:T(8,128)(2,1)S(1)}, bf16[2,1,1,1,416,128]{5,4,0,3,2,1:T(8,128)(2,1)S(1)}, u32[]{:S(2)}, u32[]{:S(2)}) collective-permute-start(bf16[2,1,1,1,416,128]{5,4,0,3,2,1:T(8,128)(2,1)S(1)} %get-tuple-element.229), channel_id=1, source_target_pairs={{0,4},{4,0},{1,5},{5,1},{2,6},{6,2},{3,7},{7,3},{8,12},{12,8},{9,1... | collective-permute-start | bytes 638984 | tf_op jit(solution)/shard_map/ppermute | solution.py:466
  501.8 10.6 %collective-permute-start.33 = (bf16[2,2,1,1,400,128]{5,4,3,2,1,0:T(8,128)(2,1)S(1)}, bf16[2,2,1,1,400,128]{5,4,3,2,1,0:T(8,128)(2,1)S(1)}, u32[]{:S(2)}, u32[]{:S(2)}) collective-permute-start(bf16[2,2,1,1,400,128]{5,4,3,2,1,0:T(8,128)(2,1)S(1)} %maximum_select_fusion.18), channel_id=1, source_target_pairs={{0,4},{4,0},{1,5},{5,1},{2,6},{6,2},{3,7},{7,3},{8,12},{12,8},{9,1... | collective-permute-start | bytes 1228808 | tf_op jit(solution)/shard_map/ppermute | solution.py:466
  504.1 16.5 %collective-permute-start.35 = (bf16[2,1,2,1,416,128]{5,4,3,2,1,0:T(8,128)(2,1)}, bf16[2,1,2,1,416,128]{5,4,3,2,1,0:T(8,128)(2,1)}, u32[]{:S(2)}, u32[]{:S(2)}) collective-permute-start(bf16[2,1,2,1,416,128]{5,4,3,2,1,0:T(8,128)(2,1)} %maximum_select_fusion.15), channel_id=1, source_target_pairs={{0,8},{8,0},{1,9},{9,1},{2,10},{10,2},{3,11},{11,3},{4,12},{12,4},... | collective-permute-start | bytes 1277960 | tf_op jit(solution)/shard_map/ppermute | solution.py:466
  507.6 14.3 %collective-permute-start.23 = (bf16[128,1024]{0,1:T(8,128)(2,1)}, bf16[128,1024]{0,1:T(8,128)(2,1)}, u32[]{:S(2)}, u32[]{:S(2)}) collective-permute-start(bf16[128,1024]{0,1:T(8,128)(2,1)} %fusion.15), channel_id=1, source_target_pairs={{0,16},{16,0},{1,17},{17,1},{2,18},{18,2},{3,19},{19,3},{4,20},{20... | collective-permute-start | bytes 786440 | tf_op jit(solution)/shard_map/ppermute | solution.py:466
  512.5 9.5 %copy-start.25 = (f32[128,1024]{0,1:T(8,128)S(1)}, f32[128,1024]{0,1:T(8,128)}, u32[]{:S(2)}) copy-start(f32[128,1024]{0,1:T(8,128)} %copy-done.23) | copy-start | bytes 1572868
  513.5 19.3 %all-to-all-start.10 = ((bf16[16,128,128]{1,2,0:T(8,128)(2,1)}), bf16[16,128,128]{1,2,0:T(8,128)(2,1)S(1)}, u32[]{:S(2)}, u32[]{:S(2)}) async-start(bf16[16,128,128]{1,2,0:T(8,128)(2,1)} %copy.127), calls=%async_computation.10 | async-start | bytes 1048576 | tf_op jit(solution)/shard_map/all_to_all | solution.py:969
  532.9 5.2 collective-permute-start.36
  533.0 6.8 %collective-permute-start.37 = (bf16[2,2,2,1,416,128]{5,4,3,2,1,0:T(8,128)(2,1)S(1)}, bf16[2,2,2,1,416,128]{5,4,3,2,1,0:T(8,128)(2,1)S(1)}, u32[]{:S(2)}, u32[]{:S(2)}) collective-permute-start(bf16[2,2,2,1,416,128]{5,4,3,2,1,0:T(8,128)(2,1)S(1)} %maximum_select_fusion.8), channel_id=1, source_target_pairs={{0,2},{2,0},{1,3},{3,1},{4,6},{6,4},{5,7},{7,5},{8,10},{10,8},{9,1... | collective-permute-start | bytes 2555912 | tf_op jit(solution)/shard_map/ppermute | solution.py:466
  (68 other events, 244.8 us)

commit v4 on v3

--- a/solution.py
+++ b/solution.py
@@ -777,7 +777,7 @@
             ],
             out_specs=[row_spec(n) for n in columns],
         ),
-        compiler_params=pltpu.CompilerParams(vmem_limit_bytes=48 << 20),
+        compiler_params=pltpu.CompilerParams(vmem_limit_bytes=60 << 20),
     )(where, rows, grads, up_weight, down_weight)
 
 
@@ -904,12 +904,11 @@
     low, high, other_columns, counts = together(low, high, other_columns, counts)
     low = gather_step(low, "c")
     high = gather_step(high, "b")
-    counts = gather_step(counts, "b")
     out_part = share_swap(w_out)
     other_gain_two = swap(ffn_gain, "f")
     other_router = swap(w_router, "f")
-    low, high, other_cotangent, other_row_of, counts, expert_weights, out_part = together(
-        low, high, other_cotangent, other_row_of, counts, expert_weights, out_part
+    low, high, other_cotangent, other_row_of, expert_weights, out_part = together(
+        low, high, other_cotangent, other_row_of, expert_weights, out_part
     )
     low_own = low.reshape(length // 2, 512)
     high_own = high.reshape(length // 2, 512)
@@ -918,7 +917,7 @@
     expert_weights = lax.all_to_all(
         expert_weights, CTX, split_axis=0, concat_axis=0, tiled=True
     )
-    counts = gather_step(counts, "d")
+    counts = gather_step(gather_step(counts, "d"), "b")
     head_weight = in_order(my_columns, other_columns, "f", 0)
 
     order = block_order[0]
@@ -959,7 +958,7 @@
             jax.ShapeDtypeStruct((length, 64), bf16),
         ],
         [pltpu.VMEM((128, length), bf16)],
-        32 << 20,
+        60 << 20,
     )(
         place, h_place, first_key, low_own, high_own, low_next, high_next, head_weight, fine,
         coarse, start,
@@ -978,12 +977,12 @@
     out_full = share_join(w_out, out_part)
     gain_two_f = in_order(ffn_gain, other_gain_two, "f", 0).astype(f32)
     router_full = in_order(w_router, other_router, "f", 0)
-    attended_head, expert_weights, grad_rows, out_full, weight_part, counts = together(
-        attended_head, expert_weights, grad_rows, out_full, weight_part, counts
+    attended_head, expert_weights, grad_rows, out_full, weight_part = together(
+        attended_head, expert_weights, grad_rows, out_full, weight_part
     )
     attended = to_tokens(attended_head)
     weight_full = share_join(query_key_value_weight, weight_part)
-    attended, grad_rows = together(attended, grad_rows)
+    attended, grad_rows, counts = together(attended, grad_rows, counts)
     grad_rows = exchange(grad_rows)
     attended = attended.transpose(1, 0, 2).reshape(rows, 1024)
     middle_state = inputs + jnp.dot(attended, out_full, preferred_element_type=f32)
@@ -1102,7 +1101,7 @@
             pltpu.VMEM((length, 128), f32),
             pltpu.VMEM((length, 128), f32),
         ],
-        32 << 20,
+        60 << 20,
     )(
         place, first_key, idd.astype(jnp.int32)[None], query, key, value, mixed, grad_heads,
         fine, coarse, start,

time: 556 us -> 551 us (level)
  blocking collectives: 53.2 us -> 28.5 us
  starting transfers between devices: 84.9 us -> 98.5 us
  Pallas kernels: 46.9 us -> 56.8 us
    all_to_all x1 -> x0, blocking collectives: 25.2 us -> none  [to_tokens(): lax.all_to_all(value_heads.reshape(16, rows, -1), CTX, split_axis=0, conc...]
    all_to_all x1, waiting for transfers between devices: 22.3 us -> 3.06 us  [fast_shards(): lax.all_to_all(expert_weights, CTX, split_axis=0, concat_axis=0, tiled=True)]
    all_to_all x2 -> x3, starting transfers between devices: 10.3 us -> 25.4 us  [to_tokens(): lax.all_to_all(value_heads.reshape(16, rows, -1), CTX, split_axis=0, conc...]
    all_to_all x5, waiting for transfers between devices: 31.4 us -> 41 us  [exchange(): return lax.all_to_all(sent, HALF, split_axis=0, concat_axis=0, tiled=True)]
    pallas_call x3, Pallas kernels: 28.5 us -> 38 us  [run(): pl.pallas_call(kernel, out_shape=outs, grid_spec=pltpu.PrefetchScalarGrid...]
    unnamed x174 -> x160, local copies, waits for them, and re-layouts: 18 us -> 10.3 us
    concatenate x5, local copies, waits for them, and re-layouts: 6.57 us -> 0.62 us  [fast_shards(): jnp.concatenate([grad_router_part, grad_gain_two[:, None], jnp.zeros((wid...]
    select_n x21 -> x22, other arithmetic: 19.2 us -> 21 us  [in_order(): jnp.where(first, jnp.concatenate([mine, other], dim), jnp.concatenate([ot...]
  transfers between devices with their start and end apart: 47 -> 48, of which waited for: 24 -> 28; matrix products, arithmetic and copies ran while one was open for 21% -> 22% of each run, Pallas kernels for 6% -> 8%
where the time goes in v4:
time: 551 us; the launch traced here: 541 us
  waiting for transfers between devices  215 us (39%)
  starting transfers between devices  98.5 us (18%)
  other arithmetic  65.3 us (12%)
  Pallas kernels  56.8 us (10%)
  matrix products  39.1 us (7%)
  local copies, waits for them, and re-layouts  35.5 us (6%)
  blocking collectives  28.5 us (5%)
    ppermute x38, waiting for transfers between devices, swap(): return lax.ppermute(value, axis, [(0, 1), (1, 0)])  160 us
    all_to_all x5, waiting for transfers between devices, exchange(): return lax.all_to_all(sent, HALF, split_axis=0, concat_axis=0, tiled=True)  41 us
    pallas_call x3, Pallas kernels, run(): pl.pallas_call(kernel, out_shape=outs, grid_spec=pltpu.PrefetchScalarGrid...  38 us
    ppermute x38, starting transfers between devices, swap(): return lax.ppermute(value, axis, [(0, 1), (1, 0)])  37.8 us
    all_to_all x1, blocking collectives, exchange(): return lax.all_to_all(sent, HALF, split_axis=0, concat_axis=0, tiled=True)  28.5 us
    all_to_all x3, starting transfers between devices, to_tokens(): lax.all_to_all(value_heads.reshape(16, rows, -1), CTX, split_axis=0, conc...  25.4 us
    all_to_all x5, starting transfers between devices, exchange(): return lax.all_to_all(sent, HALF, split_axis=0, concat_axis=0, tiled=True)  23.6 us
    select_n x22, other arithmetic, in_order(): jnp.where(first, jnp.concatenate([mine, other], dim), jnp.concatenate([ot...  21 us
  transfers between devices with their start and end apart: 48, of which 28 were waited for; matrix products, arithmetic and copies ran while one was open for 22% of the time, Pallas kernels for 8%

profile of v4, /device:TPU:0, one launch (start us, length us, event | category | flops | bytes accessed | tf_op | source)
XLA Modules:
  0.0 540.8 jit_solution(977761675076972849)
XLA Ops:
  0.7 3.0 collective-permute-start
  5.8 2.7 collective-permute-start.2
  11.2 3.7 pad_maximum_fusion
  14.9 9.9 %collective-permute-done.1 = bf16[1,1,1,1,128,1024]{4,5,3,2,1,0:T(8,128)(2,1)S(1)} collective-permute-done((bf16[1,1,1,1,128,1024]{4,5,3,2,1,0:T(8,128)(2,1)S(1)}, bf16[1,1,1,1,128,1024]{4,5,3,2,1,0:T(8,128)(2,1)S(1)}, u32[]{:S(2)}, u32[]{:S(2)}) %collective-permute-start.1) | collective-permute-done | bytes 262176 | tf_op jit(solution)/shard_map/ppermute | solution.py:466
  30.2 2.2 collective-permute-done.6
  33.1 2.6 collective-permute-done.3
  44.1 3.5 collective-permute-done.7
  48.6 6.1 %collective-permute-done.8 = bf16[2,1,2,1,128,512]{4,5,3,2,1,0:T(8,128)(2,1)S(1)} collective-permute-done((bf16[2,1,2,1,128,512]{4,5,3,2,1,0:T(8,128)(2,1)S(1)}, bf16[2,1,2,1,128,512]{4,5,3,2,1,0:T(8,128)(2,1)S(1)}, u32[]{:S(2)}, u32[]{:S(2)}) %collective-permute-start.8) | collective-permute-done | bytes 524320 | tf_op jit(solution)/shard_map/ppermute | solution.py:466
  57.3 4.8 all-to-all-start
  69.1 3.1 convert_reduce_fusion
  79.4 2.7 convolution_convert_fusion.3
  82.1 2.5 maximum_select_fusion.13.weight
  84.6 2.2 copy.103
  86.8 2.3 copy.104
  89.7 2.8 slice_select_fusion
  97.5 2.3 maximum_select_fusion.1
  99.8 18.6 %shard_map.187 = (bf16[2048,128]{1,0:T(8,128)(2,1)}, bf16[2048,128]{1,0:T(8,128)(2,1)}, bf16[2048,128]{1,0:T(8,128)(2,1)}, f32[72,2048]{1,0:T(8,128)}, bf16[2048,64]{1,0:T(8,128)(2,1)}) custom-call(s32[32]{0:T(128)} %copy-done.71, s32[32]{0:T(128)} %select_reduce_fusion.1.h_place, s32[8]{0:T(128)} %and_select_fusion.first_key, bf16[1024,512]{1,0:T(8,128)(2,1)} %bitcast.183, ...), custom_call_target="tpu_custom_call" | custom-call | tf_op jit(solution)/shard_map/pallas_call | solution.py:812
  118.4 3.1 all-to-all-done
  121.5 2.3 copy.112
  123.8 15.5 %all-to-all-start.1 = ((bf16[16,128,64]{1,2,0:T(8,128)(2,1)}), bf16[16,128,64]{1,2,0:T(8,128)(2,1)}, u32[]{:S(2)}, u32[]{:S(2)}) async-start(bf16[16,128,64]{1,2,0:T(8,128)(2,1)} %copy.112), calls=%async_computation.1 | async-start | bytes 524288 | tf_op jit(solution)/shard_map/all_to_all | solution.py:968
  142.5 2.5 collective-permute-done.19
  145.6 3.8 all-to-all-done.1
  149.4 4.0 all-to-all-start.2
  154.7 2.7 multiply_reduce_fusion.2
  163.0 2.5 maximum_select_fusion.2
  165.6 3.6 maximum_select_fusion
  169.2 28.4 %collective-permute-done.21 = bf16[128,1152]{0,1:T(8,128)(2,1)} collective-permute-done((bf16[128,1152]{0,1:T(8,128)(2,1)S(1)}, bf16[128,1152]{0,1:T(8,128)(2,1)}, u32[]{:S(2)}, u32[]{:S(2)}) %collective-permute-start.21) | collective-permute-done | bytes 294944 | tf_op jit(solution)/shard_map/ppermute | solution.py:466
  199.3 5.8 %all-to-all-start.3 = ((bf16[16,48,1152]{2,1,0:T(8,128)(2,1)}), bf16[16,48,1152]{2,1,0:T(8,128)(2,1)}, u32[]{:S(2)}, u32[]{:S(2)}) async-start(bf16[16,48,1152]{2,1,0:T(8,128)(2,1)} %convolution_convert_fusion.1), calls=%async_computation.3 | async-start | bytes 3538944 | tf_op jit(solution)/shard_map/all_to_all | solution.py:902
  205.2 3.1 slice.136
  208.3 2.4 slice.137
  210.7 2.8 convolution_convert_fusion
  213.5 15.0 %all-to-all-done.3 = bf16[16,48,1152]{2,1,0:T(8,128)(2,1)} async-done(((bf16[16,48,1152]{2,1,0:T(8,128)(2,1)}), bf16[16,48,1152]{2,1,0:T(8,128)(2,1)}, u32[]{:S(2)}, u32[]{:S(2)}) %all-to-all-start.3) | async-done | bytes 1769504 | tf_op jit(solution)/shard_map/all_to_all | solution.py:902
  228.6 4.8 all-to-all-start.4
  233.4 9.5 %shard_map.188 = (bf16[768,1152]{1,0:T(8,128)(2,1)}, bf16[768,1024]{1,0:T(8,128)(2,1)}, bf16[768,512]{1,0:T(8,128)(2,1)}, bf16[768,1024]{1,0:T(8,128)(2,1)}, bf16[768,1024]{1,0:T(8,128)(2,1)}) custom-call(s32[1]{0:T(128)} %bitcast.33.where, bf16[768,1152]{1,0:T(8,128)(2,1)} %bitcast.38.rows, bf16[16,2,48,1024]{3,2,1,0:T(8,128)(2,1)} %bitcast.173, ...), custom_call_target="tpu_custom_call" | custom-call | tf_op jit(solution)/shard_map/pallas_call | solution.py:766
  242.9 13.8 %all-to-all-done.4 = bf16[16,48,1152]{2,1,0:T(8,128)(2,1)S(1)} async-done(((bf16[16,48,1152]{2,1,0:T(8,128)(2,1)}), bf16[16,48,1152]{2,1,0:T(8,128)(2,1)S(1)}, u32[]{:S(2)}, u32[]{:S(2)}) %all-to-all-start.4) | async-done | bytes 1769504 | tf_op jit(solution)/shard_map/all_to_all | solution.py:902
  257.9 9.4 %shard_map.189 = (bf16[768,1152]{1,0:T(8,128)(2,1)}, bf16[768,1024]{1,0:T(8,128)(2,1)}, bf16[768,512]{1,0:T(8,128)(2,1)}, bf16[768,1024]{1,0:T(8,128)(2,1)}, bf16[768,1024]{1,0:T(8,128)(2,1)}) custom-call(s32[1]{0:T(128)} %bitcast.33.where, bf16[768,1152]{1,0:T(8,128)(2,1)} %bitcast.185, bf16[16,2,48,1024]{3,2,1,0:T(8,128)(2,1)} %bitcast.174, ...), custom_call_target="tpu_custom_call" | custom-call | tf_op jit(solution)/shard_map/pallas_call | solution.py:766
  267.3 28.5 %all_to_all.55 = bf16[16,48,1152]{2,1,0:T(8,128)(2,1)} all-to-all(bf16[16,48,1152]{2,1,0:T(8,128)(2,1)} %bitcast.201), channel_id=1, replica_groups=mesh['a'=2,'b'=2,'c'=2,'d'=2,'f'=2] {'b','c','d','f'}, dimensions={0} | all-to-all | bytes 3538944 | tf_op jit(solution)/shard_map/all_to_all | solution.py:902
  295.8 4.2 all-to-all-start.6
  300.1 2.5 fusion.90
  302.7 3.4 fusion.3
  313.5 15.2 %collective-permute-done.22 = bf16[128,1152]{0,1:T(8,128)(2,1)S(1)} collective-permute-done((bf16[128,1152]{0,1:T(8,128)(2,1)S(1)}, bf16[128,1152]{0,1:T(8,128)(2,1)S(1)}, u32[]{:S(2)}, u32[]{:S(2)}) %collective-permute-start.22) | collective-permute-done | bytes 294944 | tf_op jit(solution)/shard_map/ppermute | solution.py:466
  334.6 5.1 all-to-all-start.7
  339.7 3.5 pad_maximum_fusion.3
  343.3 6.5 %all-to-all-done.7 = bf16[16,128,64]{1,2,0:T(8,128)(2,1)S(1)} async-done(((bf16[16,128,64]{1,2,0:T(8,128)(2,1)}), bf16[16,128,64]{1,2,0:T(8,128)(2,1)S(1)}, u32[]{:S(2)}, u32[]{:S(2)}) %all-to-all-start.7) | async-done | bytes 262176 | tf_op jit(solution)/shard_map/all_to_all | solution.py:968
  350.8 4.8 all-to-all-start.8
  360.1 15.8 %shard_map.190 = (f32[2048,128]{1,0:T(8,128)}, bf16[2048,128]{1,0:T(8,128)(2,1)}) custom-call(s32[32]{0:T(128)} %copy-done.71, s32[8]{0:T(128)} %and_select_fusion.first_key, s32[1]{0:T(128)} %bitcast.55.core, bf16[2048,128]{1,0:T(8,128)(2,1)} %get-tuple-element.159.query, bf16[2048,128]{1,0:T(8,128)(2,1)} %get-tuple-element.160.key, ...), custom_call_target="tpu_custom_call" | custom-call | tf_op jit(solution)/shard_map/pallas_call | solution.py:812
  376.4 3.4 collective-permute-done.24
  385.9 9.4 %all-to-all-done.8 = bf16[16,96,1024]{2,1,0:T(8,128)(2,1)} async-done(((bf16[16,96,1024]{2,1,0:T(8,128)(2,1)}), bf16[16,96,1024]{2,1,0:T(8,128)(2,1)}, u32[]{:S(2)}, u32[]{:S(2)}) %all-to-all-start.8) | async-done | bytes 3145760 | tf_op jit(solution)/shard_map/all_to_all | solution.py:902
  395.3 6.8 %all-to-all-start.9 = ((bf16[16,96,1024]{2,1,0:T(8,128)(2,1)}), bf16[16,96,1024]{2,1,0:T(8,128)(2,1)}, u32[]{:S(2)}, u32[]{:S(2)}) async-start(bf16[16,96,1024]{2,1,0:T(8,128)(2,1)} %pad_maximum_fusion.2), calls=%async_computation.9 | async-start | bytes 6291456 | tf_op jit(solution)/shard_map/all_to_all | solution.py:1114
  404.6 6.7 %collective-permute-done.27 = bf16[256,1152]{1,0:T(8,128)(2,1)} collective-permute-done((bf16[256,1152]{1,0:T(8,128)(2,1)}, bf16[256,1152]{1,0:T(8,128)(2,1)}, u32[]{:S(2)}, u32[]{:S(2)}) %collective-permute-start.27) | collective-permute-done | bytes 589856 | tf_op jit(solution)/shard_map/ppermute | solution.py:466
  414.9 19.8 %collective-permute-done.28 = bf16[128,1152]{1,0:T(8,128)(2,1)S(1)} collective-permute-done((bf16[128,1152]{1,0:T(8,128)(2,1)S(1)}, bf16[128,1152]{1,0:T(8,128)(2,1)S(1)}, u32[]{:S(2)}, u32[]{:S(2)}) %collective-permute-start.28) | collective-permute-done | bytes 294944 | tf_op jit(solution)/shard_map/ppermute | solution.py:466
  435.2 21.9 %collective-permute-done.29 = bf16[64,1152]{1,0:T(8,128)(2,1)S(1)} collective-permute-done((bf16[64,1152]{1,0:T(8,128)(2,1)S(1)}, bf16[64,1152]{1,0:T(8,128)(2,1)S(1)}, u32[]{:S(2)}, u32[]{:S(2)}) %collective-permute-start.29) | collective-permute-done | bytes 147488 | tf_op jit(solution)/shard_map/ppermute | solution.py:466
  457.1 4.6 collective-permute-start.30
  461.7 15.1 %collective-permute-done.30 = bf16[32,1152]{1,0:T(8,128)(2,1)S(1)} collective-permute-done((bf16[32,1152]{1,0:T(8,128)(2,1)S(1)}, bf16[32,1152]{1,0:T(8,128)(2,1)S(1)}, u32[]{:S(2)}, u32[]{:S(2)}) %collective-permute-start.30) | collective-permute-done | bytes 73760 | tf_op jit(solution)/shard_map/ppermute | solution.py:466
  477.0 10.9 %collective-permute-done.31 = bf16[1,1,1,1,816,128]{5,4,3,2,1,0:T(8,128)(2,1)S(1)} collective-permute-done((bf16[1,1,1,1,816,128]{5,4,3,2,1,0:T(8,128)(2,1)S(1)}, bf16[1,1,1,1,816,128]{5,4,3,2,1,0:T(8,128)(2,1)S(1)}, u32[]{:S(2)}, u32[]{:S(2)}) %collective-permute-start.31) | collective-permute-done | bytes 208928 | tf_op jit(solution)/shard_map/ppermute | solution.py:466
  489.7 5.5 %collective-permute-done.32 = bf16[2,1,1,1,400,128]{5,4,0,3,2,1:T(8,128)(2,1)S(1)} collective-permute-done((bf16[2,1,1,1,400,128]{5,4,0,3,2,1:T(8,128)(2,1)S(1)}, bf16[2,1,1,1,400,128]{5,4,0,3,2,1:T(8,128)(2,1)S(1)}, u32[]{:S(2)}, u32[]{:S(2)}) %collective-permute-start.32) | collective-permute-done | bytes 204832 | tf_op jit(solution)/shard_map/ppermute | solution.py:466
  498.9 2.2 fusion.15
  501.1 2.6 collective-permute-start.23
  507.0 4.9 all-to-all-start.10
  511.9 2.3 collective-permute-done.35
  518.8 2.8 slice_convert_fusion.1
  521.6 4.1 slice_convert_fusion
  527.0 3.5 fusion.22
  534.8 3.6 shard_map.191
  (343 shorter events, 108.8 us)
Async XLA Ops:
  0.7 9.2 %collective-permute-start = (bf16[512]{0:T(512)(128)(2,1)}, bf16[512]{0:T(512)(128)(2,1)S(1)}, u32[]{:S(2)}, u32[]{:S(2)}) collective-permute-start(bf16[512]{0:T(512)(128)(2,1)} %param.16), channel_id=1, source_target_pairs={{0,1},{1,0},{2,3},{3,2},{4,5},{5,4},{6,7},{7,6},{8,9},{9,8},{10,11... | collective-permute-start | bytes 3080 | tf_op jit(solution)/shard_map/ppermute | solution.py:466
  5.8 5.4 collective-permute-start.2
  9.6 145.1 %copy-start.13 = (bf16[1,128,1024]{1,2,0:T(8,128)(2,1)}, bf16[1,128,1024]{1,2,0:T(8,128)(2,1)S(1)}, u32[]{:S(2)}) copy-start(bf16[1,128,1024]{1,2,0:T(8,128)(2,1)S(1)} %copy.101) | copy-start | bytes 786436
  10.8 14.1 %collective-permute-start.1 = (bf16[1,1,1,1,128,1024]{4,5,3,2,1,0:T(8,128)(2,1)S(1)}, bf16[1,1,1,1,128,1024]{4,5,3,2,1,0:T(8,128)(2,1)S(1)}, u32[]{:S(2)}, u32[]{:S(2)}) collective-permute-start(bf16[1,1,1,1,128,1024]{4,5,3,2,1,0:T(8,128)(2,1)S(1)} %bitcast.206), channel_id=1, source_target_pairs={{0,16},{16,0},{1,17},{17,1},{2,18},{18,2},{3,19},{19,3},{4,20},{20... | collective-permute-start | bytes 786440 | tf_op jit(solution)/shard_map/ppermute | solution.py:466
  25.0 8.0 %collective-permute-start.4 = (bf16[2,1,1,1,128,512]{4,5,3,2,1,0:T(8,128)(2,1)S(1)}, bf16[2,1,1,1,128,512]{4,5,3,2,1,0:T(8,128)(2,1)S(1)}, u32[]{:S(2)}, u32[]{:S(2)}) collective-permute-start(bf16[2,1,1,1,128,512]{4,5,3,2,1,0:T(8,128)(2,1)S(1)} %get-tuple-element.224), channel_id=1, source_target_pairs={{0,4},{4,0},{1,5},{5,1},{2,6},{6,2},{3,7},{7,3},{8,12},{12,8},{9,1... | collective-permute-start | bytes 786440 | tf_op jit(solution)/shard_map/ppermute | solution.py:466
  28.8 6.9 %collective-permute-start.3 = (bf16[2,1,1,1,128,512]{4,5,3,2,1,0:T(8,128)(2,1)S(1)}, bf16[2,1,1,1,128,512]{4,5,3,2,1,0:T(8,128)(2,1)S(1)}, u32[]{:S(2)}, u32[]{:S(2)}) collective-permute-start(bf16[2,1,1,1,128,512]{4,5,3,2,1,0:T(8,128)(2,1)S(1)} %get-tuple-element.225), channel_id=1, source_target_pairs={{0,8},{8,0},{1,9},{9,1},{2,10},{10,2},{3,11},{11,3},{4,12},{12,4},... | collective-permute-start | bytes 786440 | tf_op jit(solution)/shard_map/ppermute | solution.py:466
  28.8 3.6 collective-permute-start.6
  29.6 6.7 %collective-permute-start.5 = (bf16[512,256]{1,0:T(8,128)(2,1)S(1)}, bf16[512,256]{1,0:T(8,128)(2,1)S(1)}, u32[]{:S(2)}, u32[]{:S(2)}) collective-permute-start(bf16[512,256]{1,0:T(8,128)(2,1)S(1)} %pad_maximum_fusion.8), channel_id=1, source_target_pairs={{0,1},{1,0},{2,3},{3,2},{4,5},{5,4},{6,7},{7,6},{8,9},{9,8},{10,11... | collective-permute-start | bytes 786440 | tf_op jit(solution)/shard_map/ppermute | solution.py:466
  36.3 11.3 %collective-permute-start.7 = (bf16[2,2,1,1,128,512]{4,5,3,2,1,0:T(8,128)(2,1)S(1)}, bf16[2,2,1,1,128,512]{4,5,3,2,1,0:T(8,128)(2,1)S(1)}, u32[]{:S(2)}, u32[]{:S(2)}) collective-permute-start(bf16[2,2,1,1,128,512]{4,5,3,2,1,0:T(8,128)(2,1)S(1)} %maximum_select_fusion.11), channel_id=1, source_target_pairs={{0,4},{4,0},{1,5},{5,1},{2,6},{6,2},{3,7},{7,3},{8,12},{12,8},{9,1... | collective-permute-start | bytes 1572872 | tf_op jit(solution)/shard_map/ppermute | solution.py:466
  37.7 17.0 %collective-permute-start.8 = (bf16[2,1,2,1,128,512]{4,5,3,2,1,0:T(8,128)(2,1)S(1)}, bf16[2,1,2,1,128,512]{4,5,3,2,1,0:T(8,128)(2,1)S(1)}, u32[]{:S(2)}, u32[]{:S(2)}) collective-permute-start(bf16[2,1,2,1,128,512]{4,5,3,2,1,0:T(8,128)(2,1)S(1)} %maximum_select_fusion.12), channel_id=1, source_target_pairs={{0,8},{8,0},{1,9},{9,1},{2,10},{10,2},{3,11},{11,3},{4,12},{12,4},... | collective-permute-start | bytes 1572872 | tf_op jit(solution)/shard_map/ppermute | solution.py:466
  40.3 16.1 %collective-permute-start.11 = (bf16[256,1024]{1,0:T(8,128)(2,1)}, bf16[256,1024]{1,0:T(8,128)(2,1)S(1)}, u32[]{:S(2)}, u32[]{:S(2)}) collective-permute-start(bf16[256,1024]{1,0:T(8,128)(2,1)} %slice_select_fusion.1), channel_id=1, source_target_pairs={{0,1},{1,0},{2,3},{3,2},{4,5},{5,4},{6,7},{7,6},{8,9},{9,8},{10,11... | collective-permute-start | bytes 1572872 | tf_op jit(solution)/shard_map/ppermute | solution.py:466
  41.1 14.8 %copy-start.25 = (bf16[1,128,1024]{1,2,0:T(8,128)(2,1)}, bf16[1,128,1024]{1,2,0:T(8,128)(2,1)S(1)}, u32[]{:S(2)}) copy-start(bf16[1,128,1024]{1,2,0:T(8,128)(2,1)S(1)} %copy.102) | copy-start | bytes 786436
  41.1 14.8 %collective-permute-start.9 = (bf16[128,1024]{0,1:T(8,128)(2,1)S(1)}, bf16[128,1024]{0,1:T(8,128)(2,1)S(1)}, u32[]{:S(2)}, u32[]{:S(2)}) collective-permute-start(bf16[128,1024]{0,1:T(8,128)(2,1)S(1)} %bitcast.205), channel_id=1, source_target_pairs={{0,16},{16,0},{1,17},{17,1},{2,18},{18,2},{3,19},{19,3},{4,20},{20... | collective-permute-start | bytes 786440 | tf_op jit(solution)/shard_map/ppermute | solution.py:466
  42.3 13.6 %collective-permute-start.10 = (f32[128,32]{0,1:T(8,128)S(1)}, f32[128,32]{0,1:T(8,128)S(1)}, u32[]{:S(2)}, u32[]{:S(2)}) collective-permute-start(f32[128,32]{0,1:T(8,128)S(1)} %get-tuple-element.106), channel_id=1, source_target_pairs={{0,16},{16,0},{1,17},{17,1},{2,18},{18,2},{3,19},{19,3},{4,20},{20... | collective-permute-start | bytes 49160 | tf_op jit(solution)/shard_map/ppermute | solution.py:466
  57.3 64.1 %all-to-all-start = ((bf16[16,96,1024]{2,1,0:T(8,128)(2,1)}), bf16[16,96,1024]{2,1,0:T(8,128)(2,1)S(1)}, u32[]{:S(2)}, u32[]{:S(2)}) async-start(bf16[16,96,1024]{2,1,0:T(8,128)(2,1)} %pad_maximum_fusion), calls=%async_computation | async-start | bytes 6291456 | tf_op jit(solution)/shard_map/all_to_all | solution.py:917
  73.5 16.2 %collective-permute-start.14 = (bf16[512]{0:T(512)(128)(2,1)}, bf16[512]{0:T(512)(128)(2,1)}, u32[]{:S(2)}, u32[]{:S(2)}) collective-permute-start(bf16[512]{0:T(512)(128)(2,1)} %param.19), channel_id=1, source_target_pairs={{0,1},{1,0},{2,3},{3,2},{4,5},{5,4},{6,7},{7,6},{8,9},{9,8},{10,11... | collective-permute-start | bytes 3080 | tf_op jit(solution)/shard_map/ppermute | solution.py:466
  74.0 15.7 %collective-permute-start.15 = (bf16[512,32]{0,1:T(8,128)(2,1)}, bf16[512,32]{0,1:T(8,128)(2,1)}, u32[]{:S(2)}, u32[]{:S(2)}) collective-permute-start(bf16[512,32]{0,1:T(8,128)(2,1)} %param.20), channel_id=1, source_target_pairs={{0,1},{1,0},{2,3},{3,2},{4,5},{5,4},{6,7},{7,6},{8,9},{9,8},{10,11... | collective-permute-start | bytes 98312 | tf_op jit(solution)/shard_map/ppermute | solution.py:466
  89.1 10.7 %collective-permute-start.12 = (bf16[1024,512]{1,0:T(8,128)(2,1)}, bf16[1024,512]{1,0:T(8,128)(2,1)}, u32[]{:S(2)}, u32[]{:S(2)}) collective-permute-start(bf16[1024,512]{1,0:T(8,128)(2,1)} %bitcast.182), channel_id=1, source_target_pairs={{0,2},{2,0},{1,3},{3,1},{4,6},{6,4},{5,7},{7,5},{8,10},{10,8},{9,1... | collective-permute-start | bytes 3145736 | tf_op jit(solution)/shard_map/ppermute | solution.py:466
  89.2 10.6 %collective-permute-start.13 = (bf16[1024,512]{1,0:T(8,128)(2,1)}, bf16[1024,512]{1,0:T(8,128)(2,1)}, u32[]{:S(2)}, u32[]{:S(2)}) collective-permute-start(bf16[1024,512]{1,0:T(8,128)(2,1)} %bitcast.179), channel_id=1, source_target_pairs={{0,2},{2,0},{1,3},{3,1},{4,6},{6,4},{5,7},{7,5},{8,10},{10,8},{9,1... | collective-permute-start | bytes 3145736 | tf_op jit(solution)/shard_map/ppermute | solution.py:466
  92.4 26.0 %collective-permute-start.17 = (bf16[256,2048]{1,0:T(8,128)(2,1)}, bf16[256,2048]{1,0:T(8,128)(2,1)}, u32[]{:S(2)}, u32[]{:S(2)}) collective-permute-start(bf16[256,2048]{1,0:T(8,128)(2,1)} %slice_select_fusion), channel_id=1, source_target_pairs={{0,1},{1,0},{2,3},{3,2},{4,5},{5,4},{6,7},{7,6},{8,9},{9,8},{10,11... | collective-permute-start | bytes 3145736 | tf_op jit(solution)/shard_map/ppermute | solution.py:466
  93.0 3.3 collective-permute-start.16
  99.8 39.4 %copy-start.58 = (f32[2,1,2,1,1,32]{5,4,3,2,1,0:T(1,128)S(1)}, f32[2,1,2,1,1,32]{5,4,3,2,1,0:T(1,128)}, u32[]{:S(2)}) copy-start(f32[2,1,2,1,1,32]{5,4,3,2,1,0:T(1,128)} %broadcast_select_fusion.7) | copy-start | bytes 1540
  121.5 27.9 %copy-start.4 = (bf16[16,96,1024]{2,1,0:T(8,128)(2,1)}, bf16[16,96,1024]{2,1,0:T(8,128)(2,1)S(1)}, u32[]{:S(2)}) copy-start(bf16[16,96,1024]{2,1,0:T(8,128)(2,1)S(1)} %all-to-all-done) | copy-start | bytes 9437188
  123.8 25.6 %all-to-all-start.1 = ((bf16[16,128,64]{1,2,0:T(8,128)(2,1)}), bf16[16,128,64]{1,2,0:T(8,128)(2,1)}, u32[]{:S(2)}, u32[]{:S(2)}) async-start(bf16[16,128,64]{1,2,0:T(8,128)(2,1)} %copy.112), calls=%async_computation.1 | async-start | bytes 524288 | tf_op jit(solution)/shard_map/all_to_all | solution.py:968
  139.3 1.2 collective-permute-start.18
  140.5 4.4 collective-permute-start.19
  149.4 49.9 %all-to-all-start.2 = ((bf16[16,96,1024]{2,1,0:T(8,128)(2,1)}), bf16[16,96,1024]{2,1,0:T(8,128)(2,1)S(1)}, u32[]{:S(2)}, u32[]{:S(2)}) async-start(bf16[16,96,1024]{2,1,0:T(8,128)(2,1)} %pad_maximum_fusion.1), calls=%async_computation.2 | async-start | bytes 6291456 | tf_op jit(solution)/shard_map/all_to_all | solution.py:902
  154.3 8.7 %collective-permute-start.20 = (bf16[256,2048]{1,0:T(8,128)(2,1)}, bf16[256,2048]{1,0:T(8,128)(2,1)S(1)}, u32[]{:S(2)}, u32[]{:S(2)}) collective-permute-start(bf16[256,2048]{1,0:T(8,128)(2,1)} %collective-permute-done.17), channel_id=1, source_target_pairs={{0,2},{2,0},{1,3},{3,1},{4,6},{6,4},{5,7},{7,5},{8,10},{10,8},{9,1... | collective-permute-start | bytes 3145736 | tf_op jit(solution)/shard_map/ppermute | solution.py:466
  160.0 37.6 %collective-permute-start.21 = (bf16[128,1152]{0,1:T(8,128)(2,1)S(1)}, bf16[128,1152]{0,1:T(8,128)(2,1)}, u32[]{:S(2)}, u32[]{:S(2)}) collective-permute-start(bf16[128,1152]{0,1:T(8,128)(2,1)S(1)} %maximum_maximum_fusion.1), channel_id=1, source_target_pairs={{0,16},{16,0},{1,17},{17,1},{2,18},{18,2},{3,19},{19,3},{4,20},{20... | collective-permute-start | bytes 884744 | tf_op jit(solution)/shard_map/ppermute | solution.py:466
  199.3 29.2 %all-to-all-start.3 = ((bf16[16,48,1152]{2,1,0:T(8,128)(2,1)}), bf16[16,48,1152]{2,1,0:T(8,128)(2,1)}, u32[]{:S(2)}, u32[]{:S(2)}) async-start(bf16[16,48,1152]{2,1,0:T(8,128)(2,1)} %convolution_convert_fusion.1), calls=%async_computation.3 | async-start | bytes 3538944 | tf_op jit(solution)/shard_map/all_to_all | solution.py:902
  228.6 28.1 %all-to-all-start.4 = ((bf16[16,48,1152]{2,1,0:T(8,128)(2,1)}), bf16[16,48,1152]{2,1,0:T(8,128)(2,1)S(1)}, u32[]{:S(2)}, u32[]{:S(2)}) async-start(bf16[16,48,1152]{2,1,0:T(8,128)(2,1)} %convolution_convert_fusion), calls=%async_computation.4 | async-start | bytes 3538944 | tf_op jit(solution)/shard_map/all_to_all | solution.py:902
  295.8 33.7 %all-to-all-start.6 = ((bf16[16,48,1152]{2,1,0:T(8,128)(2,1)}), bf16[16,48,1152]{2,1,0:T(8,128)(2,1)S(1)}, u32[]{:S(2)}, u32[]{:S(2)}) async-start(bf16[16,48,1152]{2,1,0:T(8,128)(2,1)} %bitcast.200), calls=%async_computation.6 | async-start | bytes 3538944 | tf_op jit(solution)/shard_map/all_to_all | solution.py:902
  309.1 19.6 %collective-permute-start.22 = (bf16[128,1152]{0,1:T(8,128)(2,1)S(1)}, bf16[128,1152]{0,1:T(8,128)(2,1)S(1)}, u32[]{:S(2)}, u32[]{:S(2)}) collective-permute-start(bf16[128,1152]{0,1:T(8,128)(2,1)S(1)} %fusion.1), channel_id=1, source_target_pairs={{0,16},{16,0},{1,17},{17,1},{2,18},{18,2},{3,19},{19,3},{4,20},{20... | collective-permute-start | bytes 884744 | tf_op jit(solution)/shard_map/ppermute | solution.py:466
  311.4 18.2 %copy-start.39 = (f32[128,2,1,8]{0,1,3,2:T(2,128)S(1)}, f32[128,2,1,8]{0,1,3,2:T(2,128)}, u32[]{:S(2)}) copy-start(f32[128,2,1,8]{0,1,3,2:T(2,128)} %copy-done.37) | copy-start | bytes 24580
  313.4 17.0 %copy-start.33 = (pred[128,32]{0,1:T(8,128)(4,1)S(1)}, pred[128,32]{0,1:T(8,128)(4,1)}, u32[]{:S(2)}) copy-start(pred[128,32]{0,1:T(8,128)(4,1)} %copy-done.31) | copy-start | bytes 12292
  313.4 17.0 %copy-start.49 = (pred[128,32]{0,1:T(8,128)(4,1)S(1)}, pred[128,32]{0,1:T(8,128)(4,1)}, u32[]{:S(2)}) copy-start(pred[128,32]{0,1:T(8,128)(4,1)} %copy-done.48) | copy-start | bytes 12292
  313.4 17.0 %copy-start.54 = (f32[128]{0:T(128)S(1)}, f32[128]{0:T(128)}, u32[]{:S(2)}) copy-start(f32[128]{0:T(128)} %copy-done.53) | copy-start | bytes 1540
  313.4 17.0 %copy-start.56 = (f32[128]{0:T(128)S(1)}, f32[128]{0:T(128)}, u32[]{:S(2)}) copy-start(f32[128]{0:T(128)} %copy-done.55) | copy-start | bytes 1540
  313.4 17.1 %copy-start.3 = (f32[128,1024]{0,1:T(8,128)S(1)}, f32[128,1024]{0,1:T(8,128)}, u32[]{:S(2)}) copy-start(f32[128,1024]{0,1:T(8,128)} %copy-done.2) | copy-start | bytes 1572868
  313.4 17.1 %copy-start.46 = (f32[1024]{0:T(1024)S(1)}, f32[1024]{0:T(1024)}, u32[]{:S(2)}) copy-start(f32[1024]{0:T(1024)} %copy-done.45) | copy-start | bytes 12292
  313.4 17.1 %copy-start.51 = (bf16[512,32]{0,1:T(8,128)(2,1)S(1)}, bf16[512,32]{0,1:T(8,128)(2,1)}, u32[]{:S(2)}) copy-start(bf16[512,32]{0,1:T(8,128)(2,1)} %param.20) | copy-start | bytes 98308
  313.4 17.1 %copy-start.66 = (f32[128]{0:T(128)S(1)}, f32[128]{0:T(128)}, u32[]{:S(2)}) copy-start(f32[128]{0:T(128)} %copy-done.65) | copy-start | bytes 1540
  313.5 18.6 %copy-start.26 = (bf16[1,128,1024]{1,2,0:T(8,128)(2,1)S(1)}, bf16[1,128,1024]{1,2,0:T(8,128)(2,1)}, u32[]{:S(2)}) copy-start(bf16[1,128,1024]{1,2,0:T(8,128)(2,1)} %copy-done.25) | copy-start | bytes 786436
  334.6 15.1 %all-to-all-start.7 = ((bf16[16,128,64]{1,2,0:T(8,128)(2,1)}), bf16[16,128,64]{1,2,0:T(8,128)(2,1)S(1)}, u32[]{:S(2)}, u32[]{:S(2)}) async-start(bf16[16,128,64]{1,2,0:T(8,128)(2,1)} %bitcast.48), calls=%async_computation.7 | async-start | bytes 524288 | tf_op jit(solution)/shard_map/all_to_all | solution.py:968
  350.8 44.5 %all-to-all-start.8 = ((bf16[16,96,1024]{2,1,0:T(8,128)(2,1)}), bf16[16,96,1024]{2,1,0:T(8,128)(2,1)}, u32[]{:S(2)}, u32[]{:S(2)}) async-start(bf16[16,96,1024]{2,1,0:T(8,128)(2,1)} %pad_maximum_fusion.3), calls=%async_computation.8 | async-start | bytes 6291456 | tf_op jit(solution)/shard_map/all_to_all | solution.py:902
  375.9 5.4 %collective-permute-start.26 = (bf16[512,1152]{1,0:T(8,128)(2,1)}, bf16[512,1152]{1,0:T(8,128)(2,1)}, u32[]{:S(2)}, u32[]{:S(2)}) collective-permute-start(bf16[512,1152]{1,0:T(8,128)(2,1)} %pad_maximum_fusion.5), channel_id=1, source_target_pairs={{0,2},{2,0},{1,3},{3,1},{4,6},{6,4},{5,7},{7,5},{8,10},{10,8},{9,1... | collective-permute-start | bytes 3538952 | tf_op jit(solution)/shard_map/ppermute | solution.py:466
  376.3 3.6 collective-permute-start.24
  383.9 27.3 %collective-permute-start.27 = (bf16[256,1152]{1,0:T(8,128)(2,1)}, bf16[256,1152]{1,0:T(8,128)(2,1)}, u32[]{:S(2)}, u32[]{:S(2)}) collective-permute-start(bf16[256,1152]{1,0:T(8,128)(2,1)} %dynamic-slice_convert_fusion), channel_id=1, source_target_pairs={{0,1},{1,0},{2,3},{3,2},{4,5},{5,4},{6,7},{7,6},{8,9},{9,8},{10,11... | collective-permute-start | bytes 1769480 | tf_op jit(solution)/shard_map/ppermute | solution.py:466
  385.9 16.3 %copy-start.7 = (bf16[2,2,2,1,128,512]{5,4,2,1,0,3:T(8,128)(2,1)S(1)}, bf16[2,2,2,1,128,512]{5,4,2,1,0,3:T(8,128)(2,1)}, u32[]{:S(2)}) copy-start(bf16[2,2,2,1,128,512]{5,4,2,1,0,3:T(8,128)(2,1)} %copy.103) | copy-start | bytes 3145732
  395.3 110.7 %all-to-all-start.9 = ((bf16[16,96,1024]{2,1,0:T(8,128)(2,1)}), bf16[16,96,1024]{2,1,0:T(8,128)(2,1)}, u32[]{:S(2)}, u32[]{:S(2)}) async-start(bf16[16,96,1024]{2,1,0:T(8,128)(2,1)} %pad_maximum_fusion.2), calls=%async_computation.9 | async-start | bytes 6291456 | tf_op jit(solution)/shard_map/all_to_all | solution.py:1114
  412.5 22.2 %collective-permute-start.28 = (bf16[128,1152]{1,0:T(8,128)(2,1)S(1)}, bf16[128,1152]{1,0:T(8,128)(2,1)S(1)}, u32[]{:S(2)}, u32[]{:S(2)}) collective-permute-start(bf16[128,1152]{1,0:T(8,128)(2,1)S(1)} %dynamic-slice_convert_fusion.1), channel_id=1, source_target_pairs={{0,4},{4,0},{1,5},{5,1},{2,6},{6,2},{3,7},{7,3},{8,12},{12,8},{9,1... | collective-permute-start | bytes 884744 | tf_op jit(solution)/shard_map/ppermute | solution.py:466
  413.0 21.9 %copy-start.30 = (bf16[512,64]{1,0:T(8,128)(2,1)S(1)}, bf16[512,64]{1,0:T(8,128)(2,1)}, u32[]{:S(2)}) copy-start(bf16[512,64]{1,0:T(8,128)(2,1)} %get-tuple-element.212) | copy-start | bytes 196612
  414.8 20.1 %collective-permute-start.25 = (f32[512,128]{1,0:T(8,128)S(1)}, f32[512,128]{1,0:T(8,128)S(1)}, u32[]{:S(2)}, u32[]{:S(2)}) collective-permute-start(f32[512,128]{1,0:T(8,128)S(1)} %get-tuple-element.254), channel_id=1, source_target_pairs={{0,1},{1,0},{2,3},{3,2},{4,5},{5,4},{6,7},{7,6},{8,9},{9,8},{10,11... | collective-permute-start | bytes 786440 | tf_op jit(solution)/shard_map/ppermute | solution.py:466
  434.8 22.3 %collective-permute-start.29 = (bf16[64,1152]{1,0:T(8,128)(2,1)S(1)}, bf16[64,1152]{1,0:T(8,128)(2,1)S(1)}, u32[]{:S(2)}, u32[]{:S(2)}) collective-permute-start(bf16[64,1152]{1,0:T(8,128)(2,1)S(1)} %dynamic-slice_convert_fusion.2), channel_id=1, source_target_pairs={{0,8},{8,0},{1,9},{9,1},{2,10},{10,2},{3,11},{11,3},{4,12},{12,4},... | collective-permute-start | bytes 442376 | tf_op jit(solution)/shard_map/ppermute | solution.py:466
  457.1 19.7 %collective-permute-start.30 = (bf16[32,1152]{1,0:T(8,128)(2,1)S(1)}, bf16[32,1152]{1,0:T(8,128)(2,1)S(1)}, u32[]{:S(2)}, u32[]{:S(2)}) collective-permute-start(bf16[32,1152]{1,0:T(8,128)(2,1)S(1)} %dynamic-slice_convert_fusion.4), channel_id=1, source_target_pairs={{0,16},{16,0},{1,17},{17,1},{2,18},{18,2},{3,19},{19,3},{4,20},{20... | collective-permute-start | bytes 221192 | tf_op jit(solution)/shard_map/ppermute | solution.py:466
  477.0 11.0 %collective-permute-start.31 = (bf16[1,1,1,1,816,128]{5,4,3,2,1,0:T(8,128)(2,1)S(1)}, bf16[1,1,1,1,816,128]{5,4,3,2,1,0:T(8,128)(2,1)S(1)}, u32[]{:S(2)}, u32[]{:S(2)}) collective-permute-start(bf16[1,1,1,1,816,128]{5,4,3,2,1,0:T(8,128)(2,1)S(1)} %maximum_bitcast_fusion), channel_id=1, source_target_pairs={{0,16},{16,0},{1,17},{17,1},{2,18},{18,2},{3,19},{19,3},{4,20},{20... | collective-permute-start | bytes 626696 | tf_op jit(solution)/shard_map/ppermute | solution.py:466
  488.1 7.1 %collective-permute-start.32 = (bf16[2,1,1,1,400,128]{5,4,0,3,2,1:T(8,128)(2,1)S(1)}, bf16[2,1,1,1,400,128]{5,4,0,3,2,1:T(8,128)(2,1)S(1)}, u32[]{:S(2)}, u32[]{:S(2)}) collective-permute-start(bf16[2,1,1,1,400,128]{5,4,0,3,2,1:T(8,128)(2,1)S(1)} %get-tuple-element.230), channel_id=1, source_target_pairs={{0,8},{8,0},{1,9},{9,1},{2,10},{10,2},{3,11},{11,3},{4,12},{12,4},... | collective-permute-start | bytes 614408 | tf_op jit(solution)/shard_map/ppermute | solution.py:466
  488.3 8.5 %collective-permute-start.34 = (bf16[2,1,1,1,416,128]{5,4,0,3,2,1:T(8,128)(2,1)S(1)}, bf16[2,1,1,1,416,128]{5,4,0,3,2,1:T(8,128)(2,1)S(1)}, u32[]{:S(2)}, u32[]{:S(2)}) collective-permute-start(bf16[2,1,1,1,416,128]{5,4,0,3,2,1:T(8,128)(2,1)S(1)} %get-tuple-element.227), channel_id=1, source_target_pairs={{0,4},{4,0},{1,5},{5,1},{2,6},{6,2},{3,7},{7,3},{8,12},{12,8},{9,1... | collective-permute-start | bytes 638984 | tf_op jit(solution)/shard_map/ppermute | solution.py:466
  495.3 10.6 %collective-permute-start.33 = (bf16[2,2,1,1,400,128]{5,4,3,2,1,0:T(8,128)(2,1)S(1)}, bf16[2,2,1,1,400,128]{5,4,3,2,1,0:T(8,128)(2,1)S(1)}, u32[]{:S(2)}, u32[]{:S(2)}) collective-permute-start(bf16[2,2,1,1,400,128]{5,4,3,2,1,0:T(8,128)(2,1)S(1)} %maximum_select_fusion.18), channel_id=1, source_target_pairs={{0,4},{4,0},{1,5},{5,1},{2,6},{6,2},{3,7},{7,3},{8,12},{12,8},{9,1... | collective-permute-start | bytes 1228808 | tf_op jit(solution)/shard_map/ppermute | solution.py:466
  497.6 16.5 %collective-permute-start.35 = (bf16[2,1,2,1,416,128]{5,4,3,2,1,0:T(8,128)(2,1)}, bf16[2,1,2,1,416,128]{5,4,3,2,1,0:T(8,128)(2,1)}, u32[]{:S(2)}, u32[]{:S(2)}) collective-permute-start(bf16[2,1,2,1,416,128]{5,4,3,2,1,0:T(8,128)(2,1)} %maximum_select_fusion.15), channel_id=1, source_target_pairs={{0,8},{8,0},{1,9},{9,1},{2,10},{10,2},{3,11},{11,3},{4,12},{12,4},... | collective-permute-start | bytes 1277960 | tf_op jit(solution)/shard_map/ppermute | solution.py:466
  501.1 14.6 %collective-permute-start.23 = (bf16[128,1024]{0,1:T(8,128)(2,1)S(1)}, bf16[128,1024]{0,1:T(8,128)(2,1)}, u32[]{:S(2)}, u32[]{:S(2)}) collective-permute-start(bf16[128,1024]{0,1:T(8,128)(2,1)S(1)} %fusion.15), channel_id=1, source_target_pairs={{0,16},{16,0},{1,17},{17,1},{2,18},{18,2},{3,19},{19,3},{4,20},{20... | collective-permute-start | bytes 786440 | tf_op jit(solution)/shard_map/ppermute | solution.py:466
  507.0 19.3 %all-to-all-start.10 = ((bf16[16,128,128]{1,2,0:T(8,128)(2,1)}), bf16[16,128,128]{1,2,0:T(8,128)(2,1)S(1)}, u32[]{:S(2)}, u32[]{:S(2)}) async-start(bf16[16,128,128]{1,2,0:T(8,128)(2,1)} %copy.139), calls=%async_computation.10 | async-start | bytes 1048576 | tf_op jit(solution)/shard_map/all_to_all | solution.py:968
  526.4 5.2 collective-permute-start.36
  526.5 6.7 %collective-permute-start.37 = (bf16[2,2,2,1,416,128]{5,4,3,2,1,0:T(8,128)(2,1)S(1)}, bf16[2,2,2,1,416,128]{5,4,3,2,1,0:T(8,128)(2,1)}, u32[]{:S(2)}, u32[]{:S(2)}) collective-permute-start(bf16[2,2,2,1,416,128]{5,4,3,2,1,0:T(8,128)(2,1)S(1)} %maximum_select_fusion.8), channel_id=1, source_target_pairs={{0,2},{2,0},{1,3},{3,1},{4,6},{6,4},{5,7},{7,5},{8,10},{10,8},{9,1... | collective-permute-start | bytes 2555912 | tf_op jit(solution)/shard_map/ppermute | solution.py:466
  (62 other events, 269.6 us)

commit v5 on v4

--- a/solution.py
+++ b/solution.py
@@ -781,28 +781,37 @@
     )(where, rows, grads, up_weight, down_weight)
 
 
-def assemble(first, second, qkv_out, out_out, beside_out, gain_out):
+def assemble(
+    core, first_own, first_next, second_own, second_next, qkv_out, out_out, beside_out, gain_out
+):
     f32 = jnp.float32
+    even_own = core[0] == 0
+    total = jnp.zeros((16, 128), f32)
     for pair in range(8):
-        for source, rows, at in ((first, 400, 0), (second, 112, 400)):
-            left = source[2 * pair, :rows, :].astype(f32)
-            right = source[2 * pair + 1, :rows, :].astype(f32)
+        for own, following, rows, at in (
+            (first_own, first_next, 400, 0), (second_own, second_next, 112, 400),
+        ):
+            mine = own[pair, :rows, :].astype(f32)
+            other = following[pair, :rows, :].astype(f32)
+            left = jnp.where(even_own, mine, other)
+            right = jnp.where(even_own, other, mine)
             here = slice(at, at + rows)
             qkv_out[here, pair * 128 : (pair + 1) * 128] = jnp.concatenate(
                 [left[:, :64], right[:, :64]], 1
             )
             qkv_out[here, 1024 + pair * 64 : 1024 + (pair + 1) * 64] = left[:, 64:]
             qkv_out[here, 1536 + pair * 64 : 1536 + (pair + 1) * 64] = right[:, 64:]
-    total = jnp.zeros((16, 128), f32)
-    for device in range(16):
-        bits = [(device >> n) & 1 for n in range(4)]
-        at = bits[0] * 256 + bits[1] * 128 + bits[2] * 64 + bits[3] * 32
-        for part in range(8):
-            out_out[at : at + 32, part * 128 : (part + 1) * 128] = second[
-                device, 112 + part * 32 : 144 + part * 32, :
-            ].astype(f32)
-        beside_out[at : at + 32, :] = second[device, 368:400, :].astype(f32)
-        total = total + second[device, 400:416, :].astype(f32)
+        mine = second_own[pair, 112:, :].astype(f32)
+        other = second_next[pair, 112:, :].astype(f32)
+        for odd in range(2):
+            rest = jnp.where(even_own == (odd == 0), mine, other)
+            at = odd * 256 + (pair & 1) * 128 + ((pair >> 1) & 1) * 64 + (pair >> 2) * 32
+            for part in range(8):
+                out_out[at : at + 32, part * 128 : (part + 1) * 128] = rest[
+                    part * 32 : part * 32 + 32, :
+                ]
+            beside_out[at : at + 32, :] = rest[256:288, :]
+            total = total + rest[288:304, :]
     gain_out[...] = total[:8, :] + total[8:, :]
 
 
@@ -1142,8 +1151,10 @@
     grad_expert_in = expert_grads[:, :64].astype(f32)
     grad_expert_out = expert_grads[:, 64:].astype(f32)
     first, second, grad_projected = together(first, second, grad_projected)
-    first = gather_step(first, "d")
-    second = gather_step(second, "d")
+    first = first.reshape(8, 400, 128)
+    second = second.reshape(8, 416, 128)
+    first_next = swap(first, "d")
+    second_next = swap(second, "d")
 
     grad_projected = grad_projected.transpose(1, 0, 2)
     grad_kv = grad_projected[:, :, 64:].reshape(rows, 8, 2, 64)
@@ -1162,7 +1173,7 @@
     )
     share_qkv, share_out, beside, gain_sum = whole_call(
         assemble,
-        0,
+        1,
         [
             jax.ShapeDtypeStruct((512, 2048), f32),
             jax.ShapeDtypeStruct((512, 1024), f32),
@@ -1171,7 +1182,7 @@
         ],
         [],
         32 << 20,
-    )(first.reshape(16, 400, 128), second.reshape(16, 416, 128))
+    )(idd.astype(jnp.int32)[None], first, first_next, second, second_next)
     share_router = beside[:, :E]
     share_two = beside[:, E]
     share_one = gain_sum[:4].reshape(512) / attn_gain.astype(f32)

time: 551 us -> 556 us (level)
    unnamed x160 -> x148, local copies, waits for them, and re-layouts: 10.3 us -> 12.4 us
    select_n x22 -> x20, other arithmetic: 21 us -> 22 us  [in_order(): jnp.where(first, jnp.concatenate([mine, other], dim), jnp.concatenate([ot...]
  transfers between devices with their start and end apart: 48 -> 48, of which waited for: 28 -> 28; matrix products, arithmetic and copies ran while one was open for 22% -> 23% of each run, Pallas kernels for 8% -> 8%
where the time goes in v5:
time: 556 us; the launch traced here: 545 us
  waiting for transfers between devices  217 us (39%)
  starting transfers between devices  98.5 us (18%)
  other arithmetic  65.8 us (12%)
  Pallas kernels  55.5 us (10%)
  matrix products  40.5 us (7%)
  local copies, waits for them, and re-layouts  37.2 us (7%)
  blocking collectives  28.4 us (5%)
    ppermute x38, waiting for transfers between devices, swap(): return lax.ppermute(value, axis, [(0, 1), (1, 0)])  157 us
    all_to_all x5, waiting for transfers between devices, exchange(): return lax.all_to_all(sent, HALF, split_axis=0, concat_axis=0, tiled=True)  42.2 us
    pallas_call x3, Pallas kernels, run(): pl.pallas_call(kernel, out_shape=outs, grid_spec=pltpu.PrefetchScalarGrid...  36.7 us
    ppermute x38, starting transfers between devices, swap(): return lax.ppermute(value, axis, [(0, 1), (1, 0)])  36.6 us
    all_to_all x1, blocking collectives, exchange(): return lax.all_to_all(sent, HALF, split_axis=0, concat_axis=0, tiled=True)  28.4 us
    all_to_all x3, starting transfers between devices, to_tokens(): lax.all_to_all(value_heads.reshape(16, rows, -1), CTX, split_axis=0, conc...  25.6 us
    all_to_all x5, starting transfers between devices, exchange(): return lax.all_to_all(sent, HALF, split_axis=0, concat_axis=0, tiled=True)  24.1 us
    select_n x20, other arithmetic, in_order(): jnp.where(first, jnp.concatenate([mine, other], dim), jnp.concatenate([ot...  22 us
  transfers between devices with their start and end apart: 48, of which 28 were waited for; matrix products, arithmetic and copies ran while one was open for 23% of the time, Pallas kernels for 8%

profile of v5, /device:TPU:0, one launch (start us, length us, event | category | flops | bytes accessed | tf_op | source)
XLA Modules:
  0.0 545.0 jit_solution(3408945747285177934)
XLA Ops:
  0.7 3.0 collective-permute-start
  5.8 2.7 collective-permute-start.2
  11.2 3.7 pad_maximum_fusion
  14.9 9.9 %collective-permute-done.1 = bf16[1,1,1,1,128,1024]{4,5,3,2,1,0:T(8,128)(2,1)S(1)} collective-permute-done((bf16[1,1,1,1,128,1024]{4,5,3,2,1,0:T(8,128)(2,1)S(1)}, bf16[1,1,1,1,128,1024]{4,5,3,2,1,0:T(8,128)(2,1)S(1)}, u32[]{:S(2)}, u32[]{:S(2)}) %collective-permute-start.1) | collective-permute-done | bytes 262176 | tf_op jit(solution)/shard_map/ppermute | solution.py:466
  29.0 3.2 collective-permute-done.6
  44.4 2.8 collective-permute-done.7
  49.0 4.9 collective-permute-done.8
  53.9 2.8 maximum_select_fusion.4
  57.3 5.4 all-to-all-start
  69.6 3.1 convert_reduce_fusion
  80.1 2.7 convolution_convert_fusion.3
  82.8 2.5 maximum_select_fusion.11.weight
  95.2 2.3 maximum_select_fusion.1
  99.5 17.3 %shard_map.187 = (bf16[2048,128]{1,0:T(8,128)(2,1)}, bf16[2048,128]{1,0:T(8,128)(2,1)}, bf16[2048,128]{1,0:T(8,128)(2,1)}, f32[72,2048]{1,0:T(8,128)}, bf16[2048,64]{1,0:T(8,128)(2,1)}) custom-call(s32[32]{0:T(128)} %copy-done.66, s32[32]{0:T(128)} %select_reduce_fusion.1.h_place, s32[8]{0:T(128)} %and_select_fusion.first_key, bf16[1024,512]{1,0:T(8,128)(2,1)} %bitcast.185, ...), custom_call_target="tpu_custom_call" | custom-call | tf_op jit(solution)/shard_map/pallas_call | solution.py:821
  116.8 5.3 all-to-all-done
  124.0 15.4 %all-to-all-start.1 = ((bf16[16,128,64]{1,2,0:T(8,128)(2,1)}), bf16[16,128,64]{1,2,0:T(8,128)(2,1)S(1)}, u32[]{:S(2)}, u32[]{:S(2)}) async-start(bf16[16,128,64]{1,2,0:T(8,128)(2,1)} %copy.112), calls=%async_computation.1 | async-start | bytes 524288 | tf_op jit(solution)/shard_map/all_to_all | solution.py:977
  142.7 2.5 collective-permute-done.19
  145.2 4.3 all-to-all-done.1
  150.3 4.0 all-to-all-start.2
  155.5 2.7 multiply_reduce_fusion.2
  164.3 2.5 maximum_select_fusion.2
  166.9 3.6 maximum_select_fusion
  170.5 27.9 %collective-permute-done.21 = bf16[128,1152]{0,1:T(8,128)(2,1)} collective-permute-done((bf16[128,1152]{0,1:T(8,128)(2,1)S(1)}, bf16[128,1152]{0,1:T(8,128)(2,1)}, u32[]{:S(2)}, u32[]{:S(2)}) %collective-permute-start.21) | collective-permute-done | bytes 294944 | tf_op jit(solution)/shard_map/ppermute | solution.py:466
  200.2 5.8 %all-to-all-start.3 = ((bf16[16,48,1152]{2,1,0:T(8,128)(2,1)}), bf16[16,48,1152]{2,1,0:T(8,128)(2,1)}, u32[]{:S(2)}, u32[]{:S(2)}) async-start(bf16[16,48,1152]{2,1,0:T(8,128)(2,1)} %convolution_convert_fusion.1), calls=%async_computation.3 | async-start | bytes 3538944 | tf_op jit(solution)/shard_map/all_to_all | solution.py:911
  206.0 3.1 slice.136
  209.1 2.3 slice.137
  211.5 2.8 convolution_convert_fusion
  214.3 15.1 %all-to-all-done.3 = bf16[16,48,1152]{2,1,0:T(8,128)(2,1)} async-done(((bf16[16,48,1152]{2,1,0:T(8,128)(2,1)}), bf16[16,48,1152]{2,1,0:T(8,128)(2,1)}, u32[]{:S(2)}, u32[]{:S(2)}) %all-to-all-start.3) | async-done | bytes 1769504 | tf_op jit(solution)/shard_map/all_to_all | solution.py:911
  229.4 4.8 all-to-all-start.4
  234.2 9.4 %shard_map.188 = (bf16[768,1152]{1,0:T(8,128)(2,1)}, bf16[768,1024]{1,0:T(8,128)(2,1)}, bf16[768,512]{1,0:T(8,128)(2,1)}, bf16[768,1024]{1,0:T(8,128)(2,1)}, bf16[768,1024]{1,0:T(8,128)(2,1)}) custom-call(s32[1]{0:T(128)} %bitcast.33.where, bf16[768,1152]{1,0:T(8,128)(2,1)} %bitcast.38.rows, bf16[16,2,48,1024]{3,2,1,0:T(8,128)(2,1)} %bitcast.175, ...), custom_call_target="tpu_custom_call" | custom-call | tf_op jit(solution)/shard_map/pallas_call | solution.py:766
  243.6 13.9 %all-to-all-done.4 = bf16[16,48,1152]{2,1,0:T(8,128)(2,1)S(1)} async-done(((bf16[16,48,1152]{2,1,0:T(8,128)(2,1)}), bf16[16,48,1152]{2,1,0:T(8,128)(2,1)S(1)}, u32[]{:S(2)}, u32[]{:S(2)}) %all-to-all-start.4) | async-done | bytes 1769504 | tf_op jit(solution)/shard_map/all_to_all | solution.py:911
  258.7 9.4 %shard_map.189 = (bf16[768,1152]{1,0:T(8,128)(2,1)}, bf16[768,1024]{1,0:T(8,128)(2,1)}, bf16[768,512]{1,0:T(8,128)(2,1)}, bf16[768,1024]{1,0:T(8,128)(2,1)}, bf16[768,1024]{1,0:T(8,128)(2,1)}) custom-call(s32[1]{0:T(128)} %bitcast.33.where, bf16[768,1152]{1,0:T(8,128)(2,1)} %bitcast.187, bf16[16,2,48,1024]{3,2,1,0:T(8,128)(2,1)} %bitcast.176, ...), custom_call_target="tpu_custom_call" | custom-call | tf_op jit(solution)/shard_map/pallas_call | solution.py:766
  268.1 28.4 %all_to_all.55 = bf16[16,48,1152]{2,1,0:T(8,128)(2,1)S(1)} all-to-all(bf16[16,48,1152]{2,1,0:T(8,128)(2,1)} %bitcast.203), channel_id=1, replica_groups=mesh['a'=2,'b'=2,'c'=2,'d'=2,'f'=2] {'b','c','d','f'}, dimensions={0} | all-to-all | bytes 3538944 | tf_op jit(solution)/shard_map/all_to_all | solution.py:911
  296.6 4.8 all-to-all-start.6
  301.4 2.8 fusion.90
  304.2 3.4 fusion.3
  314.9 15.0 %collective-permute-done.22 = bf16[128,1152]{0,1:T(8,128)(2,1)S(1)} collective-permute-done((bf16[128,1152]{0,1:T(8,128)(2,1)S(1)}, bf16[128,1152]{0,1:T(8,128)(2,1)S(1)}, u32[]{:S(2)}, u32[]{:S(2)}) %collective-permute-start.22) | collective-permute-done | bytes 294944 | tf_op jit(solution)/shard_map/ppermute | solution.py:466
  330.9 2.2 fusion
  337.7 5.2 all-to-all-start.7
  343.0 3.5 pad_maximum_fusion.3
  346.5 6.5 %all-to-all-done.7 = bf16[16,128,64]{1,2,0:T(8,128)(2,1)S(1)} async-done(((bf16[16,128,64]{1,2,0:T(8,128)(2,1)}), bf16[16,128,64]{1,2,0:T(8,128)(2,1)S(1)}, u32[]{:S(2)}, u32[]{:S(2)}) %all-to-all-start.7) | async-done | bytes 262176 | tf_op jit(solution)/shard_map/all_to_all | solution.py:977
  354.1 4.8 all-to-all-start.8
  363.8 14.6 %shard_map.190 = (f32[2048,128]{1,0:T(8,128)}, bf16[2048,128]{1,0:T(8,128)(2,1)}) custom-call(s32[32]{0:T(128)} %copy-done.66, s32[8]{0:T(128)} %and_select_fusion.first_key, s32[1]{0:T(128)} %bitcast.55.core, bf16[2048,128]{1,0:T(8,128)(2,1)} %get-tuple-element.159.query, bf16[2048,128]{1,0:T(8,128)(2,1)} %get-tuple-element.160.key, ...), custom_call_target="tpu_custom_call" | custom-call | tf_op jit(solution)/shard_map/pallas_call | solution.py:821
  378.8 3.3 collective-permute-done.24
  383.5 2.2 convert_add_fusion
  388.2 10.3 %all-to-all-done.8 = bf16[16,96,1024]{2,1,0:T(8,128)(2,1)} async-done(((bf16[16,96,1024]{2,1,0:T(8,128)(2,1)}), bf16[16,96,1024]{2,1,0:T(8,128)(2,1)}, u32[]{:S(2)}, u32[]{:S(2)}) %all-to-all-start.8) | async-done | bytes 3145760 | tf_op jit(solution)/shard_map/all_to_all | solution.py:911
  398.5 6.8 %all-to-all-start.9 = ((bf16[16,96,1024]{2,1,0:T(8,128)(2,1)}), bf16[16,96,1024]{2,1,0:T(8,128)(2,1)}, u32[]{:S(2)}, u32[]{:S(2)}) async-start(bf16[16,96,1024]{2,1,0:T(8,128)(2,1)} %pad_maximum_fusion.2), calls=%async_computation.9 | async-start | bytes 6291456 | tf_op jit(solution)/shard_map/all_to_all | solution.py:1123
  407.8 6.7 %collective-permute-done.27 = bf16[256,1152]{1,0:T(8,128)(2,1)} collective-permute-done((bf16[256,1152]{1,0:T(8,128)(2,1)}, bf16[256,1152]{1,0:T(8,128)(2,1)}, u32[]{:S(2)}, u32[]{:S(2)}) %collective-permute-start.27) | collective-permute-done | bytes 589856 | tf_op jit(solution)/shard_map/ppermute | solution.py:466
  416.9 21.0 %collective-permute-done.28 = bf16[128,1152]{1,0:T(8,128)(2,1)S(1)} collective-permute-done((bf16[128,1152]{1,0:T(8,128)(2,1)S(1)}, bf16[128,1152]{1,0:T(8,128)(2,1)S(1)}, u32[]{:S(2)}, u32[]{:S(2)}) %collective-permute-start.28) | collective-permute-done | bytes 294944 | tf_op jit(solution)/shard_map/ppermute | solution.py:466
  438.4 21.9 %collective-permute-done.29 = bf16[64,1152]{1,0:T(8,128)(2,1)S(1)} collective-permute-done((bf16[64,1152]{1,0:T(8,128)(2,1)S(1)}, bf16[64,1152]{1,0:T(8,128)(2,1)S(1)}, u32[]{:S(2)}, u32[]{:S(2)}) %collective-permute-start.29) | collective-permute-done | bytes 147488 | tf_op jit(solution)/shard_map/ppermute | solution.py:466
  460.4 4.6 collective-permute-start.30
  465.0 15.1 %collective-permute-done.30 = bf16[32,1152]{1,0:T(8,128)(2,1)S(1)} collective-permute-done((bf16[32,1152]{1,0:T(8,128)(2,1)S(1)}, bf16[32,1152]{1,0:T(8,128)(2,1)S(1)}, u32[]{:S(2)}, u32[]{:S(2)}) %collective-permute-start.30) | collective-permute-done | bytes 73760 | tf_op jit(solution)/shard_map/ppermute | solution.py:466
  480.3 10.9 %collective-permute-done.31 = bf16[1,1,1,1,816,128]{5,4,3,2,1,0:T(8,128)(2,1)S(1)} collective-permute-done((bf16[1,1,1,1,816,128]{5,4,3,2,1,0:T(8,128)(2,1)S(1)}, bf16[1,1,1,1,816,128]{5,4,3,2,1,0:T(8,128)(2,1)S(1)}, u32[]{:S(2)}, u32[]{:S(2)}) %collective-permute-start.31) | collective-permute-done | bytes 208928 | tf_op jit(solution)/shard_map/ppermute | solution.py:466
  492.9 5.5 %collective-permute-done.32 = bf16[2,1,1,1,400,128]{5,4,0,3,2,1:T(8,128)(2,1)S(1)} collective-permute-done((bf16[2,1,1,1,400,128]{5,4,0,3,2,1:T(8,128)(2,1)S(1)}, bf16[2,1,1,1,400,128]{5,4,0,3,2,1:T(8,128)(2,1)S(1)}, u32[]{:S(2)}, u32[]{:S(2)}) %collective-permute-start.32) | collective-permute-done | bytes 204832 | tf_op jit(solution)/shard_map/ppermute | solution.py:466
  501.4 2.1 fusion.15
  503.5 2.6 collective-permute-start.23
  506.2 3.0 collective-permute-done.33
  510.2 4.9 all-to-all-start.10
  515.2 2.2 collective-permute-done.35
  518.7 2.1 fusion.37
  521.6 2.8 slice_convert_fusion.1
  524.4 4.1 slice_convert_fusion
  531.3 3.4 fusion.22
  537.8 4.9 shard_map.191
  (329 shorter events, 109.9 us)
Async XLA Ops:
  0.7 9.2 %collective-permute-start = (bf16[512]{0:T(512)(128)(2,1)}, bf16[512]{0:T(512)(128)(2,1)S(1)}, u32[]{:S(2)}, u32[]{:S(2)}) collective-permute-start(bf16[512]{0:T(512)(128)(2,1)} %param.16), channel_id=1, source_target_pairs={{0,1},{1,0},{2,3},{3,2},{4,5},{5,4},{6,7},{7,6},{8,9},{9,8},{10,11... | collective-permute-start | bytes 3080 | tf_op jit(solution)/shard_map/ppermute | solution.py:466
  5.8 5.4 collective-permute-start.2
  9.6 145.9 %copy-start.13 = (bf16[1,128,1024]{1,2,0:T(8,128)(2,1)}, bf16[1,128,1024]{1,2,0:T(8,128)(2,1)S(1)}, u32[]{:S(2)}) copy-start(bf16[1,128,1024]{1,2,0:T(8,128)(2,1)S(1)} %copy.101) | copy-start | bytes 786436
  10.8 14.1 %collective-permute-start.1 = (bf16[1,1,1,1,128,1024]{4,5,3,2,1,0:T(8,128)(2,1)S(1)}, bf16[1,1,1,1,128,1024]{4,5,3,2,1,0:T(8,128)(2,1)S(1)}, u32[]{:S(2)}, u32[]{:S(2)}) collective-permute-start(bf16[1,1,1,1,128,1024]{4,5,3,2,1,0:T(8,128)(2,1)S(1)} %bitcast.207), channel_id=1, source_target_pairs={{0,16},{16,0},{1,17},{17,1},{2,18},{18,2},{3,19},{19,3},{4,20},{20... | collective-permute-start | bytes 786440 | tf_op jit(solution)/shard_map/ppermute | solution.py:466
  25.0 7.9 %collective-permute-start.4 = (bf16[2,1,1,1,128,512]{4,5,3,2,1,0:T(8,128)(2,1)S(1)}, bf16[2,1,1,1,128,512]{4,5,3,2,1,0:T(8,128)(2,1)S(1)}, u32[]{:S(2)}, u32[]{:S(2)}) collective-permute-start(bf16[2,1,1,1,128,512]{4,5,3,2,1,0:T(8,128)(2,1)S(1)} %get-tuple-element.224), channel_id=1, source_target_pairs={{0,4},{4,0},{1,5},{5,1},{2,6},{6,2},{3,7},{7,3},{8,12},{12,8},{9,1... | collective-permute-start | bytes 786440 | tf_op jit(solution)/shard_map/ppermute | solution.py:466
  27.6 55.2 %copy-start.27 = (bf16[512,64]{1,0:T(8,128)(2,1)}, bf16[512,64]{1,0:T(8,128)(2,1)S(1)}, u32[]{:S(2)}) copy-start(bf16[512,64]{1,0:T(8,128)(2,1)S(1)} %get-tuple-element.219) | copy-start | bytes 196612
  27.6 6.9 %collective-permute-start.3 = (bf16[2,1,1,1,128,512]{4,5,3,2,1,0:T(8,128)(2,1)S(1)}, bf16[2,1,1,1,128,512]{4,5,3,2,1,0:T(8,128)(2,1)S(1)}, u32[]{:S(2)}, u32[]{:S(2)}) collective-permute-start(bf16[2,1,1,1,128,512]{4,5,3,2,1,0:T(8,128)(2,1)S(1)} %get-tuple-element.225), channel_id=1, source_target_pairs={{0,8},{8,0},{1,9},{9,1},{2,10},{10,2},{3,11},{11,3},{4,12},{12,4},... | collective-permute-start | bytes 786440 | tf_op jit(solution)/shard_map/ppermute | solution.py:466
  27.6 4.7 collective-permute-start.6
  28.4 6.9 %collective-permute-start.5 = (bf16[512,256]{1,0:T(8,128)(2,1)S(1)}, bf16[512,256]{1,0:T(8,128)(2,1)S(1)}, u32[]{:S(2)}, u32[]{:S(2)}) collective-permute-start(bf16[512,256]{1,0:T(8,128)(2,1)S(1)} %pad_maximum_fusion.8), channel_id=1, source_target_pairs={{0,1},{1,0},{2,3},{3,2},{4,5},{5,4},{6,7},{7,6},{8,9},{9,8},{10,11... | collective-permute-start | bytes 786440 | tf_op jit(solution)/shard_map/ppermute | solution.py:466
  35.4 11.9 %collective-permute-start.7 = (bf16[2,2,1,1,128,512]{4,5,3,2,1,0:T(8,128)(2,1)}, bf16[2,2,1,1,128,512]{4,5,3,2,1,0:T(8,128)(2,1)}, u32[]{:S(2)}, u32[]{:S(2)}) collective-permute-start(bf16[2,2,1,1,128,512]{4,5,3,2,1,0:T(8,128)(2,1)} %maximum_select_fusion.9), channel_id=1, source_target_pairs={{0,4},{4,0},{1,5},{5,1},{2,6},{6,2},{3,7},{7,3},{8,12},{12,8},{9,1... | collective-permute-start | bytes 1572872 | tf_op jit(solution)/shard_map/ppermute | solution.py:466
  36.6 17.3 %collective-permute-start.8 = (bf16[2,1,2,1,128,512]{4,5,3,2,1,0:T(8,128)(2,1)}, bf16[2,1,2,1,128,512]{4,5,3,2,1,0:T(8,128)(2,1)}, u32[]{:S(2)}, u32[]{:S(2)}) collective-permute-start(bf16[2,1,2,1,128,512]{4,5,3,2,1,0:T(8,128)(2,1)} %maximum_select_fusion.10), channel_id=1, source_target_pairs={{0,8},{8,0},{1,9},{9,1},{2,10},{10,2},{3,11},{11,3},{4,12},{12,4},... | collective-permute-start | bytes 1572872 | tf_op jit(solution)/shard_map/ppermute | solution.py:466
  39.2 18.1 %collective-permute-start.11 = (bf16[256,1024]{1,0:T(8,128)(2,1)}, bf16[256,1024]{1,0:T(8,128)(2,1)}, u32[]{:S(2)}, u32[]{:S(2)}) collective-permute-start(bf16[256,1024]{1,0:T(8,128)(2,1)} %slice_select_fusion.1), channel_id=1, source_target_pairs={{0,1},{1,0},{2,3},{3,2},{4,5},{5,4},{6,7},{7,6},{8,9},{9,8},{10,11... | collective-permute-start | bytes 1572872 | tf_op jit(solution)/shard_map/ppermute | solution.py:466
  41.5 15.8 %collective-permute-start.9 = (bf16[128,1024]{0,1:T(8,128)(2,1)}, bf16[128,1024]{0,1:T(8,128)(2,1)}, u32[]{:S(2)}, u32[]{:S(2)}) collective-permute-start(bf16[128,1024]{0,1:T(8,128)(2,1)} %bitcast.7), channel_id=1, source_target_pairs={{0,16},{16,0},{1,17},{17,1},{2,18},{18,2},{3,19},{19,3},{4,20},{20... | collective-permute-start | bytes 786440 | tf_op jit(solution)/shard_map/ppermute | solution.py:466
  42.7 14.0 %collective-permute-start.10 = (f32[128,32]{0,1:T(8,128)S(1)}, f32[128,32]{0,1:T(8,128)S(1)}, u32[]{:S(2)}, u32[]{:S(2)}) collective-permute-start(f32[128,32]{0,1:T(8,128)S(1)} %get-tuple-element.106), channel_id=1, source_target_pairs={{0,16},{16,0},{1,17},{17,1},{2,18},{18,2},{3,19},{19,3},{4,20},{20... | collective-permute-start | bytes 49160 | tf_op jit(solution)/shard_map/ppermute | solution.py:466
  57.3 64.8 %all-to-all-start = ((bf16[16,96,1024]{2,1,0:T(8,128)(2,1)}), bf16[16,96,1024]{2,1,0:T(8,128)(2,1)}, u32[]{:S(2)}, u32[]{:S(2)}) async-start(bf16[16,96,1024]{2,1,0:T(8,128)(2,1)} %pad_maximum_fusion), calls=%async_computation | async-start | bytes 6291456 | tf_op jit(solution)/shard_map/all_to_all | solution.py:926
  74.0 14.6 %collective-permute-start.14 = (bf16[512]{0:T(512)(128)(2,1)}, bf16[512]{0:T(512)(128)(2,1)}, u32[]{:S(2)}, u32[]{:S(2)}) collective-permute-start(bf16[512]{0:T(512)(128)(2,1)} %param.19), channel_id=1, source_target_pairs={{0,1},{1,0},{2,3},{3,2},{4,5},{5,4},{6,7},{7,6},{8,9},{9,8},{10,11... | collective-permute-start | bytes 3080 | tf_op jit(solution)/shard_map/ppermute | solution.py:466
  74.0 14.6 %collective-permute-start.15 = (bf16[512,32]{0,1:T(8,128)(2,1)}, bf16[512,32]{0,1:T(8,128)(2,1)}, u32[]{:S(2)}, u32[]{:S(2)}) collective-permute-start(bf16[512,32]{0,1:T(8,128)(2,1)} %param.20), channel_id=1, source_target_pairs={{0,1},{1,0},{2,3},{3,2},{4,5},{5,4},{6,7},{7,6},{8,9},{9,8},{10,11... | collective-permute-start | bytes 98312 | tf_op jit(solution)/shard_map/ppermute | solution.py:466
  88.0 9.5 %collective-permute-start.12 = (bf16[1024,512]{1,0:T(8,128)(2,1)}, bf16[1024,512]{1,0:T(8,128)(2,1)S(1)}, u32[]{:S(2)}, u32[]{:S(2)}) collective-permute-start(bf16[1024,512]{1,0:T(8,128)(2,1)} %bitcast.184), channel_id=1, source_target_pairs={{0,2},{2,0},{1,3},{3,1},{4,6},{6,4},{5,7},{7,5},{8,10},{10,8},{9,1... | collective-permute-start | bytes 3145736 | tf_op jit(solution)/shard_map/ppermute | solution.py:466
  88.1 9.4 %collective-permute-start.13 = (bf16[1024,512]{1,0:T(8,128)(2,1)S(1)}, bf16[1024,512]{1,0:T(8,128)(2,1)S(1)}, u32[]{:S(2)}, u32[]{:S(2)}) collective-permute-start(bf16[1024,512]{1,0:T(8,128)(2,1)S(1)} %bitcast.181), channel_id=1, source_target_pairs={{0,2},{2,0},{1,3},{3,1},{4,6},{6,4},{5,7},{7,5},{8,10},{10,8},{9,1... | collective-permute-start | bytes 3145736 | tf_op jit(solution)/shard_map/ppermute | solution.py:466
  89.7 27.1 %collective-permute-start.17 = (bf16[256,2048]{1,0:T(8,128)(2,1)}, bf16[256,2048]{1,0:T(8,128)(2,1)}, u32[]{:S(2)}, u32[]{:S(2)}) collective-permute-start(bf16[256,2048]{1,0:T(8,128)(2,1)} %slice_select_fusion), channel_id=1, source_target_pairs={{0,1},{1,0},{2,3},{3,2},{4,5},{5,4},{6,7},{7,6},{8,9},{9,8},{10,11... | collective-permute-start | bytes 3145736 | tf_op jit(solution)/shard_map/ppermute | solution.py:466
  89.7 3.7 collective-permute-start.16
  89.9 121.6 %copy-start.42 = (f32[128,2,1,8]{0,1,3,2:T(2,128)}, f32[128,2,1,8]{0,1,3,2:T(2,128)S(1)}, u32[]{:S(2)}) copy-start(f32[128,2,1,8]{0,1,3,2:T(2,128)S(1)} %copy_select_fusion) | copy-start | bytes 24580
  99.5 40.0 %copy-start.55 = (f32[2,1,2,1,1,32]{5,4,3,2,1,0:T(1,128)S(1)}, f32[2,1,2,1,1,32]{5,4,3,2,1,0:T(1,128)}, u32[]{:S(2)}) copy-start(f32[2,1,2,1,1,32]{5,4,3,2,1,0:T(1,128)} %broadcast_select_fusion.7) | copy-start | bytes 1540
  124.0 25.5 %all-to-all-start.1 = ((bf16[16,128,64]{1,2,0:T(8,128)(2,1)}), bf16[16,128,64]{1,2,0:T(8,128)(2,1)S(1)}, u32[]{:S(2)}, u32[]{:S(2)}) async-start(bf16[16,128,64]{1,2,0:T(8,128)(2,1)} %copy.112), calls=%async_computation.1 | async-start | bytes 524288 | tf_op jit(solution)/shard_map/all_to_all | solution.py:977
  139.5 1.3 collective-permute-start.18
  140.8 4.4 collective-permute-start.19
  150.3 50.0 %all-to-all-start.2 = ((bf16[16,96,1024]{2,1,0:T(8,128)(2,1)}), bf16[16,96,1024]{2,1,0:T(8,128)(2,1)S(1)}, u32[]{:S(2)}, u32[]{:S(2)}) async-start(bf16[16,96,1024]{2,1,0:T(8,128)(2,1)} %pad_maximum_fusion.1), calls=%async_computation.2 | async-start | bytes 6291456 | tf_op jit(solution)/shard_map/all_to_all | solution.py:911
  155.1 9.2 %collective-permute-start.20 = (bf16[256,2048]{1,0:T(8,128)(2,1)}, bf16[256,2048]{1,0:T(8,128)(2,1)S(1)}, u32[]{:S(2)}, u32[]{:S(2)}) collective-permute-start(bf16[256,2048]{1,0:T(8,128)(2,1)} %collective-permute-done.17), channel_id=1, source_target_pairs={{0,2},{2,0},{1,3},{3,1},{4,6},{6,4},{5,7},{7,5},{8,10},{10,8},{9,1... | collective-permute-start | bytes 3145736 | tf_op jit(solution)/shard_map/ppermute | solution.py:466
  161.3 37.1 %collective-permute-start.21 = (bf16[128,1152]{0,1:T(8,128)(2,1)S(1)}, bf16[128,1152]{0,1:T(8,128)(2,1)}, u32[]{:S(2)}, u32[]{:S(2)}) collective-permute-start(bf16[128,1152]{0,1:T(8,128)(2,1)S(1)} %maximum_maximum_fusion.1), channel_id=1, source_target_pairs={{0,16},{16,0},{1,17},{17,1},{2,18},{18,2},{3,19},{19,3},{4,20},{20... | collective-permute-start | bytes 884744 | tf_op jit(solution)/shard_map/ppermute | solution.py:466
  200.2 29.1 %all-to-all-start.3 = ((bf16[16,48,1152]{2,1,0:T(8,128)(2,1)}), bf16[16,48,1152]{2,1,0:T(8,128)(2,1)}, u32[]{:S(2)}, u32[]{:S(2)}) async-start(bf16[16,48,1152]{2,1,0:T(8,128)(2,1)} %convolution_convert_fusion.1), calls=%async_computation.3 | async-start | bytes 3538944 | tf_op jit(solution)/shard_map/all_to_all | solution.py:911
  229.4 28.1 %all-to-all-start.4 = ((bf16[16,48,1152]{2,1,0:T(8,128)(2,1)}), bf16[16,48,1152]{2,1,0:T(8,128)(2,1)S(1)}, u32[]{:S(2)}, u32[]{:S(2)}) async-start(bf16[16,48,1152]{2,1,0:T(8,128)(2,1)} %convolution_convert_fusion), calls=%async_computation.4 | async-start | bytes 3538944 | tf_op jit(solution)/shard_map/all_to_all | solution.py:911
  296.6 34.3 %all-to-all-start.6 = ((bf16[16,48,1152]{2,1,0:T(8,128)(2,1)}), bf16[16,48,1152]{2,1,0:T(8,128)(2,1)}, u32[]{:S(2)}, u32[]{:S(2)}) async-start(bf16[16,48,1152]{2,1,0:T(8,128)(2,1)} %bitcast.42), calls=%async_computation.6 | async-start | bytes 3538944 | tf_op jit(solution)/shard_map/all_to_all | solution.py:911
  310.5 19.4 %collective-permute-start.22 = (bf16[128,1152]{0,1:T(8,128)(2,1)S(1)}, bf16[128,1152]{0,1:T(8,128)(2,1)S(1)}, u32[]{:S(2)}, u32[]{:S(2)}) collective-permute-start(bf16[128,1152]{0,1:T(8,128)(2,1)S(1)} %fusion.1), channel_id=1, source_target_pairs={{0,16},{16,0},{1,17},{17,1},{2,18},{18,2},{3,19},{19,3},{4,20},{20... | collective-permute-start | bytes 884744 | tf_op jit(solution)/shard_map/ppermute | solution.py:466
  312.9 18.0 %copy-start.41 = (f32[128,2,1,8]{0,1,3,2:T(2,128)S(1)}, f32[128,2,1,8]{0,1,3,2:T(2,128)}, u32[]{:S(2)}) copy-start(f32[128,2,1,8]{0,1,3,2:T(2,128)} %copy-done.39) | copy-start | bytes 24580
  314.8 18.3 %copy-start.37 = (pred[128,32]{0,1:T(8,128)(4,1)S(1)}, pred[128,32]{0,1:T(8,128)(4,1)}, u32[]{:S(2)}) copy-start(pred[128,32]{0,1:T(8,128)(4,1)} %copy-done.35) | copy-start | bytes 12292
  314.9 18.3 %copy-start.48 = (pred[128,32]{0,1:T(8,128)(4,1)S(1)}, pred[128,32]{0,1:T(8,128)(4,1)}, u32[]{:S(2)}) copy-start(pred[128,32]{0,1:T(8,128)(4,1)} %copy-done.47) | copy-start | bytes 12292
  314.9 18.3 %copy-start.52 = (f32[128]{0:T(128)S(1)}, f32[128]{0:T(128)}, u32[]{:S(2)}) copy-start(f32[128]{0:T(128)} %copy-done.51) | copy-start | bytes 1540
  314.9 18.3 %copy-start.54 = (f32[128]{0:T(128)S(1)}, f32[128]{0:T(128)}, u32[]{:S(2)}) copy-start(f32[128]{0:T(128)} %copy-done.53) | copy-start | bytes 1540
  314.9 18.4 %copy-start.3 = (f32[128,1024]{0,1:T(8,128)S(1)}, f32[128,1024]{0,1:T(8,128)}, u32[]{:S(2)}) copy-start(f32[128,1024]{0,1:T(8,128)} %copy-done.2) | copy-start | bytes 1572868
  314.9 18.4 %copy-start.45 = (f32[1024]{0:T(1024)S(1)}, f32[1024]{0:T(1024)}, u32[]{:S(2)}) copy-start(f32[1024]{0:T(1024)} %copy-done.44) | copy-start | bytes 12292
  314.9 18.4 %copy-start.50 = (bf16[512,32]{0,1:T(8,128)(2,1)S(1)}, bf16[512,32]{0,1:T(8,128)(2,1)}, u32[]{:S(2)}) copy-start(bf16[512,32]{0,1:T(8,128)(2,1)} %param.20) | copy-start | bytes 98308
  314.9 18.4 %copy-start.61 = (f32[128]{0:T(128)S(1)}, f32[128]{0:T(128)}, u32[]{:S(2)}) copy-start(f32[128]{0:T(128)} %copy-done.60) | copy-start | bytes 1540
  337.7 15.3 %all-to-all-start.7 = ((bf16[16,128,64]{1,2,0:T(8,128)(2,1)}), bf16[16,128,64]{1,2,0:T(8,128)(2,1)S(1)}, u32[]{:S(2)}, u32[]{:S(2)}) async-start(bf16[16,128,64]{1,2,0:T(8,128)(2,1)} %bitcast.48), calls=%async_computation.7 | async-start | bytes 524288 | tf_op jit(solution)/shard_map/all_to_all | solution.py:977
  354.1 44.5 %all-to-all-start.8 = ((bf16[16,96,1024]{2,1,0:T(8,128)(2,1)}), bf16[16,96,1024]{2,1,0:T(8,128)(2,1)}, u32[]{:S(2)}, u32[]{:S(2)}) async-start(bf16[16,96,1024]{2,1,0:T(8,128)(2,1)} %pad_maximum_fusion.3), calls=%async_computation.8 | async-start | bytes 6291456 | tf_op jit(solution)/shard_map/all_to_all | solution.py:911
  378.3 5.2 collective-permute-start.26
  378.7 3.4 collective-permute-start.24
  386.7 27.8 %collective-permute-start.27 = (bf16[256,1152]{1,0:T(8,128)(2,1)}, bf16[256,1152]{1,0:T(8,128)(2,1)}, u32[]{:S(2)}, u32[]{:S(2)}) collective-permute-start(bf16[256,1152]{1,0:T(8,128)(2,1)} %dynamic-slice_convert_fusion), channel_id=1, source_target_pairs={{0,1},{1,0},{2,3},{3,2},{4,5},{5,4},{6,7},{7,6},{8,9},{9,8},{10,11... | collective-permute-start | bytes 1769480 | tf_op jit(solution)/shard_map/ppermute | solution.py:466
  388.2 17.2 %copy-start.25 = (bf16[8,1,128,128]{3,2,1,0:T(8,128)(2,1)}, bf16[8,1,128,128]{3,2,1,0:T(8,128)(2,1)S(1)}, u32[]{:S(2)}) copy-start(bf16[8,1,128,128]{3,2,1,0:T(8,128)(2,1)S(1)} %get-tuple-element.223) | copy-start | bytes 786436
  398.5 110.7 %all-to-all-start.9 = ((bf16[16,96,1024]{2,1,0:T(8,128)(2,1)}), bf16[16,96,1024]{2,1,0:T(8,128)(2,1)}, u32[]{:S(2)}, u32[]{:S(2)}) async-start(bf16[16,96,1024]{2,1,0:T(8,128)(2,1)} %pad_maximum_fusion.2), calls=%async_computation.9 | async-start | bytes 6291456 | tf_op jit(solution)/shard_map/all_to_all | solution.py:1123
  415.7 22.2 %collective-permute-start.28 = (bf16[128,1152]{1,0:T(8,128)(2,1)S(1)}, bf16[128,1152]{1,0:T(8,128)(2,1)S(1)}, u32[]{:S(2)}, u32[]{:S(2)}) collective-permute-start(bf16[128,1152]{1,0:T(8,128)(2,1)S(1)} %dynamic-slice_convert_fusion.1), channel_id=1, source_target_pairs={{0,4},{4,0},{1,5},{5,1},{2,6},{6,2},{3,7},{7,3},{8,12},{12,8},{9,1... | collective-permute-start | bytes 884744 | tf_op jit(solution)/shard_map/ppermute | solution.py:466
  416.3 21.9 %copy-start.28 = (bf16[512,64]{1,0:T(8,128)(2,1)S(1)}, bf16[512,64]{1,0:T(8,128)(2,1)}, u32[]{:S(2)}) copy-start(bf16[512,64]{1,0:T(8,128)(2,1)} %copy-done.27) | copy-start | bytes 196612
  416.3 21.9 %copy-start.34 = (bf16[512,64]{1,0:T(8,128)(2,1)S(1)}, bf16[512,64]{1,0:T(8,128)(2,1)}, u32[]{:S(2)}) copy-start(bf16[512,64]{1,0:T(8,128)(2,1)} %get-tuple-element.212) | copy-start | bytes 196612
  416.8 21.3 %collective-permute-start.25 = (f32[512,128]{1,0:T(8,128)S(1)}, f32[512,128]{1,0:T(8,128)S(1)}, u32[]{:S(2)}, u32[]{:S(2)}) collective-permute-start(f32[512,128]{1,0:T(8,128)S(1)} %get-tuple-element.254), channel_id=1, source_target_pairs={{0,1},{1,0},{2,3},{3,2},{4,5},{5,4},{6,7},{7,6},{8,9},{9,8},{10,11... | collective-permute-start | bytes 786440 | tf_op jit(solution)/shard_map/ppermute | solution.py:466
  438.0 22.3 %collective-permute-start.29 = (bf16[64,1152]{1,0:T(8,128)(2,1)S(1)}, bf16[64,1152]{1,0:T(8,128)(2,1)S(1)}, u32[]{:S(2)}, u32[]{:S(2)}) collective-permute-start(bf16[64,1152]{1,0:T(8,128)(2,1)S(1)} %dynamic-slice_convert_fusion.2), channel_id=1, source_target_pairs={{0,8},{8,0},{1,9},{9,1},{2,10},{10,2},{3,11},{11,3},{4,12},{12,4},... | collective-permute-start | bytes 442376 | tf_op jit(solution)/shard_map/ppermute | solution.py:466
  460.4 19.7 %collective-permute-start.30 = (bf16[32,1152]{1,0:T(8,128)(2,1)S(1)}, bf16[32,1152]{1,0:T(8,128)(2,1)S(1)}, u32[]{:S(2)}, u32[]{:S(2)}) collective-permute-start(bf16[32,1152]{1,0:T(8,128)(2,1)S(1)} %dynamic-slice_convert_fusion.4), channel_id=1, source_target_pairs={{0,16},{16,0},{1,17},{17,1},{2,18},{18,2},{3,19},{19,3},{4,20},{20... | collective-permute-start | bytes 221192 | tf_op jit(solution)/shard_map/ppermute | solution.py:466
  480.2 11.0 %collective-permute-start.31 = (bf16[1,1,1,1,816,128]{5,4,3,2,1,0:T(8,128)(2,1)S(1)}, bf16[1,1,1,1,816,128]{5,4,3,2,1,0:T(8,128)(2,1)S(1)}, u32[]{:S(2)}, u32[]{:S(2)}) collective-permute-start(bf16[1,1,1,1,816,128]{5,4,3,2,1,0:T(8,128)(2,1)S(1)} %maximum_bitcast_fusion), channel_id=1, source_target_pairs={{0,16},{16,0},{1,17},{17,1},{2,18},{18,2},{3,19},{19,3},{4,20},{20... | collective-permute-start | bytes 626696 | tf_op jit(solution)/shard_map/ppermute | solution.py:466
  491.3 7.1 %collective-permute-start.32 = (bf16[2,1,1,1,400,128]{5,4,0,3,2,1:T(8,128)(2,1)S(1)}, bf16[2,1,1,1,400,128]{5,4,0,3,2,1:T(8,128)(2,1)S(1)}, u32[]{:S(2)}, u32[]{:S(2)}) collective-permute-start(bf16[2,1,1,1,400,128]{5,4,0,3,2,1:T(8,128)(2,1)S(1)} %get-tuple-element.230), channel_id=1, source_target_pairs={{0,8},{8,0},{1,9},{9,1},{2,10},{10,2},{3,11},{11,3},{4,12},{12,4},... | collective-permute-start | bytes 614408 | tf_op jit(solution)/shard_map/ppermute | solution.py:466
  491.5 8.4 %collective-permute-start.34 = (bf16[2,1,1,1,416,128]{5,4,0,3,2,1:T(8,128)(2,1)S(1)}, bf16[2,1,1,1,416,128]{5,4,0,3,2,1:T(8,128)(2,1)S(1)}, u32[]{:S(2)}, u32[]{:S(2)}) collective-permute-start(bf16[2,1,1,1,416,128]{5,4,0,3,2,1:T(8,128)(2,1)S(1)} %get-tuple-element.227), channel_id=1, source_target_pairs={{0,4},{4,0},{1,5},{5,1},{2,6},{6,2},{3,7},{7,3},{8,12},{12,8},{9,1... | collective-permute-start | bytes 638984 | tf_op jit(solution)/shard_map/ppermute | solution.py:466
  498.5 10.6 %collective-permute-start.33 = (bf16[2,2,1,1,400,128]{5,4,3,2,1,0:T(8,128)(2,1)S(1)}, bf16[2,2,1,1,400,128]{5,4,3,2,1,0:T(8,128)(2,1)S(1)}, u32[]{:S(2)}, u32[]{:S(2)}) collective-permute-start(bf16[2,2,1,1,400,128]{5,4,3,2,1,0:T(8,128)(2,1)S(1)} %maximum_select_fusion.16), channel_id=1, source_target_pairs={{0,4},{4,0},{1,5},{5,1},{2,6},{6,2},{3,7},{7,3},{8,12},{12,8},{9,1... | collective-permute-start | bytes 1228808 | tf_op jit(solution)/shard_map/ppermute | solution.py:466
  500.8 16.5 %collective-permute-start.35 = (bf16[2,1,2,1,416,128]{5,4,3,2,1,0:T(8,128)(2,1)}, bf16[2,1,2,1,416,128]{5,4,3,2,1,0:T(8,128)(2,1)}, u32[]{:S(2)}, u32[]{:S(2)}) collective-permute-start(bf16[2,1,2,1,416,128]{5,4,3,2,1,0:T(8,128)(2,1)} %maximum_select_fusion.13), channel_id=1, source_target_pairs={{0,8},{8,0},{1,9},{9,1},{2,10},{10,2},{3,11},{11,3},{4,12},{12,4},... | collective-permute-start | bytes 1277960 | tf_op jit(solution)/shard_map/ppermute | solution.py:466
  503.5 15.1 %collective-permute-start.23 = (bf16[128,1024]{0,1:T(8,128)(2,1)S(1)}, bf16[128,1024]{0,1:T(8,128)(2,1)}, u32[]{:S(2)}, u32[]{:S(2)}) collective-permute-start(bf16[128,1024]{0,1:T(8,128)(2,1)S(1)} %fusion.15), channel_id=1, source_target_pairs={{0,16},{16,0},{1,17},{17,1},{2,18},{18,2},{3,19},{19,3},{4,20},{20... | collective-permute-start | bytes 786440 | tf_op jit(solution)/shard_map/ppermute | solution.py:466
  510.2 19.4 %all-to-all-start.10 = ((bf16[16,128,128]{1,2,0:T(8,128)(2,1)}), bf16[16,128,128]{1,2,0:T(8,128)(2,1)}, u32[]{:S(2)}, u32[]{:S(2)}) async-start(bf16[16,128,128]{1,2,0:T(8,128)(2,1)} %copy.139), calls=%async_computation.10 | async-start | bytes 1048576 | tf_op jit(solution)/shard_map/all_to_all | solution.py:977
  530.8 7.0 %collective-permute-start.36 = (bf16[8,400,128]{2,1,0:T(8,128)(2,1)S(1)}, bf16[8,400,128]{2,1,0:T(8,128)(2,1)}, u32[]{:S(2)}, u32[]{:S(2)}) collective-permute-start(bf16[8,400,128]{2,1,0:T(8,128)(2,1)S(1)} %bitcast.172), channel_id=1, source_target_pairs={{0,2},{2,0},{1,3},{3,1},{4,6},{6,4},{5,7},{7,5},{8,10},{10,8},{9,1... | collective-permute-start | bytes 2457608 | tf_op jit(solution)/shard_map/ppermute | solution.py:466
  530.8 6.9 %collective-permute-start.37 = (bf16[8,416,128]{2,1,0:T(8,128)(2,1)S(1)}, bf16[8,416,128]{2,1,0:T(8,128)(2,1)S(1)}, u32[]{:S(2)}, u32[]{:S(2)}) collective-permute-start(bf16[8,416,128]{2,1,0:T(8,128)(2,1)S(1)} %bitcast.170), channel_id=1, source_target_pairs={{0,2},{2,0},{1,3},{3,1},{4,6},{6,4},{5,7},{7,5},{8,10},{10,8},{9,1... | collective-permute-start | bytes 2555912 | tf_op jit(solution)/shard_map/ppermute | solution.py:466
  (56 other events, 260.4 us)
